TPU v7x, 32 devices: a whole 2x2x4 slice. The times are simulated.
32 devices in a mesh: lat: 8 (over z, x), section: 4 (over y, core).
Axes of the slice: x: 2, y: 2, z: 4, core: 2. Of those that a mesh axis runs over, the one named last changes fastest.
Arguments:
- saved_input: bfloat16 [4, 2, 4096, 256], P('section', None, 'lat'), may hold values from -6 to 6
- cotangent: bfloat16 [2, 4096, 256], P(None, 'lat'), may hold values from -6 to 6
- quad_values: bfloat16 [3, 64, 5, 64, 64], P(None, 'lat'), may hold values from -0.3125 to 0.3125
- block_index: int32 [64, 5], P('lat'), may hold values from 0 to 63, as said below
- block_mask: int32 [64, 5], P('lat'), may hold values from 0 to 1
- weights: bfloat16 [4, 3, 256, 256], P('section'), may hold values from -0.21875 to 0.21875
Outputs:
- grad_input: bfloat16 [4, 2, 4096, 256], P('section', None, 'lat')
- grad_weight: float32 [4, 3, 256, 256], P('section')
Inputs may be any that keep to these rules, and one draw needn't show every extreme that they name: block_index[b, j] lies within 2 blocks of b; entries of one row name distinct blocks where block_mask is 1.
All inputs are finite; a program needn't handle non-finite values.
Results may differ from a plain program's by a relative error of at most 0.0085.
Values may be sent and summed in bfloat16 or wider, within the bound.
No kernel may reach another device: no remote copies, remote signals or barrier semaphores. Data moves between devices by JAX's collectives and lax.ppermute only.
A program may use at most 64 MiB of HBM per device.

v0:
```python
import functools

import jax
import jax.numpy as jnp
from jax import lax
from jax.experimental import pallas as pl
from jax.experimental.pallas import tpu as pltpu
from jax.sharding import PartitionSpec as P


KB = 3
BLK = 64
HALO = 2
MB = 2
GRP = 4
SPAN = GRP + 2 * HALO
BF = jnp.bfloat16
F32 = jnp.float32
VM = pl.BlockSpec(memory_space=pltpu.VMEM)
ANY = pl.BlockSpec(memory_space=pl.ANY)
HB = pl.BlockSpec(memory_space=pltpu.HBM)


def gelu_slope(value):
    return (
        0.5 * (1.0 + lax.erf(value * 0.7071067811865476))
        + value * jnp.exp(-0.5 * value * value) * 0.3989422804014327
    )


def params(mib=24):
    return pltpu.CompilerParams(vmem_limit_bytes=mib << 20)


def near_pairs(lats, sections, side):
    pairs = []
    for i in range(lats):
        j = i ^ 1 if side == 0 else (i + 1 if i % 2 else i - 1)
        for s in range(sections):
            other = j * sections + s if 0 <= j < lats else i * sections + (s ^ 1)
            pairs.append((i * sections + s, other))
    return pairs


def edge_pairs(lats, sections):
    both = [near_pairs(lats, sections, side) for side in range(2)]
    pairs = []
    for i in range(lats):
        for s in range(sections):
            here = i * sections + s
            if s % 2 and (i == 0 or i == lats - 1):
                pairs.append((here, i * sections + (s + 2) % sections))
            else:
                pairs.append((here, dict(both[s % 2])[here]))
    return pairs


def hop_pairs(sections, turn):
    if turn % 2:
        return [(s, s ^ 1) for s in range(sections)]
    return [(s, (s - 1) % sections) for s in range(sections)]


def slant_pairs(lats, sections, turn, upward):
    last, low = lats - 1, turn - 1
    ways = {(i, turn): (i + 1, low) for i in range(last)}
    if turn % 2 and sections > 2:
        aside = (turn - 2) % sections
        ways[last, turn] = (last, aside)
        ways.update({(i, aside): (i - 1, aside) for i in range(1, lats)})
        ways[0, aside] = (0, low)
        ways.update({(i, low): (i, turn) for i in range(lats)})
        for i in range(lats):
            for s in range(sections):
                ways.setdefault((i, s), (i ^ 1, s))
        assert len(set(ways.values())) == lats * sections
    if not upward:
        ways = {(last - i, s): (last - j, r) for (i, s), (j, r) in ways.items()}
    return [(i * sections + s, j * sections + r) for (i, s), (j, r) in ways.items()]


def cost(flops):
    return pl.CostEstimate(flops=flops, bytes_accessed=flops // 256, transcendentals=0)


def dot(a, b):
    return jnp.dot(a, b, preferred_element_type=F32)


def band_kernel(
    blocks, index_in, mask_in, quad_in, band_ref, flip_ref, index_ref, mask_ref, quad_ref, table_ref, sems
):
    first = lax.axis_index("lat") * blocks
    small = [
        pltpu.make_async_copy(index_in, index_ref, sems.at[KB]),
        pltpu.make_async_copy(mask_in, mask_ref, sems.at[KB + 1]),
    ]
    large = [pltpu.make_async_copy(quad_in.at[k], quad_ref.at[k], sems.at[k]) for k in range(KB)]
    for c in small + large:
        c.start()
    for c in small:
        c.wait()
    for b in range(blocks):
        for d in range(2 * HALO + 2):
            table_ref[b, d] = 0
        for j in range(index_ref.shape[1]):
            d = index_ref[b, j] - (first + b) + HALO
            table_ref[b, jnp.where(mask_ref[b, j] != 0, d, 2 * HALO + 1)] = j + 1
    empty = jnp.zeros((BLK, BLK), BF)
    for k in range(KB):
        large[k].wait()
        for b in range(blocks):
            g, r = b // GRP, b % GRP
            tiles = [empty] * r
            for d in range(2 * HALO + 1):
                entry = table_ref[b, d]
                tile = quad_ref[k, b, jnp.maximum(entry - 1, 0)]
                tiles.append(jnp.where(entry > 0, tile, empty))
            tiles += [empty] * (GRP - 1 - r)
            half, rest = divmod(r * BLK, HALO * BLK)
            row = (half * KB + k) * HALO * BLK + rest
            band_ref[g, row : row + BLK, :] = jnp.concatenate(tiles, axis=1)
            if rest + BLK == HALO * BLK:
                part = slice(row - rest, row + BLK)
                flip_ref[g, :, part] = band_ref[g, part, :].T


def band_call(block_index, block_mask, quad):
    blocks = quad.shape[1]
    groups = blocks // GRP
    return pl.pallas_call(
        functools.partial(band_kernel, blocks),
        out_shape=(
            pltpu.VMEM((groups, KB * GRP * BLK, SPAN * BLK), BF),
            pltpu.VMEM((groups, SPAN * BLK, KB * GRP * BLK), BF),
        ),
        in_specs=[HB] * 3,
        out_specs=(VM, VM),
        scratch_shapes=[
            pltpu.SMEM(block_index.shape, jnp.int32),
            pltpu.SMEM(block_mask.shape, jnp.int32),
            pltpu.VMEM(quad.shape, BF),
            pltpu.SMEM((blocks, 2 * HALO + 2), jnp.int32),
            pltpu.SemaphoreType.DMA((KB + 2,)),
        ],
        compiler_params=params(),
        name="band",
    )(*(pltpu.with_memory_space_constraint(a, pltpu.HBM) for a in (block_index, block_mask, quad)))


def hidden_kernel(inner, x_ref, band_ref, w_ref, *refs):
    hid_ref, gp_ref = refs[-2:]
    pair = HALO * BLK
    deep = KB * pair
    groups = band_ref.shape[0]
    spots = [(g, h) for g in range(groups) for h in range(2)]
    spots = spots[1:-1] if inner else [spots[0], spots[-1]]
    odd = lax.axis_index("lat") % 2 == 1
    parts = []
    for m in range(MB):
        for g, h in spots:
            at = (2 * g + h - 1) * pair
            if inner:
                window = x_ref[0, m, at : at + 3 * pair, :]
            elif g == 0:
                rim = jnp.where(odd, refs[0][m], refs[1][m])
                window = jnp.concatenate([rim, x_ref[0, m, : 2 * pair, :]], axis=0)
            else:
                rim = jnp.where(odd, refs[1][m], refs[0][m])
                window = jnp.concatenate([x_ref[0, m, at:, :], rim], axis=0)
            band = band_ref[g, h * deep : (h + 1) * deep, h * pair : h * pair + 3 * pair]
            parts.append(dot(band, window).astype(BF))
            hid_ref[m, g, h * deep : (h + 1) * deep, :] = parts[-1]
    z = None
    for k in range(KB):
        rows = jnp.concatenate([p[k * pair : (k + 1) * pair] for p in parts], axis=0)
        new = dot(rows, w_ref[0, k])
        z = new if z is None else z + new
    gp = gelu_slope(z)
    for i, (m, g, h) in enumerate((m, g, h) for m in range(MB) for g, h in spots):
        gp_ref[m, (2 * g + h) * pair : (2 * g + h + 1) * pair, :] = gp[i * pair : (i + 1) * pair]


def hidden_call(x, band, weights, *rest):
    _, mb, rows, ch = x.shape
    args = (x, band, weights) + rest
    return pl.pallas_call(
        functools.partial(hidden_kernel, not rest),
        out_shape=(
            pltpu.VMEM((mb, band.shape[0], KB * GRP * BLK, ch), BF),
            pltpu.VMEM((mb, rows, ch), F32),
        ),
        in_specs=[VM] * len(args),
        out_specs=(VM, VM),
        input_output_aliases={5: 0, 6: 1} if rest else {},
        compiler_params=params(),
        cost_estimate=None if rest else cost(1 << 30),
        name="outer" if rest else "inner",
    )(*args)


PARTS = {
    "edge": ("left", "right", "slope"),
    "slope": ("slope", "done"),
    "tips": ("left", "right"),
    "bulk": ("out",),
    "head": ("slope", "done", "out", "sent0"),
    "tail": ("left", "right", "slope", "done", "out", "sent1"),
}
MICROS = {"head": (0,), "tail": (1,)}


def back_terms(slope, w_ref, stack_ref):
    pair = HALO * BLK
    for k in range(KB):
        back = lax.dot_general(
            slope, w_ref[0, k], (((1,), (1,)), ((), ())), preferred_element_type=F32
        ).astype(BF)
        for h in range(slope.shape[0] // pair):
            stack_ref[(h * KB + k) * pair : (h * KB + k + 1) * pair, :] = back[h * pair : (h + 1) * pair]


def step_kernel(turn, lats, part, form, *refs):
    outs, (stack_ref, term_ref) = dict(zip(PARTS[part], refs[-2 - len(PARTS[part]) :])), refs[-2:]
    (gp_ref, flip_ref, w_ref), rest = refs[:3], refs[3:]
    lat = lax.axis_index("lat")
    rows = gp_ref.shape[1]
    size = GRP * BLK
    edge = HALO * BLK
    lap = 2 * edge
    groups = rows // size

    micros = MICROS.get(part, range(MB))
    slope_ref = outs.get("slope", gp_ref)

    def grad_of(m, g):
        at = slice(g * size, (g + 1) * size)
        grad = (rest[m][at, :] if form == "micro" else rest[0][m, at, :]).astype(F32)
        if form == "whole":
            return grad
        below_ref, above_ref = rest[MB : MB + 2] if form == "micro" else rest[1:3]
        parts = [grad[i * edge : (i + 1) * edge] for i in range(size // edge)]
        if g == 0:
            parts[0] += jnp.where(lat > 0, below_ref[m].astype(F32), 0.0)
        if g == groups - 1:
            parts[-1] += jnp.where(lat < lats - 1, above_ref[m].astype(F32), 0.0)
        return jnp.concatenate(parts, axis=0).astype(BF).astype(F32)

    def tips():
        rims = [slope_ref[m, at : at + edge, :] for m in range(MB) for at in (0, rows - edge)]
        back_terms(jnp.concatenate(rims, axis=0), w_ref, stack_ref)
        deep = KB * edge
        for m in range(MB):
            low = stack_ref[2 * m * deep : (2 * m + 1) * deep, :]
            outs["left"][m] = dot(flip_ref[0, :edge, :deep], low).astype(BF)
            high = stack_ref[(2 * m + 1) * deep : (2 * m + 2) * deep, :]
            outs["right"][m] = dot(flip_ref[groups - 1, size + edge :, deep:], high).astype(BF)

    def slopes():
        for m in micros:
            for g in range(groups):
                grad = grad_of(m, g)
                at = slice(g * size, (g + 1) * size)
                outs["slope"][m, at, :] = (grad * gp_ref[m, at, :]).astype(BF)
                if "done" in outs and g == 0:
                    outs["done"][m, :edge, :] = grad[:edge].astype(BF)
                if "done" in outs and g == groups - 1:
                    outs["done"][m, edge:, :] = grad[size - edge :].astype(BF)

    def terms(m):
        for g in range(groups):
            grad = grad_of(m, g)
            back_terms(slope_ref[m, g * size : (g + 1) * size, :], w_ref, stack_ref)
            term = dot(flip_ref[g], stack_ref[: KB * size, :])
            low = g * size
            if g == 0:
                term_ref[low + edge : low + lap, :] = term[edge:lap] + grad[: lap - edge]
            else:
                term_ref[low : low + lap, :] += term[:lap]
                term_ref[low + edge : low + lap, :] += grad[: lap - edge]
            term_ref[low + lap : low + size + edge, :] = term[lap : size + edge] + grad[lap - edge :]
            if g < groups - 1:
                term_ref[low + size + edge : low + size + lap, :] = term[size + edge :]
        out = term_ref[edge : edge + rows, :].astype(BF)
        outs["out"][m] = out
        if part in MICROS:
            outs[f"sent{m}"][...] = out

    @pl.when(lax.axis_index("section") == turn)
    def _():
        if "slope" in outs:
            slopes()
        if "out" in outs:
            for m in micros:
                terms(m)
        if "left" in outs:
            tips()


def step_call(turn, lats, part, grads, flip, weights, state):
    mb, rows, ch = state["gp"].shape
    edge = HALO * BLK
    names = PARTS[part]
    known = [name for name in names if name in state]
    form = {1: "whole", 3: "summed", 4: "micro"}[len(grads)]
    factor = state["gp" if "slope" in names else "slope"]
    args = (factor, flip, weights) + grads + tuple(state[name] for name in known)
    tall = {"left": edge, "right": edge, "done": 2 * edge}
    shapes = {name: (mb, tall.get(name, rows), ch) for name in names}
    shapes.update({name: (rows, ch) for name in names if name.startswith("sent")})
    outs = pl.pallas_call(
        functools.partial(step_kernel, turn, lats, part, form),
        out_shape=tuple(pltpu.VMEM(shapes[name], BF) for name in names),
        in_specs=[VM] * len(args),
        out_specs=(VM,) * len(names),
        input_output_aliases={
            len(args) - len(known) + i: names.index(name) for i, name in enumerate(known)
        },
        scratch_shapes=[
            pltpu.VMEM((KB * max(GRP * BLK, 2 * MB * edge), ch), BF),
            pltpu.VMEM((rows + 2 * edge, ch), F32),
        ],
        compiler_params=params(),
    )(*args)
    state.update(zip(names, outs))


def weight_terms(hid_ref, slope_ref, acc_ref):
    size = GRP * BLK
    edge = HALO * BLK
    for k in range(KB):
        total = None
        for m in range(MB):
            for g in range(hid_ref.shape[1]):
                pairs = [hid_ref[m, g, i * edge : (i + 1) * edge, :] for i in (k, KB + k)]
                part = lax.dot_general(
                    jnp.concatenate(pairs, axis=0),
                    slope_ref[m, g * size : (g + 1) * size, :],
                    (((0,), (0,)), ((), ())),
                    preferred_element_type=F32,
                )
                total = part if total is None else total + part
        acc_ref[k * total.shape[0] : (k + 1) * total.shape[0], :] = total


def weight_call(hid, slope):
    ch = slope.shape[2]
    return pl.pallas_call(
        weight_terms,
        out_shape=pltpu.VMEM((KB * ch, ch), F32),
        in_specs=[VM] * 2,
        out_specs=VM,
        compiler_params=params(),
        name="weight",
    )(hid, slope)


def lay_edges(even_ref, odd_ref):
    odd = lax.axis_index("lat") % 2 == 1
    return jnp.concatenate([jnp.where(odd, odd_ref[m], even_ref[m]) for m in range(MB)], axis=0)


def cut_kernel(hid_ref, slope_ref, own_ref, one_ref, pair_ref, two_ref, three_ref, far_ref, acc_ref):
    weight_terms(hid_ref, slope_ref, acc_ref)
    me = lax.axis_index("lat")
    piece = own_ref.shape[0]

    def cut(bits):
        return acc_ref[pl.ds(pl.multiple_of((me ^ bits) * piece, piece), piece), :]

    own_ref[...] = cut(0)
    one_ref[...] = cut(1).astype(BF)
    for j, bits in enumerate((5, 7)):
        pair_ref[j * piece : (j + 1) * piece, :] = cut(bits).astype(BF)
    two_ref[...] = cut(2).astype(BF)
    three_ref[...] = cut(3).astype(BF)
    far_ref[:piece, :] = cut(4)
    far_ref[piece:, :] = cut(6)


def middle_kernel(far_ref, pair_ref, four_ref, six_ref):
    piece = four_ref.shape[0]
    four_ref[...] = (far_ref[:piece, :] + pair_ref[:piece, :].astype(F32)).astype(BF)
    six_ref[...] = (far_ref[piece:, :] + pair_ref[piece:, :].astype(F32)).astype(BF)


def give_kernel(left_ref, right_ref, out_ref):
    out_ref[...] = lay_edges(left_ref, right_ref)


def sum_kernel(own_ref, *refs):
    total = own_ref[...]
    for ref in refs[:-1]:
        total += ref[: total.shape[0], :].astype(F32)
    refs[-1][...] = total.astype(BF)


def pack_kernel(*refs):
    at = 0
    for ref in refs[:-1]:
        for value in [ref[...]] if len(ref.shape) == 2 else [ref[m] for m in range(ref.shape[0])]:
            refs[-1][at : at + value.shape[0], :] = value
            at += value.shape[0]


def rims_kernel(got_ref, left_ref, right_ref, out_ref):
    second = lax.axis_index("section") % 2 == 1
    out_ref[...] = jnp.where(second, got_ref[...], lay_edges(right_ref, left_ref))


def join_kernel(spots, piece, *refs):
    refs, (weight_ref, wide_ref, sems) = refs[: len(set(s[0] for s in spots))], refs[-3:]
    me = lax.axis_index("lat")
    copies = []
    for j, (source, part, bits) in enumerate(spots):
        wide_ref[j] = refs[source][part * piece : (part + 1) * piece, :].astype(F32)
        at = pl.multiple_of((me ^ bits) * piece, piece)
        copies.append(pltpu.make_async_copy(wide_ref.at[j], weight_ref.at[pl.ds(at, piece)], sems.at[j]))
        copies[-1].start()
    for c in copies:
        c.wait()


def join_call(lats, spots, sources, old=()):
    ch = sources[0].shape[1]
    piece = KB * ch // lats
    return pl.pallas_call(
        functools.partial(join_kernel, spots, piece),
        out_shape=jax.ShapeDtypeStruct((KB * ch, ch), F32),
        in_specs=[VM] * len(sources) + [ANY] * len(old),
        out_specs=ANY,
        input_output_aliases={len(sources): 0} if old else {},
        scratch_shapes=[
            pltpu.VMEM((len(spots), piece, ch), F32),
            pltpu.SemaphoreType.DMA((len(spots),)),
        ],
        compiler_params=params(),
    )(*sources, *old)


def small_call(kernel, shapes, *args, scratch=()):
    return pl.pallas_call(
        kernel,
        out_shape=tuple(shapes),
        in_specs=[VM] * len(args),
        out_specs=(VM,) * len(shapes),
        scratch_shapes=list(scratch),
        compiler_params=params(),
    )(*args)


def reduce_weight(lats, sections, hid, state):
    left, right, slope, done = (state[name] for name in ("left", "right", "slope", "done"))
    ch = slope.shape[2]
    piece = KB * ch // lats
    edges = MB * left.shape[1]
    swap = [(s, s ^ 1) for s in range(sections)]

    def vmem(rows, dtype=BF):
        return pltpu.VMEM((rows, ch), dtype)

    def meet(a, bits):
        return lax.ppermute(a, "lat", [(i, i ^ bits) for i in range(lats)])

    shapes = (vmem(piece, F32), vmem(piece), vmem(2 * piece), vmem(piece), vmem(piece), vmem(2 * piece, F32))
    own, one, pair, two, three, far = small_call(cut_kernel, shapes, hid, slope, scratch=(vmem(KB * ch, F32),))
    pair, two, three, one = meet(pair, 1), meet(two, 2), meet(three, 3), meet(one, 1)
    (give,) = small_call(give_kernel, (vmem(edges),), left, right)
    got = lax.ppermute(give, "section", swap)
    four, six = small_call(middle_kernel, (vmem(piece), vmem(piece)), far, pair)
    four, six = meet(four, 4), meet(six, 6)
    (rims,) = small_call(rims_kernel, (vmem(edges),), got, left, right)
    rims = lax.ppermute(rims, ("lat", "section"), edge_pairs(lats, sections))
    (mine,) = small_call(sum_kernel, (vmem(piece),), own, one, two, three, four, six)
    four, six = meet(mine, 4), meet(mine, 6)
    two, three = meet(mine, 2), meet(mine, 3)
    (one,) = small_call(pack_kernel, (vmem(3 * piece),), mine, four, six)
    one = meet(one, 1)
    (aside,) = small_call(pack_kernel, (vmem(edges + MB * done.shape[1]),), rims, done)
    aside = lax.ppermute(aside, "section", swap)
    spots = [(j, 0, bits) for j, bits in enumerate((0, 2, 3, 4, 6))]
    weight = join_call(lats, spots, (mine, two, three, four, six))
    spots = [(0, j, bits) for j, bits in enumerate((1, 5, 7))]
    weight = join_call(lats, spots, (one,), (weight,))
    return weight, rims, aside


def grad_kernel(lats, main_ref, near_ref, far_ref, grad_ref):
    rows = main_ref.shape[1]
    edge = HALO * BLK
    me = lax.axis_index("lat")
    odd = me % 2 == 1
    behind = far_ref.shape[0] > MB * edge
    finished = jnp.logical_and(lax.axis_index("section") % 2 == 1, behind)
    for m in range(MB):
        near = near_ref[m * edge : (m + 1) * edge, :].astype(F32)
        far = far_ref[m * edge : (m + 1) * edge, :].astype(F32)
        below = jnp.where(me > 0, jnp.where(odd, near, far), 0.0)
        above = jnp.where(me < lats - 1, jnp.where(odd, far, near), 0.0)
        low = (main_ref[m, :edge, :].astype(F32) + below).astype(BF)
        high = (main_ref[m, rows - edge :, :].astype(F32) + above).astype(BF)
        if behind:
            at = (MB + 2 * m) * edge
            low = jnp.where(finished, far_ref[at : at + edge, :], low)
            high = jnp.where(finished, far_ref[at + edge : at + 2 * edge, :], high)
        grad_ref[0, m, :edge, :] = low
        grad_ref[0, m, edge : rows - edge, :] = main_ref[m, edge : rows - edge, :]
        grad_ref[0, m, rows - edge :, :] = high


def grad_call(lats, main, near, far):
    return pl.pallas_call(
        functools.partial(grad_kernel, lats),
        out_shape=jax.ShapeDtypeStruct((1,) + main.shape, BF),
        in_specs=[VM] * 3,
        out_specs=VM,
        compiler_params=params(),
        name="grad",
    )(main, near, far)


def per_device(saved_input, cotangent, quad_values, block_index, block_mask, weights):
    sections = lax.axis_size("section")
    lats = lax.axis_size("lat")
    edge = HALO * BLK
    rows = saved_input.shape[2]
    both = ("lat", "section")
    odd = lax.axis_index("lat") % 2
    sides = [near_pairs(lats, sections, side) for side in range(2)]

    def rim(high):
        return lax.dynamic_slice_in_dim(saved_input[0], high * (rows - edge), edge, axis=1)

    far = lax.ppermute(rim(odd), both, sides[1])
    near = lax.ppermute(rim(1 - odd), both, sides[0])
    band, flip = band_call(block_index, block_mask, quad_values)
    hid, gp = hidden_call(saved_input, band, weights)
    hid, gp = hidden_call(saved_input, band, weights, near, far, hid, gp)

    state, grads = {"gp": gp}, (cotangent,)

    def send(array, pairs, axis=both):
        return lax.ppermute(array, axis, pairs)

    for turn in reversed(range(sections)):
        if turn == 0:
            step_call(turn, lats, "slope", grads, flip, weights, state)
            step_call(turn, lats, "tips", grads, flip, weights, state)
            step_call(turn, lats, "bulk", grads, flip, weights, state)
            continue
        if turn % 2:
            step_call(turn, lats, "edge", grads, flip, weights, state)
            step_call(turn, lats, "bulk", grads, flip, weights, state)
            sent = {"main": state["out"]}
        else:
            step_call(turn, lats, "head", grads, flip, weights, state)
            step_call(turn, lats, "tail", grads, flip, weights, state)
            sent = {"main0": state["sent0"], "main1": state["sent1"]}
        hop = hop_pairs(sections, turn)
        grads = tuple(send(array, hop, "section") for array in sent.values())
        low = send(state["right"], slant_pairs(lats, sections, turn, True))
        high = send(state["left"], slant_pairs(lats, sections, turn, False))
        grads += (low, high)

    left, right, slope = (state[name] for name in PARTS["edge"])
    channels = saved_input.shape[3]
    if lats == 8 and sections % 2 == 0:
        weight, near, far = reduce_weight(lats, sections, hid, state)
        grad = grad_call(lats, state["out"], near, far)
    else:
        give = jnp.where(odd == 1, left, right), jnp.where(odd == 1, right, left)
        near, far = (lax.ppermute(g, both, p).reshape(-1, channels) for g, p in zip(give, sides))
        weight = lax.psum(weight_call(hid, slope), "lat")
        grad = grad_call(lats, state["out"], near, far)
    return grad, weight.reshape(1, KB, channels, channels)


def solution(mesh):
    in_specs = (
        P("section", None, "lat", None),
        P(None, "lat", None),
        P(None, "lat", None, None, None),
        P("lat", None),
        P("lat", None),
        P("section", None, None, None),
    )
    out_specs = (P("section", None, "lat", None), P("section", None, None, None))
    return jax.shard_map(
        per_device, mesh=mesh, in_specs=in_specs, out_specs=out_specs, check_vma=False
    )
```

profile of v0, /device:TPU:0, one launch (start us, length us, event | category | flops | bytes accessed | tf_op | source)
XLA Modules:
  0.0 84.2 jit_solution(10133770731252367966)
XLA Ops:
  0.7 1.1 %dynamic-slice_bitcast_fusion = (bf16[2,128,256]{2,1,0:T(8,128)(2,1)S(1)}, bf16[2,128,256]{2,1,0:T(8,128)(2,1)S(1)}) fusion(bf16[1,2,512,256]{3,2,1,0:T(8,128)(2,1)} %x_ref.3, s32[]{:T(128)S(6)} %select_n.15, s32[]{:T(128)S(6)} %select_n.14), kind=kLoop, calls=%fused_computation | loop fusion | bytes 524296 | tf_op jit(solution)/shard_map/dynamic_slice | solution.py:532
  1.7 0.6 collective-permute-start.1
  2.3 4.0 %collective-permute-start = (bf16[2,128,256]{2,1,0:T(8,128)(2,1)S(1)}, bf16[2,128,256]{2,1,0:T(8,128)(2,1)S(1)}, u32[]{:S(2)}, u32[]{:S(2)}) collective-permute-start(bf16[2,128,256]{2,1,0:T(8,128)(2,1)S(1)} %get-tuple-element.71), channel_id=1, source_target_pairs={{0,4},{1,5},{2,6},{3,7},{4,0},{5,1},{6,2},{7,3},{8,12},{9,13},{10,... | collective-permute-start | bytes 393224 | tf_op jit(solution)/shard_map/ppermute | solution.py:535
  6.3 2.4 %band.1 = (bf16[2,768,512]{2,1,0:T(8,128)(2,1)S(1)}, bf16[2,512,768]{2,1,0:T(8,128)(2,1)S(1)}) custom-call(s32[8,5]{1,0:T(8,128)} %index_in.1, s32[8,5]{1,0:T(8,128)} %mask_in.1, bf16[3,8,5,64,64]{4,3,2,1,0:T(8,128)(2,1)} %quad_in.1), custom_call_target="tpu_custom_call" | custom-call | tf_op jit(solution)/shard_map/band/pallas_call | solution.py:131
  8.7 0.9 %inner.1 = (bf16[2,2,768,256]{3,2,1,0:T(8,128)(2,1)S(1)}, f32[2,512,256]{2,1,0:T(8,128)S(1)}) custom-call(bf16[1,2,512,256]{3,2,1,0:T(8,128)(2,1)S(1)} %copy-done.2, bf16[2,768,512]{2,1,0:T(8,128)(2,1)S(1)} %get-tuple-element.36.band_ref, bf16[1,3,256,256]{3,2,1,0:T(8,128)(2,1)S(1)} %copy-done), custom_call_target="tpu_custom_call" | custom-call | flops 1073741824 | bytes 4194304 | tf_op jit(solution)/shard_map/inner/pallas_call | solution.py:187
  9.6 0.0 collective-permute-done.1.refs_1_
  9.7 1.6 %collective-permute-done.refs_0_ = bf16[2,128,256]{2,1,0:T(8,128)(2,1)S(1)} collective-permute-done((bf16[2,128,256]{2,1,0:T(8,128)(2,1)S(1)}, bf16[2,128,256]{2,1,0:T(8,128)(2,1)S(1)}, u32[]{:S(2)}, u32[]{:S(2)}) %collective-permute-start) | collective-permute-done | bytes 131104 | tf_op jit(solution)/shard_map/ppermute | solution.py:535
  11.2 0.9 %outer.1 = (bf16[2,2,768,256]{3,2,1,0:T(8,128)(2,1)S(1)}, f32[2,512,256]{2,1,0:T(8,128)S(1)}) custom-call(bf16[1,2,512,256]{3,2,1,0:T(8,128)(2,1)S(1)} %copy-done.2, bf16[2,768,512]{2,1,0:T(8,128)(2,1)S(1)} %get-tuple-element.36.band_ref, bf16[1,3,256,256]{3,2,1,0:T(8,128)(2,1)S(1)} %copy-done, ...), custom_call_target="tpu_custom_call", output_to_operand_aliasing={{0}: (5, {}), {1}: (6, {})} | custom-call | tf_op jit(solution)/shard_map/outer/pallas_call | solution.py:187
  12.2 0.1 copy-done.1
  12.3 0.0 collective-permute-start.2
  12.3 2.5 %collective-permute-start.3 = (bf16[2,128,256]{2,1,0:T(8,128)(2,1)S(1)}, bf16[2,128,256]{2,1,0:T(8,128)(2,1)S(1)}, u32[]{:S(2)}, u32[]{:S(2)}) collective-permute-start(bf16[2,128,256]{2,1,0:T(8,128)(2,1)S(1)} %get-tuple-element.42.refs_7_), channel_id=1, source_target_pairs={{3,6},{7,10},{11,14},{15,18},{19,22},{23,26},{27,30},{31,29},{5,1}... | collective-permute-start | bytes 393224 | tf_op jit(solution)/shard_map/ppermute | solution.py:543
  14.8 0.1 collective-permute-start.4
  14.9 4.8 %collective-permute-done.3.refs_4_ = bf16[2,128,256]{2,1,0:T(8,128)(2,1)S(1)} collective-permute-done((bf16[2,128,256]{2,1,0:T(8,128)(2,1)S(1)}, bf16[2,128,256]{2,1,0:T(8,128)(2,1)S(1)}, u32[]{:S(2)}, u32[]{:S(2)}) %collective-permute-start.3) | collective-permute-done | bytes 131104 | tf_op jit(solution)/shard_map/ppermute | solution.py:543
  19.7 1.9 %collective-permute-done.4.refs_5_ = bf16[2,128,256]{2,1,0:T(8,128)(2,1)S(1)} collective-permute-done((bf16[2,128,256]{2,1,0:T(8,128)(2,1)S(1)}, bf16[2,128,256]{2,1,0:T(8,128)(2,1)S(1)}, u32[]{:S(2)}, u32[]{:S(2)}) %collective-permute-start.4) | collective-permute-done | bytes 131104 | tf_op jit(solution)/shard_map/ppermute | solution.py:543
  21.5 0.0 collective-permute-done.2.refs_3_
  21.5 0.5 collective-permute-start.5
  22.1 2.3 %collective-permute-start.6 = (bf16[512,256]{1,0:T(8,128)(2,1)S(1)}, bf16[512,256]{1,0:T(8,128)(2,1)S(1)}, u32[]{:S(2)}, u32[]{:S(2)}) collective-permute-start(bf16[512,256]{1,0:T(8,128)(2,1)S(1)} %get-tuple-element.48), channel_id=1, source_target_pairs={{0,3},{1,0},{2,1},{3,2},{4,7},{5,4},{6,5},{7,6},{8,11},{9,8},{10,9... | collective-permute-start | bytes 786440 | tf_op jit(solution)/shard_map/ppermute | solution.py:543
  24.4 0.7 collective-permute-start.7
  25.0 0.7 collective-permute-start.8
  25.7 0.0 collective-permute-done.7.refs_5_
  25.7 0.0 collective-permute-done.8.refs_6_
  25.7 0.2 collective-permute-done.5.refs_3_
  26.0 2.8 %collective-permute-done.6.refs_4_ = bf16[512,256]{1,0:T(8,128)(2,1)S(1)} collective-permute-done((bf16[512,256]{1,0:T(8,128)(2,1)S(1)}, bf16[512,256]{1,0:T(8,128)(2,1)S(1)}, u32[]{:S(2)}, u32[]{:S(2)}) %collective-permute-start.6) | collective-permute-done | bytes 262176 | tf_op jit(solution)/shard_map/ppermute | solution.py:543
  28.8 6.6 %collective-permute-start.9 = (bf16[2,512,256]{2,1,0:T(8,128)(2,1)S(1)}, bf16[2,512,256]{2,1,0:T(8,128)(2,1)S(1)}, u32[]{:S(2)}, u32[]{:S(2)}) collective-permute-start(bf16[2,512,256]{2,1,0:T(8,128)(2,1)S(1)} %shard_map.82.refs_6_), channel_id=1, source_target_pairs={{0,1},{1,0},{2,3},{3,2},{4,5},{5,4},{6,7},{7,6},{8,9},{9,8},{10,11... | collective-permute-start | bytes 1572872 | tf_op jit(solution)/shard_map/ppermute | solution.py:543
  35.4 0.1 collective-permute-start.10
  35.4 3.3 %collective-permute-start.11 = (bf16[2,128,256]{2,1,0:T(8,128)(2,1)S(1)}, bf16[2,128,256]{2,1,0:T(8,128)(2,1)S(1)}, u32[]{:S(2)}, u32[]{:S(2)}) collective-permute-start(bf16[2,128,256]{2,1,0:T(8,128)(2,1)S(1)} %get-tuple-element.55.refs_6_), channel_id=1, source_target_pairs={{29,24},{25,20},{21,16},{17,12},{13,8},{9,4},{5,0},{1,3},{27,31},{... | collective-permute-start | bytes 393224 | tf_op jit(solution)/shard_map/ppermute | solution.py:543
  38.8 1.0 %collective-permute-done.10.refs_4_ = bf16[2,128,256]{2,1,0:T(8,128)(2,1)S(1)} collective-permute-done((bf16[2,128,256]{2,1,0:T(8,128)(2,1)S(1)}, bf16[2,128,256]{2,1,0:T(8,128)(2,1)S(1)}, u32[]{:S(2)}, u32[]{:S(2)}) %collective-permute-start.10) | collective-permute-done | bytes 131104 | tf_op jit(solution)/shard_map/ppermute | solution.py:543
  39.8 3.7 %collective-permute-done.11.refs_5_ = bf16[2,128,256]{2,1,0:T(8,128)(2,1)S(1)} collective-permute-done((bf16[2,128,256]{2,1,0:T(8,128)(2,1)S(1)}, bf16[2,128,256]{2,1,0:T(8,128)(2,1)S(1)}, u32[]{:S(2)}, u32[]{:S(2)}) %collective-permute-start.11) | collective-permute-done | bytes 131104 | tf_op jit(solution)/shard_map/ppermute | solution.py:543
  43.5 0.0 collective-permute-done.9.refs_3_
  43.5 0.2 shard_map.83
  43.7 0.8 shard_map.85
  44.5 0.1 collective-permute-start.12
  44.6 1.3 %collective-permute-done.12.got_ref = bf16[256,256]{1,0:T(8,128)(2,1)S(1)} collective-permute-done((bf16[256,256]{1,0:T(8,128)(2,1)S(1)}, bf16[256,256]{1,0:T(8,128)(2,1)S(1)}, u32[]{:S(2)}, u32[]{:S(2)}) %collective-permute-start.12) | collective-permute-done | bytes 131104 | tf_op jit(solution)/shard_map/ppermute | solution.py:469
  46.0 1.1 %collective-permute-start.13 = (bf16[256,256]{1,0:T(8,128)(2,1)S(1)}, bf16[256,256]{1,0:T(8,128)(2,1)S(1)}, u32[]{:S(2)}, u32[]{:S(2)}) collective-permute-start(bf16[256,256]{1,0:T(8,128)(2,1)S(1)} %shard_map.87), channel_id=1, source_target_pairs={{0,4},{1,3},{2,6},{3,1},{4,0},{5,9},{6,2},{7,11},{8,12},{9,5},{10,... | collective-permute-start | bytes 393224 | tf_op jit(solution)/shard_map/ppermute | solution.py:473
  47.0 4.0 %collective-permute-done.13.refs_0_.near_ref = bf16[256,256]{1,0:T(8,128)(2,1)S(1)} collective-permute-done((bf16[256,256]{1,0:T(8,128)(2,1)S(1)}, bf16[256,256]{1,0:T(8,128)(2,1)S(1)}, u32[]{:S(2)}, u32[]{:S(2)}) %collective-permute-start.13) | collective-permute-done | bytes 131104 | tf_op jit(solution)/shard_map/ppermute | solution.py:473
  51.1 0.1 collective-permute-start.14
  51.1 0.7 shard_map.89
  51.8 2.5 %collective-permute-start.18 = (bf16[192,256]{1,0:T(8,128)(2,1)S(1)}, bf16[192,256]{1,0:T(8,128)(2,1)S(1)}, u32[]{:S(2)}, u32[]{:S(2)}) collective-permute-start(bf16[192,256]{1,0:T(8,128)(2,1)S(1)} %get-tuple-element.67), channel_id=1, source_target_pairs={{0,4},{4,0},{8,12},{12,8},{16,20},{20,16},{24,28},{28,24},{1,5},{5... | collective-permute-start | bytes 294920 | tf_op jit(solution)/shard_map/ppermute | solution.py:463
  54.3 0.1 collective-permute-start.15
  54.3 3.8 %collective-permute-start.16 = (bf16[96,256]{1,0:T(8,128)(2,1)S(1)}, bf16[96,256]{1,0:T(8,128)(2,1)S(1)}, u32[]{:S(2)}, u32[]{:S(2)}) collective-permute-start(bf16[96,256]{1,0:T(8,128)(2,1)S(1)} %get-tuple-element.64), channel_id=1, source_target_pairs={{0,8},{4,12},{8,0},{12,4},{16,24},{20,28},{24,16},{28,20},{1,9},{5... | collective-permute-start | bytes 147464 | tf_op jit(solution)/shard_map/ppermute | solution.py:463
  58.2 0.0 collective-permute-start.17
  58.2 0.0 collective-permute-done.18.pair_ref
  58.2 4.0 %collective-permute-start.19 = (bf16[96,256]{1,0:T(8,128)(2,1)S(1)}, bf16[96,256]{1,0:T(8,128)(2,1)S(1)}, u32[]{:S(2)}, u32[]{:S(2)}) collective-permute-start(bf16[96,256]{1,0:T(8,128)(2,1)S(1)} %get-tuple-element.68), channel_id=1, source_target_pairs={{0,16},{4,20},{8,24},{12,28},{16,0},{20,4},{24,8},{28,12},{1,17},{... | collective-permute-start | bytes 147464 | tf_op jit(solution)/shard_map/ppermute | solution.py:463
  62.2 0.0 collective-permute-done.15.refs_0_
  62.2 2.2 %collective-permute-start.20 = (bf16[96,256]{1,0:T(8,128)(2,1)S(1)}, bf16[96,256]{1,0:T(8,128)(2,1)S(1)}, u32[]{:S(2)}, u32[]{:S(2)}) collective-permute-start(bf16[96,256]{1,0:T(8,128)(2,1)S(1)} %get-tuple-element.69), channel_id=1, source_target_pairs={{0,24},{4,28},{8,16},{12,20},{16,8},{20,12},{24,0},{28,4},{1,25},{... | collective-permute-start | bytes 147464 | tf_op jit(solution)/shard_map/ppermute | solution.py:463
  64.4 0.0 collective-permute-done.16.refs_1_
  64.4 0.0 collective-permute-done.17.refs_2_
  64.4 0.5 collective-permute-done.19.refs_3_
  65.0 3.1 %collective-permute-done.20.refs_4_ = bf16[96,256]{1,0:T(8,128)(2,1)S(1)} collective-permute-done((bf16[96,256]{1,0:T(8,128)(2,1)S(1)}, bf16[96,256]{1,0:T(8,128)(2,1)S(1)}, u32[]{:S(2)}, u32[]{:S(2)}) %collective-permute-start.20) | collective-permute-done | bytes 49184 | tf_op jit(solution)/shard_map/ppermute | solution.py:463
  68.1 2.4 %collective-permute-start.22 = (bf16[96,256]{1,0:T(8,128)(2,1)S(1)}, bf16[96,256]{1,0:T(8,128)(2,1)S(1)}, u32[]{:S(2)}, u32[]{:S(2)}) collective-permute-start(bf16[96,256]{1,0:T(8,128)(2,1)S(1)} %shard_map.91.refs_0_), channel_id=1, source_target_pairs={{0,24},{4,28},{8,16},{12,20},{16,8},{20,12},{24,0},{28,4},{1,25},{... | collective-permute-start | bytes 147464 | tf_op jit(solution)/shard_map/ppermute | solution.py:463
  70.5 0.0 collective-permute-start.21
  70.5 3.6 %collective-permute-done.22.refs_2_.refs_4_ = bf16[96,256]{1,0:T(8,128)(2,1)S(1)} collective-permute-done((bf16[96,256]{1,0:T(8,128)(2,1)S(1)}, bf16[96,256]{1,0:T(8,128)(2,1)S(1)}, u32[]{:S(2)}, u32[]{:S(2)}) %collective-permute-start.22) | collective-permute-done | bytes 49184 | tf_op jit(solution)/shard_map/ppermute | solution.py:463
  74.1 1.4 %collective-permute-done.21.refs_1_.refs_3_ = bf16[96,256]{1,0:T(8,128)(2,1)S(1)} collective-permute-done((bf16[96,256]{1,0:T(8,128)(2,1)S(1)}, bf16[96,256]{1,0:T(8,128)(2,1)S(1)}, u32[]{:S(2)}, u32[]{:S(2)}) %collective-permute-start.21) | collective-permute-done | bytes 49184 | tf_op jit(solution)/shard_map/ppermute | solution.py:463
  75.5 0.1 collective-permute-start.23
  75.6 1.1 %collective-permute-start.25 = (bf16[96,256]{1,0:T(8,128)(2,1)S(1)}, bf16[96,256]{1,0:T(8,128)(2,1)S(1)}, u32[]{:S(2)}, u32[]{:S(2)}) collective-permute-start(bf16[96,256]{1,0:T(8,128)(2,1)S(1)} %shard_map.91.refs_0_), channel_id=1, source_target_pairs={{0,12},{4,8},{8,4},{12,0},{16,28},{20,24},{24,20},{28,16},{1,13},{... | collective-permute-start | bytes 147464 | tf_op jit(solution)/shard_map/ppermute | solution.py:463
  76.7 2.4 %collective-permute-start.24 = (bf16[96,256]{1,0:T(8,128)(2,1)S(1)}, bf16[96,256]{1,0:T(8,128)(2,1)S(1)}, u32[]{:S(2)}, u32[]{:S(2)}) collective-permute-start(bf16[96,256]{1,0:T(8,128)(2,1)S(1)} %shard_map.91.refs_0_), channel_id=1, source_target_pairs={{0,8},{4,12},{8,0},{12,4},{16,24},{20,28},{24,16},{28,20},{1,9},{5... | collective-permute-start | bytes 147464 | tf_op jit(solution)/shard_map/ppermute | solution.py:463
  79.1 1.9 %shard_map.84.main_ref = bf16[2,512,256]{2,1,0:T(8,128)(2,1)S(1)} custom-call(bf16[2,512,256]{2,1,0:T(8,128)(2,1)S(1)} %get-tuple-element.57.refs_0_.slope_ref, bf16[2,512,768]{2,1,0:T(8,128)(2,1)S(1)} %get-tuple-element.40.refs_1_, bf16[1,3,256,256]{3,2,1,0:T(8,128)(2,1)S(1)} %copy-done, ...), custom_call_target="tpu_custom_call", output_to_operand_aliasing={{}: (6, {})} | custom-call | tf_op jit(solution)/shard_map/pallas_call | solution.py:311
  81.0 0.0 collective-permute-done.25.refs_2_
  81.1 0.6 collective-permute-done.24.refs_1_
  81.7 0.8 shard_map.93.refs_1_
  82.5 0.0 collective-permute-done.23.refs_0_
  82.5 0.7 shard_map.94
  83.3 0.0 collective-permute-done.14.far_ref
  83.3 0.9 %grad.1 = bf16[1,2,512,256]{3,2,1,0:T(8,128)(2,1)} custom-call(bf16[2,512,256]{2,1,0:T(8,128)(2,1)S(1)} %shard_map.84.main_ref, bf16[256,256]{1,0:T(8,128)(2,1)S(1)} %collective-permute-done.13.refs_0_.near_ref, bf16[768,256]{1,0:T(8,128)(2,1)S(1)} %collective-permute-done.14.far_ref), custom_call_target="tpu_custom_call" | custom-call | tf_op jit(solution)/shard_map/grad/pallas_call | solution.py:512
  (17 shorter events, 0.2 us)
Async XLA Ops:
  0.6 8.1 %copy-start.2 = (bf16[1,2,512,256]{3,2,1,0:T(8,128)(2,1)S(1)}, bf16[1,2,512,256]{3,2,1,0:T(8,128)(2,1)}, u32[]{:S(2)}) copy-start(bf16[1,2,512,256]{3,2,1,0:T(8,128)(2,1)} %x_ref.3) | copy-start | bytes 1572868
  0.6 8.1 %copy-start = (bf16[1,3,256,256]{3,2,1,0:T(8,128)(2,1)S(1)}, bf16[1,3,256,256]{3,2,1,0:T(8,128)(2,1)}, u32[]{:S(2)}) copy-start(bf16[1,3,256,256]{3,2,1,0:T(8,128)(2,1)} %refs_2_.17) | copy-start | bytes 1179652
  1.7 7.9 %collective-permute-start.1 = (bf16[2,128,256]{2,1,0:T(8,128)(2,1)S(1)}, bf16[2,128,256]{2,1,0:T(8,128)(2,1)S(1)}, u32[]{:S(2)}, u32[]{:S(2)}) collective-permute-start(bf16[2,128,256]{2,1,0:T(8,128)(2,1)S(1)} %get-tuple-element.70), channel_id=1, source_target_pairs={{0,1},{1,0},{2,3},{3,2},{4,8},{5,9},{6,10},{7,11},{8,4},{9,5},{10,... | collective-permute-start | bytes 393224 | tf_op jit(solution)/shard_map/ppermute | solution.py:534
  2.3 8.9 %collective-permute-start = (bf16[2,128,256]{2,1,0:T(8,128)(2,1)S(1)}, bf16[2,128,256]{2,1,0:T(8,128)(2,1)S(1)}, u32[]{:S(2)}, u32[]{:S(2)}) collective-permute-start(bf16[2,128,256]{2,1,0:T(8,128)(2,1)S(1)} %get-tuple-element.71), channel_id=1, source_target_pairs={{0,4},{1,5},{2,6},{3,7},{4,0},{5,1},{6,2},{7,3},{8,12},{9,13},{10,... | collective-permute-start | bytes 393224 | tf_op jit(solution)/shard_map/ppermute | solution.py:535
  11.2 1.0 %copy-start.1 = (bf16[2,512,256]{2,1,0:T(8,128)(2,1)S(1)}, bf16[2,512,256]{2,1,0:T(8,128)(2,1)}, u32[]{:S(2)}) copy-start(bf16[2,512,256]{2,1,0:T(8,128)(2,1)} %refs_3_.3) | copy-start | bytes 1572868
  12.3 9.3 %collective-permute-start.2 = (bf16[2,512,256]{2,1,0:T(8,128)(2,1)S(1)}, bf16[2,512,256]{2,1,0:T(8,128)(2,1)S(1)}, u32[]{:S(2)}, u32[]{:S(2)}) collective-permute-start(bf16[2,512,256]{2,1,0:T(8,128)(2,1)S(1)} %shard_map.78.refs_7_), channel_id=1, source_target_pairs={{0,1},{1,0},{2,3},{3,2},{4,5},{5,4},{6,7},{7,6},{8,9},{9,8},{10,11... | collective-permute-start | bytes 1572872 | tf_op jit(solution)/shard_map/ppermute | solution.py:543
  12.3 7.4 %collective-permute-start.3 = (bf16[2,128,256]{2,1,0:T(8,128)(2,1)S(1)}, bf16[2,128,256]{2,1,0:T(8,128)(2,1)S(1)}, u32[]{:S(2)}, u32[]{:S(2)}) collective-permute-start(bf16[2,128,256]{2,1,0:T(8,128)(2,1)S(1)} %get-tuple-element.42.refs_7_), channel_id=1, source_target_pairs={{3,6},{7,10},{11,14},{15,18},{19,22},{23,26},{27,30},{31,29},{5,1}... | collective-permute-start | bytes 393224 | tf_op jit(solution)/shard_map/ppermute | solution.py:543
  14.8 6.7 %collective-permute-start.4 = (bf16[2,128,256]{2,1,0:T(8,128)(2,1)S(1)}, bf16[2,128,256]{2,1,0:T(8,128)(2,1)S(1)}, u32[]{:S(2)}, u32[]{:S(2)}) collective-permute-start(bf16[2,128,256]{2,1,0:T(8,128)(2,1)S(1)} %get-tuple-element.43.refs_6_), channel_id=1, source_target_pairs={{31,26},{27,22},{23,18},{19,14},{15,10},{11,6},{7,2},{3,1},{25,29}... | collective-permute-start | bytes 393224 | tf_op jit(solution)/shard_map/ppermute | solution.py:543
  21.5 4.4 %collective-permute-start.5 = (bf16[512,256]{1,0:T(8,128)(2,1)S(1)}, bf16[512,256]{1,0:T(8,128)(2,1)S(1)}, u32[]{:S(2)}, u32[]{:S(2)}) collective-permute-start(bf16[512,256]{1,0:T(8,128)(2,1)S(1)} %get-tuple-element.44), channel_id=1, source_target_pairs={{0,3},{1,0},{2,1},{3,2},{4,7},{5,4},{6,5},{7,6},{8,11},{9,8},{10,9... | collective-permute-start | bytes 786440 | tf_op jit(solution)/shard_map/ppermute | solution.py:543
  22.1 6.7 %collective-permute-start.6 = (bf16[512,256]{1,0:T(8,128)(2,1)S(1)}, bf16[512,256]{1,0:T(8,128)(2,1)S(1)}, u32[]{:S(2)}, u32[]{:S(2)}) collective-permute-start(bf16[512,256]{1,0:T(8,128)(2,1)S(1)} %get-tuple-element.48), channel_id=1, source_target_pairs={{0,3},{1,0},{2,1},{3,2},{4,7},{5,4},{6,5},{7,6},{8,11},{9,8},{10,9... | collective-permute-start | bytes 786440 | tf_op jit(solution)/shard_map/ppermute | solution.py:543
  24.4 1.3 %collective-permute-start.7 = (bf16[2,128,256]{2,1,0:T(8,128)(2,1)S(1)}, bf16[2,128,256]{2,1,0:T(8,128)(2,1)S(1)}, u32[]{:S(2)}, u32[]{:S(2)}) collective-permute-start(bf16[2,128,256]{2,1,0:T(8,128)(2,1)S(1)} %get-tuple-element.49.refs_8_), channel_id=1, source_target_pairs={{2,5},{6,9},{10,13},{14,17},{18,21},{22,25},{26,29}} | collective-permute-start | bytes 393224 | tf_op jit(solution)/shard_map/ppermute | solution.py:543
  25.0 0.7 collective-permute-start.8
  28.8 14.7 %collective-permute-start.9 = (bf16[2,512,256]{2,1,0:T(8,128)(2,1)S(1)}, bf16[2,512,256]{2,1,0:T(8,128)(2,1)S(1)}, u32[]{:S(2)}, u32[]{:S(2)}) collective-permute-start(bf16[2,512,256]{2,1,0:T(8,128)(2,1)S(1)} %shard_map.82.refs_6_), channel_id=1, source_target_pairs={{0,1},{1,0},{2,3},{3,2},{4,5},{5,4},{6,7},{7,6},{8,9},{9,8},{10,11... | collective-permute-start | bytes 1572872 | tf_op jit(solution)/shard_map/ppermute | solution.py:543
  35.4 4.4 %collective-permute-start.10 = (bf16[2,128,256]{2,1,0:T(8,128)(2,1)S(1)}, bf16[2,128,256]{2,1,0:T(8,128)(2,1)S(1)}, u32[]{:S(2)}, u32[]{:S(2)}) collective-permute-start(bf16[2,128,256]{2,1,0:T(8,128)(2,1)S(1)} %get-tuple-element.54.refs_7_), channel_id=1, source_target_pairs={{1,4},{5,8},{9,12},{13,16},{17,20},{21,24},{25,28},{29,31},{7,3},{... | collective-permute-start | bytes 393224 | tf_op jit(solution)/shard_map/ppermute | solution.py:543
  35.4 8.0 %collective-permute-start.11 = (bf16[2,128,256]{2,1,0:T(8,128)(2,1)S(1)}, bf16[2,128,256]{2,1,0:T(8,128)(2,1)S(1)}, u32[]{:S(2)}, u32[]{:S(2)}) collective-permute-start(bf16[2,128,256]{2,1,0:T(8,128)(2,1)S(1)} %get-tuple-element.55.refs_6_), channel_id=1, source_target_pairs={{29,24},{25,20},{21,16},{17,12},{13,8},{9,4},{5,0},{1,3},{27,31},{... | collective-permute-start | bytes 393224 | tf_op jit(solution)/shard_map/ppermute | solution.py:543
  44.5 1.4 %collective-permute-start.12 = (bf16[256,256]{1,0:T(8,128)(2,1)S(1)}, bf16[256,256]{1,0:T(8,128)(2,1)S(1)}, u32[]{:S(2)}, u32[]{:S(2)}) collective-permute-start(bf16[256,256]{1,0:T(8,128)(2,1)S(1)} %shard_map.86), channel_id=1, source_target_pairs={{0,1},{1,0},{2,3},{3,2},{4,5},{5,4},{6,7},{7,6},{8,9},{9,8},{10,11... | collective-permute-start | bytes 393224 | tf_op jit(solution)/shard_map/ppermute | solution.py:469
  46.0 5.0 %collective-permute-start.13 = (bf16[256,256]{1,0:T(8,128)(2,1)S(1)}, bf16[256,256]{1,0:T(8,128)(2,1)S(1)}, u32[]{:S(2)}, u32[]{:S(2)}) collective-permute-start(bf16[256,256]{1,0:T(8,128)(2,1)S(1)} %shard_map.87), channel_id=1, source_target_pairs={{0,4},{1,3},{2,6},{3,1},{4,0},{5,9},{6,2},{7,11},{8,12},{9,5},{10,... | collective-permute-start | bytes 393224 | tf_op jit(solution)/shard_map/ppermute | solution.py:473
  51.1 32.2 %collective-permute-start.14 = (bf16[768,256]{1,0:T(8,128)(2,1)S(1)}, bf16[768,256]{1,0:T(8,128)(2,1)S(1)}, u32[]{:S(2)}, u32[]{:S(2)}) collective-permute-start(bf16[768,256]{1,0:T(8,128)(2,1)S(1)} %shard_map.88), channel_id=1, source_target_pairs={{0,1},{1,0},{2,3},{3,2},{4,5},{5,4},{6,7},{7,6},{8,9},{9,8},{10,11... | collective-permute-start | bytes 1179656 | tf_op jit(solution)/shard_map/ppermute | solution.py:480
  51.8 6.4 %collective-permute-start.18 = (bf16[192,256]{1,0:T(8,128)(2,1)S(1)}, bf16[192,256]{1,0:T(8,128)(2,1)S(1)}, u32[]{:S(2)}, u32[]{:S(2)}) collective-permute-start(bf16[192,256]{1,0:T(8,128)(2,1)S(1)} %get-tuple-element.67), channel_id=1, source_target_pairs={{0,4},{4,0},{8,12},{12,8},{16,20},{20,16},{24,28},{28,24},{1,5},{5... | collective-permute-start | bytes 294920 | tf_op jit(solution)/shard_map/ppermute | solution.py:463
  54.3 7.9 %collective-permute-start.15 = (bf16[96,256]{1,0:T(8,128)(2,1)S(1)}, bf16[96,256]{1,0:T(8,128)(2,1)S(1)}, u32[]{:S(2)}, u32[]{:S(2)}) collective-permute-start(bf16[96,256]{1,0:T(8,128)(2,1)S(1)} %get-tuple-element.63), channel_id=1, source_target_pairs={{0,4},{4,0},{8,12},{12,8},{16,20},{20,16},{24,28},{28,24},{1,5},{5... | collective-permute-start | bytes 147464 | tf_op jit(solution)/shard_map/ppermute | solution.py:463
  54.3 10.1 %collective-permute-start.16 = (bf16[96,256]{1,0:T(8,128)(2,1)S(1)}, bf16[96,256]{1,0:T(8,128)(2,1)S(1)}, u32[]{:S(2)}, u32[]{:S(2)}) collective-permute-start(bf16[96,256]{1,0:T(8,128)(2,1)S(1)} %get-tuple-element.64), channel_id=1, source_target_pairs={{0,8},{4,12},{8,0},{12,4},{16,24},{20,28},{24,16},{28,20},{1,9},{5... | collective-permute-start | bytes 147464 | tf_op jit(solution)/shard_map/ppermute | solution.py:463
  58.2 6.3 %collective-permute-start.17 = (bf16[96,256]{1,0:T(8,128)(2,1)S(1)}, bf16[96,256]{1,0:T(8,128)(2,1)S(1)}, u32[]{:S(2)}, u32[]{:S(2)}) collective-permute-start(bf16[96,256]{1,0:T(8,128)(2,1)S(1)} %get-tuple-element.65), channel_id=1, source_target_pairs={{0,12},{4,8},{8,4},{12,0},{16,28},{20,24},{24,20},{28,16},{1,13},{... | collective-permute-start | bytes 147464 | tf_op jit(solution)/shard_map/ppermute | solution.py:463
  58.2 6.8 %collective-permute-start.19 = (bf16[96,256]{1,0:T(8,128)(2,1)S(1)}, bf16[96,256]{1,0:T(8,128)(2,1)S(1)}, u32[]{:S(2)}, u32[]{:S(2)}) collective-permute-start(bf16[96,256]{1,0:T(8,128)(2,1)S(1)} %get-tuple-element.68), channel_id=1, source_target_pairs={{0,16},{4,20},{8,24},{12,28},{16,0},{20,4},{24,8},{28,12},{1,17},{... | collective-permute-start | bytes 147464 | tf_op jit(solution)/shard_map/ppermute | solution.py:463
  62.2 5.9 %collective-permute-start.20 = (bf16[96,256]{1,0:T(8,128)(2,1)S(1)}, bf16[96,256]{1,0:T(8,128)(2,1)S(1)}, u32[]{:S(2)}, u32[]{:S(2)}) collective-permute-start(bf16[96,256]{1,0:T(8,128)(2,1)S(1)} %get-tuple-element.69), channel_id=1, source_target_pairs={{0,24},{4,28},{8,16},{12,20},{16,8},{20,12},{24,0},{28,4},{1,25},{... | collective-permute-start | bytes 147464 | tf_op jit(solution)/shard_map/ppermute | solution.py:463
  68.1 6.0 %collective-permute-start.22 = (bf16[96,256]{1,0:T(8,128)(2,1)S(1)}, bf16[96,256]{1,0:T(8,128)(2,1)S(1)}, u32[]{:S(2)}, u32[]{:S(2)}) collective-permute-start(bf16[96,256]{1,0:T(8,128)(2,1)S(1)} %shard_map.91.refs_0_), channel_id=1, source_target_pairs={{0,24},{4,28},{8,16},{12,20},{16,8},{20,12},{24,0},{28,4},{1,25},{... | collective-permute-start | bytes 147464 | tf_op jit(solution)/shard_map/ppermute | solution.py:463
  70.5 5.0 %collective-permute-start.21 = (bf16[96,256]{1,0:T(8,128)(2,1)S(1)}, bf16[96,256]{1,0:T(8,128)(2,1)S(1)}, u32[]{:S(2)}, u32[]{:S(2)}) collective-permute-start(bf16[96,256]{1,0:T(8,128)(2,1)S(1)} %shard_map.91.refs_0_), channel_id=1, source_target_pairs={{0,16},{4,20},{8,24},{12,28},{16,0},{20,4},{24,8},{28,12},{1,17},{... | collective-permute-start | bytes 147464 | tf_op jit(solution)/shard_map/ppermute | solution.py:463
  75.5 7.0 %collective-permute-start.23 = (bf16[288,256]{1,0:T(8,128)(2,1)S(1)}, bf16[288,256]{1,0:T(8,128)(2,1)S(1)}, u32[]{:S(2)}, u32[]{:S(2)}) collective-permute-start(bf16[288,256]{1,0:T(8,128)(2,1)S(1)} %shard_map.92), channel_id=1, source_target_pairs={{0,4},{4,0},{8,12},{12,8},{16,20},{20,16},{24,28},{28,24},{1,5},{5... | collective-permute-start | bytes 442376 | tf_op jit(solution)/shard_map/ppermute | solution.py:463
  75.6 5.4 %collective-permute-start.25 = (bf16[96,256]{1,0:T(8,128)(2,1)S(1)}, bf16[96,256]{1,0:T(8,128)(2,1)S(1)}, u32[]{:S(2)}, u32[]{:S(2)}) collective-permute-start(bf16[96,256]{1,0:T(8,128)(2,1)S(1)} %shard_map.91.refs_0_), channel_id=1, source_target_pairs={{0,12},{4,8},{8,4},{12,0},{16,28},{20,24},{24,20},{28,16},{1,13},{... | collective-permute-start | bytes 147464 | tf_op jit(solution)/shard_map/ppermute | solution.py:463
  76.7 5.0 %collective-permute-start.24 = (bf16[96,256]{1,0:T(8,128)(2,1)S(1)}, bf16[96,256]{1,0:T(8,128)(2,1)S(1)}, u32[]{:S(2)}, u32[]{:S(2)}) collective-permute-start(bf16[96,256]{1,0:T(8,128)(2,1)S(1)} %shard_map.91.refs_0_), channel_id=1, source_target_pairs={{0,8},{4,12},{8,0},{12,4},{16,24},{20,28},{24,16},{28,20},{1,9},{5... | collective-permute-start | bytes 147464 | tf_op jit(solution)/shard_map/ppermute | solution.py:463
where the time goes:
time: 84.4 us; the launch traced here: 84.2 us
  starting transfers between devices  41.1 us (49%)
  waiting for transfers between devices  30.6 us (36%)
  Pallas kernels  10.5 us (12%)
  local copies, waits for them, and re-layouts  1.18 us (1%)
  between operations  0.89 us (1%)
    ppermute x11, starting transfers between devices, meet(): return lax.ppermute(a, 'lat', [(i, i ^ bits) for i in range(lats)])  18.6 us
    ppermute x10, starting transfers between devices, send(): return lax.ppermute(array, axis, pairs)  16.8 us
    ppermute x10, waiting for transfers between devices, send(): return lax.ppermute(array, axis, pairs)  14.4 us
    ppermute x11, waiting for transfers between devices, meet(): return lax.ppermute(a, 'lat', [(i, i ^ bits) for i in range(lats)])  9.29 us
    ppermute x1, starting transfers between devices, per_device(): near = lax.ppermute(rim(1 - odd), both, sides[0])  4.02 us
    ppermute x1, waiting for transfers between devices, reduce_weight(): rims = lax.ppermute(rims, ('lat', 'section'), edge_pairs(lats, sections))  3.97 us
    pallas_call x9, Pallas kernels, step_call(): pl.pallas_call(functools.partial(step_kernel, turn, lats, part, form), ou...  2.95 us
    pallas_call x1, Pallas kernels, band_call(): pl.pallas_call(functools.partial(band_kernel, blocks), out_shape=(pltpu.V...  2.37 us
  transfers between devices with their start and end apart: 26, of which 14 were waited for; matrix products, arithmetic and copies ran while one was open for 0% of the time, Pallas kernels for 9%

commit v1 on v0

--- a/solution.py
+++ b/solution.py
@@ -64,8 +64,8 @@
 def slant_pairs(lats, sections, turn, upward):
     last, low = lats - 1, turn - 1
     ways = {(i, turn): (i + 1, low) for i in range(last)}
-    if turn % 2 and sections > 2:
-        aside = (turn - 2) % sections
+    if sections > 2:
+        aside = (turn - 2) % sections if turn % 2 else turn + 1
         ways[last, turn] = (last, aside)
         ways.update({(i, aside): (i - 1, aside) for i in range(1, lats)})
         ways[0, aside] = (0, low)
@@ -148,55 +148,84 @@
     )(*(pltpu.with_memory_space_constraint(a, pltpu.HBM) for a in (block_index, block_mask, quad)))
 
 
-def hidden_kernel(inner, x_ref, band_ref, w_ref, *refs):
+def hidden_kernel(part, x_ref, band_ref, w_ref, *refs):
     hid_ref, gp_ref = refs[-2:]
     pair = HALO * BLK
     deep = KB * pair
     groups = band_ref.shape[0]
     spots = [(g, h) for g in range(groups) for h in range(2)]
-    spots = spots[1:-1] if inner else [spots[0], spots[-1]]
-    odd = lax.axis_index("lat") % 2 == 1
-    parts = []
-    for m in range(MB):
-        for g, h in spots:
-            at = (2 * g + h - 1) * pair
-            if inner:
-                window = x_ref[0, m, at : at + 3 * pair, :]
-            elif g == 0:
-                rim = jnp.where(odd, refs[0][m], refs[1][m])
-                window = jnp.concatenate([rim, x_ref[0, m, : 2 * pair, :]], axis=0)
-            else:
-                rim = jnp.where(odd, refs[1][m], refs[0][m])
-                window = jnp.concatenate([x_ref[0, m, at:, :], rim], axis=0)
-            band = band_ref[g, h * deep : (h + 1) * deep, h * pair : h * pair + 3 * pair]
-            parts.append(dot(band, window).astype(BF))
-            hid_ref[m, g, h * deep : (h + 1) * deep, :] = parts[-1]
-    z = None
-    for k in range(KB):
-        rows = jnp.concatenate([p[k * pair : (k + 1) * pair] for p in parts], axis=0)
-        new = dot(rows, w_ref[0, k])
-        z = new if z is None else z + new
-    gp = gelu_slope(z)
-    for i, (m, g, h) in enumerate((m, g, h) for m in range(MB) for g, h in spots):
-        gp_ref[m, (2 * g + h) * pair : (2 * g + h + 1) * pair, :] = gp[i * pair : (i + 1) * pair]
-
-
-def hidden_call(x, band, weights, *rest):
+
+    def fill(spots):
+        parts = []
+        for m in range(MB):
+            for g, h in spots:
+                at = (2 * g + h - 1) * pair
+                if part == "inner":
+                    window = x_ref[0, m, at : at + 3 * pair, :]
+                elif g == 0:
+                    window = jnp.concatenate([refs[0][m], x_ref[0, m, : 2 * pair, :]], axis=0)
+                else:
+                    window = jnp.concatenate([x_ref[0, m, at:, :], refs[0][m]], axis=0)
+                band = band_ref[g, h * deep : (h + 1) * deep, h * pair : h * pair + 3 * pair]
+                parts.append(dot(band, window).astype(BF))
+                hid_ref[m, g, h * deep : (h + 1) * deep, :] = parts[-1]
+        z = None
+        for k in range(KB):
+            rows = jnp.concatenate([p[k * pair : (k + 1) * pair] for p in parts], axis=0)
+            new = dot(rows, w_ref[0, k])
+            z = new if z is None else z + new
+        gp = gelu_slope(z)
+        for i, (m, g, h) in enumerate((m, g, h) for m in range(MB) for g, h in spots):
+            gp_ref[m, (2 * g + h) * pair : (2 * g + h + 1) * pair, :] = gp[i * pair : (i + 1) * pair]
+
+    if part == "inner":
+        fill(spots[1:-1])
+        return
+    below = (lax.axis_index("lat") % 2 == 0) == (part == "far")
+    pl.when(below)(lambda: fill(spots[:1]))
+    pl.when(jnp.logical_not(below))(lambda: fill(spots[-1:]))
+
+
+def hidden_call(part, x, band, weights, *rest):
     _, mb, rows, ch = x.shape
     args = (x, band, weights) + rest
     return pl.pallas_call(
-        functools.partial(hidden_kernel, not rest),
+        functools.partial(hidden_kernel, part),
         out_shape=(
             pltpu.VMEM((mb, band.shape[0], KB * GRP * BLK, ch), BF),
             pltpu.VMEM((mb, rows, ch), F32),
         ),
         in_specs=[VM] * len(args),
         out_specs=(VM, VM),
-        input_output_aliases={5: 0, 6: 1} if rest else {},
+        input_output_aliases={4: 0, 5: 1} if rest else {},
         compiler_params=params(),
         cost_estimate=None if rest else cost(1 << 30),
-        name="outer" if rest else "inner",
     )(*args)
+
+
+def rim_kernel(x_ref, far_ref, near_ref, sems):
+    rows, edge = x_ref.shape[2], far_ref.shape[1]
+    odd = lax.axis_index("lat") % 2
+    copies = []
+    for i, (high, ref) in enumerate(((odd, far_ref), (1 - odd, near_ref))):
+        at = pl.multiple_of(high * (rows - edge), edge)
+        copies.append(pltpu.make_async_copy(x_ref.at[0, :, pl.ds(at, edge)], ref, sems.at[i]))
+        copies[-1].start()
+    for c in copies:
+        c.wait()
+
+
+def rim_call(x):
+    _, mb, _, ch = x.shape
+    return pl.pallas_call(
+        rim_kernel,
+        out_shape=(pltpu.VMEM((mb, HALO * BLK, ch), BF),) * 2,
+        in_specs=[HB],
+        out_specs=(VM, VM),
+        scratch_shapes=[pltpu.SemaphoreType.DMA((2,))],
+        compiler_params=params(),
+        name="rim",
+    )(pltpu.with_memory_space_constraint(x, pltpu.HBM))
 
 
 PARTS = {
@@ -522,20 +551,17 @@
 def per_device(saved_input, cotangent, quad_values, block_index, block_mask, weights):
     sections = lax.axis_size("section")
     lats = lax.axis_size("lat")
-    edge = HALO * BLK
-    rows = saved_input.shape[2]
     both = ("lat", "section")
     odd = lax.axis_index("lat") % 2
     sides = [near_pairs(lats, sections, side) for side in range(2)]
 
-    def rim(high):
-        return lax.dynamic_slice_in_dim(saved_input[0], high * (rows - edge), edge, axis=1)
-
-    far = lax.ppermute(rim(odd), both, sides[1])
-    near = lax.ppermute(rim(1 - odd), both, sides[0])
+    far, near = rim_call(saved_input)
+    far = lax.ppermute(far, both, sides[1])
+    near = lax.ppermute(near, both, sides[0])
     band, flip = band_call(block_index, block_mask, quad_values)
-    hid, gp = hidden_call(saved_input, band, weights)
-    hid, gp = hidden_call(saved_input, band, weights, near, far, hid, gp)
+    hid, gp = hidden_call("inner", saved_input, band, weights)
+    hid, gp = hidden_call("far", saved_input, band, weights, far, hid, gp)
+    hid, gp = hidden_call("near", saved_input, band, weights, near, hid, gp)
 
     state, grads = {"gp": gp}, (cotangent,)
 

time: 84.4 us -> 84.4 us (level)
  starting transfers between devices: 41.1 us -> 39.2 us
  Pallas kernels: 10.5 us -> 12.1 us
  waiting for transfers between devices: 30.6 us -> 31.8 us
  local copies, waits for them, and re-layouts: 1.18 us -> 0.32 us
    ppermute x10, waiting for transfers between devices: 14.4 us -> 16.3 us  [send(): return lax.ppermute(array, axis, pairs)]
    ppermute x10, starting transfers between devices: 16.8 us -> 14.9 us  [send(): return lax.ppermute(array, axis, pairs)]
    pallas_call x2 -> x4, Pallas kernels: 1.85 us -> 3.46 us  [the longest x3 2.38 us: hidden_call(): pl.pallas_call(functools.partial(hidden_kernel, part), out_shape=(pltpu.V...]
    dynamic_slice x1 -> x0, local copies, waits for them, and re-layouts: 1.07 us -> none  [rim(): lax.dynamic_slice_in_dim(saved_input[0], high * (rows - edge), edge, axis=1)]
  transfers between devices with their start and end apart: 26 -> 26, of which waited for: 14 -> 15; matrix products, arithmetic and copies ran while one was open for 0% -> 0% of each run, Pallas kernels for 9% -> 10%
where the time goes in v1:
time: 84.4 us; the launch traced here: 84.2 us
  starting transfers between devices  39.2 us (46%)
  waiting for transfers between devices  31.8 us (38%)
  Pallas kernels  12.1 us (14%)
  between operations  0.85 us (1%)
    ppermute x11, starting transfers between devices, meet(): return lax.ppermute(a, 'lat', [(i, i ^ bits) for i in range(lats)])  18.5 us
    ppermute x10, waiting for transfers between devices, send(): return lax.ppermute(array, axis, pairs)  16.3 us
    ppermute x10, starting transfers between devices, send(): return lax.ppermute(array, axis, pairs)  14.9 us
    ppermute x11, waiting for transfers between devices, meet(): return lax.ppermute(a, 'lat', [(i, i ^ bits) for i in range(lats)])  9.29 us
    ppermute x1, starting transfers between devices, per_device(): near = lax.ppermute(near, both, sides[0])  4.02 us
    ppermute x1, waiting for transfers between devices, reduce_weight(): rims = lax.ppermute(rims, ('lat', 'section'), edge_pairs(lats, sections))  3.97 us
    pallas_call x9, Pallas kernels, step_call(): pl.pallas_call(functools.partial(step_kernel, turn, lats, part, form), ou...  2.95 us
    pallas_call x3, Pallas kernels, hidden_call(): pl.pallas_call(functools.partial(hidden_kernel, part), out_shape=(pltpu.V...  2.38 us
  transfers between devices with their start and end apart: 26, of which 15 were waited for; matrix products, arithmetic and copies ran while one was open for 0% of the time, Pallas kernels for 10%

profile of v1, /device:TPU:0, one launch (start us, length us, event | category | flops | bytes accessed | tf_op | source)
XLA Modules:
  0.0 84.2 jit_solution(3201266415317891089)
XLA Ops:
  0.6 1.1 %rim.1 = (bf16[2,128,256]{2,1,0:T(8,128)(2,1)S(1)}, bf16[2,128,256]{2,1,0:T(8,128)(2,1)S(1)}) custom-call(bf16[1,2,512,256]{3,2,1,0:T(8,128)(2,1)} %x_ref.7), custom_call_target="tpu_custom_call" | custom-call | tf_op jit(solution)/shard_map/rim/pallas_call | solution.py:220
  1.7 0.6 collective-permute-start.1
  2.3 4.0 %collective-permute-start = (bf16[2,128,256]{2,1,0:T(8,128)(2,1)S(1)}, bf16[2,128,256]{2,1,0:T(8,128)(2,1)S(1)}, u32[]{:S(2)}, u32[]{:S(2)}) collective-permute-start(bf16[2,128,256]{2,1,0:T(8,128)(2,1)S(1)} %get-tuple-element.41), channel_id=1, source_target_pairs={{0,4},{1,5},{2,6},{3,7},{4,0},{5,1},{6,2},{7,3},{8,12},{9,13},{10,... | collective-permute-start | bytes 393224 | tf_op jit(solution)/shard_map/ppermute | solution.py:560
  6.3 2.4 %band.1 = (bf16[2,768,512]{2,1,0:T(8,128)(2,1)S(1)}, bf16[2,512,768]{2,1,0:T(8,128)(2,1)S(1)}) custom-call(s32[8,5]{1,0:T(8,128)} %index_in.1, s32[8,5]{1,0:T(8,128)} %mask_in.1, bf16[3,8,5,64,64]{4,3,2,1,0:T(8,128)(2,1)} %quad_in.1), custom_call_target="tpu_custom_call" | custom-call | tf_op jit(solution)/shard_map/band/pallas_call | solution.py:131
  8.7 0.9 %shard_map.77 = (bf16[2,2,768,256]{3,2,1,0:T(8,128)(2,1)S(1)}, f32[2,512,256]{2,1,0:T(8,128)S(1)}) custom-call(bf16[1,2,512,256]{3,2,1,0:T(8,128)(2,1)S(1)} %copy-done.1, bf16[2,768,512]{2,1,0:T(8,128)(2,1)S(1)} %get-tuple-element.40.band_ref, bf16[1,3,256,256]{3,2,1,0:T(8,128)(2,1)S(1)} %copy-done), custom_call_target="tpu_custom_call" | custom-call | flops 1073741824 | bytes 4194304 | tf_op jit(solution)/shard_map/pallas_call | solution.py:192
  9.6 0.0 collective-permute-done.1.refs_0_
  9.6 0.7 shard_map.78
  10.4 0.8 collective-permute-done.refs_0_
  11.2 0.7 shard_map.79
  12.0 0.3 copy-done.2
  12.3 0.0 collective-permute-start.2
  12.3 2.5 %collective-permute-start.3 = (bf16[2,128,256]{2,1,0:T(8,128)(2,1)S(1)}, bf16[2,128,256]{2,1,0:T(8,128)(2,1)S(1)}, u32[]{:S(2)}, u32[]{:S(2)}) collective-permute-start(bf16[2,128,256]{2,1,0:T(8,128)(2,1)S(1)} %get-tuple-element.50.refs_7_), channel_id=1, source_target_pairs={{3,6},{7,10},{11,14},{15,18},{19,22},{23,26},{27,30},{31,29},{5,1}... | collective-permute-start | bytes 393224 | tf_op jit(solution)/shard_map/ppermute | solution.py:569
  14.8 0.0 collective-permute-start.4
  14.8 4.7 %collective-permute-done.3.refs_4_ = bf16[2,128,256]{2,1,0:T(8,128)(2,1)S(1)} collective-permute-done((bf16[2,128,256]{2,1,0:T(8,128)(2,1)S(1)}, bf16[2,128,256]{2,1,0:T(8,128)(2,1)S(1)}, u32[]{:S(2)}, u32[]{:S(2)}) %collective-permute-start.3) | collective-permute-done | bytes 131104 | tf_op jit(solution)/shard_map/ppermute | solution.py:569
  19.5 1.9 %collective-permute-done.4.refs_5_ = bf16[2,128,256]{2,1,0:T(8,128)(2,1)S(1)} collective-permute-done((bf16[2,128,256]{2,1,0:T(8,128)(2,1)S(1)}, bf16[2,128,256]{2,1,0:T(8,128)(2,1)S(1)}, u32[]{:S(2)}, u32[]{:S(2)}) %collective-permute-start.4) | collective-permute-done | bytes 131104 | tf_op jit(solution)/shard_map/ppermute | solution.py:569
  21.5 0.0 collective-permute-done.2.refs_3_
  21.5 0.6 collective-permute-start.5
  22.1 2.3 %collective-permute-start.6 = (bf16[512,256]{1,0:T(8,128)(2,1)S(1)}, bf16[512,256]{1,0:T(8,128)(2,1)S(1)}, u32[]{:S(2)}, u32[]{:S(2)}) collective-permute-start(bf16[512,256]{1,0:T(8,128)(2,1)S(1)} %get-tuple-element.56), channel_id=1, source_target_pairs={{0,3},{1,0},{2,1},{3,2},{4,7},{5,4},{6,5},{7,6},{8,11},{9,8},{10,9... | collective-permute-start | bytes 786440 | tf_op jit(solution)/shard_map/ppermute | solution.py:569
  24.4 1.9 %collective-permute-start.7 = (bf16[2,128,256]{2,1,0:T(8,128)(2,1)S(1)}, bf16[2,128,256]{2,1,0:T(8,128)(2,1)S(1)}, u32[]{:S(2)}, u32[]{:S(2)}) collective-permute-start(bf16[2,128,256]{2,1,0:T(8,128)(2,1)S(1)} %get-tuple-element.57.refs_8_), channel_id=1, source_target_pairs={{2,5},{6,9},{10,13},{14,17},{18,21},{22,25},{26,29},{30,31},{7,3},... | collective-permute-start | bytes 393224 | tf_op jit(solution)/shard_map/ppermute | solution.py:569
  26.3 0.1 collective-permute-start.8
  26.4 2.9 %collective-permute-done.7.refs_5_ = bf16[2,128,256]{2,1,0:T(8,128)(2,1)S(1)} collective-permute-done((bf16[2,128,256]{2,1,0:T(8,128)(2,1)S(1)}, bf16[2,128,256]{2,1,0:T(8,128)(2,1)S(1)}, u32[]{:S(2)}, u32[]{:S(2)}) %collective-permute-start.7) | collective-permute-done | bytes 131104 | tf_op jit(solution)/shard_map/ppermute | solution.py:569
  29.3 1.9 %collective-permute-done.8.refs_6_ = bf16[2,128,256]{2,1,0:T(8,128)(2,1)S(1)} collective-permute-done((bf16[2,128,256]{2,1,0:T(8,128)(2,1)S(1)}, bf16[2,128,256]{2,1,0:T(8,128)(2,1)S(1)}, u32[]{:S(2)}, u32[]{:S(2)}) %collective-permute-start.8) | collective-permute-done | bytes 131104 | tf_op jit(solution)/shard_map/ppermute | solution.py:569
  31.2 0.0 collective-permute-done.5.refs_3_
  31.2 0.1 collective-permute-done.6.refs_4_
  31.4 5.4 %collective-permute-start.9 = (bf16[2,512,256]{2,1,0:T(8,128)(2,1)S(1)}, bf16[2,512,256]{2,1,0:T(8,128)(2,1)S(1)}, u32[]{:S(2)}, u32[]{:S(2)}) collective-permute-start(bf16[2,512,256]{2,1,0:T(8,128)(2,1)S(1)} %shard_map.85.refs_6_), channel_id=1, source_target_pairs={{0,1},{1,0},{2,3},{3,2},{4,5},{5,4},{6,7},{7,6},{8,9},{9,8},{10,11... | collective-permute-start | bytes 1572872 | tf_op jit(solution)/shard_map/ppermute | solution.py:569
  36.8 0.1 collective-permute-start.10
  36.8 1.9 %collective-permute-start.11 = (bf16[2,128,256]{2,1,0:T(8,128)(2,1)S(1)}, bf16[2,128,256]{2,1,0:T(8,128)(2,1)S(1)}, u32[]{:S(2)}, u32[]{:S(2)}) collective-permute-start(bf16[2,128,256]{2,1,0:T(8,128)(2,1)S(1)} %get-tuple-element.63.refs_6_), channel_id=1, source_target_pairs={{29,24},{25,20},{21,16},{17,12},{13,8},{9,4},{5,0},{1,3},{27,31},{... | collective-permute-start | bytes 393224 | tf_op jit(solution)/shard_map/ppermute | solution.py:569
  38.8 2.4 %collective-permute-done.10.refs_4_ = bf16[2,128,256]{2,1,0:T(8,128)(2,1)S(1)} collective-permute-done((bf16[2,128,256]{2,1,0:T(8,128)(2,1)S(1)}, bf16[2,128,256]{2,1,0:T(8,128)(2,1)S(1)}, u32[]{:S(2)}, u32[]{:S(2)}) %collective-permute-start.10) | collective-permute-done | bytes 131104 | tf_op jit(solution)/shard_map/ppermute | solution.py:569
  41.2 2.3 %collective-permute-done.11.refs_5_ = bf16[2,128,256]{2,1,0:T(8,128)(2,1)S(1)} collective-permute-done((bf16[2,128,256]{2,1,0:T(8,128)(2,1)S(1)}, bf16[2,128,256]{2,1,0:T(8,128)(2,1)S(1)}, u32[]{:S(2)}, u32[]{:S(2)}) %collective-permute-start.11) | collective-permute-done | bytes 131104 | tf_op jit(solution)/shard_map/ppermute | solution.py:569
  43.5 0.0 collective-permute-done.9.refs_3_
  43.5 0.2 shard_map.86
  43.6 0.8 shard_map.88
  44.5 0.1 collective-permute-start.12
  44.6 1.3 %collective-permute-done.12.got_ref = bf16[256,256]{1,0:T(8,128)(2,1)S(1)} collective-permute-done((bf16[256,256]{1,0:T(8,128)(2,1)S(1)}, bf16[256,256]{1,0:T(8,128)(2,1)S(1)}, u32[]{:S(2)}, u32[]{:S(2)}) %collective-permute-start.12) | collective-permute-done | bytes 131104 | tf_op jit(solution)/shard_map/ppermute | solution.py:498
  46.0 1.1 %collective-permute-start.13 = (bf16[256,256]{1,0:T(8,128)(2,1)S(1)}, bf16[256,256]{1,0:T(8,128)(2,1)S(1)}, u32[]{:S(2)}, u32[]{:S(2)}) collective-permute-start(bf16[256,256]{1,0:T(8,128)(2,1)S(1)} %shard_map.90), channel_id=1, source_target_pairs={{0,4},{1,3},{2,6},{3,1},{4,0},{5,9},{6,2},{7,11},{8,12},{9,5},{10,... | collective-permute-start | bytes 393224 | tf_op jit(solution)/shard_map/ppermute | solution.py:502
  47.0 4.0 %collective-permute-done.13.refs_0_.near_ref = bf16[256,256]{1,0:T(8,128)(2,1)S(1)} collective-permute-done((bf16[256,256]{1,0:T(8,128)(2,1)S(1)}, bf16[256,256]{1,0:T(8,128)(2,1)S(1)}, u32[]{:S(2)}, u32[]{:S(2)}) %collective-permute-start.13) | collective-permute-done | bytes 131104 | tf_op jit(solution)/shard_map/ppermute | solution.py:502
  51.0 0.1 collective-permute-start.14
  51.1 0.7 shard_map.92
  51.8 2.5 %collective-permute-start.18 = (bf16[192,256]{1,0:T(8,128)(2,1)S(1)}, bf16[192,256]{1,0:T(8,128)(2,1)S(1)}, u32[]{:S(2)}, u32[]{:S(2)}) collective-permute-start(bf16[192,256]{1,0:T(8,128)(2,1)S(1)} %get-tuple-element.75), channel_id=1, source_target_pairs={{0,4},{4,0},{8,12},{12,8},{16,20},{20,16},{24,28},{28,24},{1,5},{5... | collective-permute-start | bytes 294920 | tf_op jit(solution)/shard_map/ppermute | solution.py:492
  54.3 0.1 collective-permute-start.15
  54.3 3.8 %collective-permute-start.16 = (bf16[96,256]{1,0:T(8,128)(2,1)S(1)}, bf16[96,256]{1,0:T(8,128)(2,1)S(1)}, u32[]{:S(2)}, u32[]{:S(2)}) collective-permute-start(bf16[96,256]{1,0:T(8,128)(2,1)S(1)} %get-tuple-element.72), channel_id=1, source_target_pairs={{0,8},{4,12},{8,0},{12,4},{16,24},{20,28},{24,16},{28,20},{1,9},{5... | collective-permute-start | bytes 147464 | tf_op jit(solution)/shard_map/ppermute | solution.py:492
  58.1 0.0 collective-permute-start.17
  58.2 0.0 collective-permute-done.18.pair_ref
  58.2 4.0 %collective-permute-start.19 = (bf16[96,256]{1,0:T(8,128)(2,1)S(1)}, bf16[96,256]{1,0:T(8,128)(2,1)S(1)}, u32[]{:S(2)}, u32[]{:S(2)}) collective-permute-start(bf16[96,256]{1,0:T(8,128)(2,1)S(1)} %get-tuple-element.76), channel_id=1, source_target_pairs={{0,16},{4,20},{8,24},{12,28},{16,0},{20,4},{24,8},{28,12},{1,17},{... | collective-permute-start | bytes 147464 | tf_op jit(solution)/shard_map/ppermute | solution.py:492
  62.2 0.0 collective-permute-done.15.refs_0_
  62.2 2.2 %collective-permute-start.20 = (bf16[96,256]{1,0:T(8,128)(2,1)S(1)}, bf16[96,256]{1,0:T(8,128)(2,1)S(1)}, u32[]{:S(2)}, u32[]{:S(2)}) collective-permute-start(bf16[96,256]{1,0:T(8,128)(2,1)S(1)} %get-tuple-element.77), channel_id=1, source_target_pairs={{0,24},{4,28},{8,16},{12,20},{16,8},{20,12},{24,0},{28,4},{1,25},{... | collective-permute-start | bytes 147464 | tf_op jit(solution)/shard_map/ppermute | solution.py:492
  64.4 0.0 collective-permute-done.16.refs_1_
  64.4 0.0 collective-permute-done.17.refs_2_
  64.4 0.5 collective-permute-done.19.refs_3_
  64.9 3.1 %collective-permute-done.20.refs_4_ = bf16[96,256]{1,0:T(8,128)(2,1)S(1)} collective-permute-done((bf16[96,256]{1,0:T(8,128)(2,1)S(1)}, bf16[96,256]{1,0:T(8,128)(2,1)S(1)}, u32[]{:S(2)}, u32[]{:S(2)}) %collective-permute-start.20) | collective-permute-done | bytes 49184 | tf_op jit(solution)/shard_map/ppermute | solution.py:492
  68.1 2.4 %collective-permute-start.22 = (bf16[96,256]{1,0:T(8,128)(2,1)S(1)}, bf16[96,256]{1,0:T(8,128)(2,1)S(1)}, u32[]{:S(2)}, u32[]{:S(2)}) collective-permute-start(bf16[96,256]{1,0:T(8,128)(2,1)S(1)} %shard_map.94.refs_0_), channel_id=1, source_target_pairs={{0,24},{4,28},{8,16},{12,20},{16,8},{20,12},{24,0},{28,4},{1,25},{... | collective-permute-start | bytes 147464 | tf_op jit(solution)/shard_map/ppermute | solution.py:492
  70.5 0.0 collective-permute-start.21
  70.5 3.6 %collective-permute-done.22.refs_2_.refs_4_ = bf16[96,256]{1,0:T(8,128)(2,1)S(1)} collective-permute-done((bf16[96,256]{1,0:T(8,128)(2,1)S(1)}, bf16[96,256]{1,0:T(8,128)(2,1)S(1)}, u32[]{:S(2)}, u32[]{:S(2)}) %collective-permute-start.22) | collective-permute-done | bytes 49184 | tf_op jit(solution)/shard_map/ppermute | solution.py:492
  74.1 1.4 %collective-permute-done.21.refs_1_.refs_3_ = bf16[96,256]{1,0:T(8,128)(2,1)S(1)} collective-permute-done((bf16[96,256]{1,0:T(8,128)(2,1)S(1)}, bf16[96,256]{1,0:T(8,128)(2,1)S(1)}, u32[]{:S(2)}, u32[]{:S(2)}) %collective-permute-start.21) | collective-permute-done | bytes 49184 | tf_op jit(solution)/shard_map/ppermute | solution.py:492
  75.5 0.1 collective-permute-start.23
  75.6 1.1 %collective-permute-start.25 = (bf16[96,256]{1,0:T(8,128)(2,1)S(1)}, bf16[96,256]{1,0:T(8,128)(2,1)S(1)}, u32[]{:S(2)}, u32[]{:S(2)}) collective-permute-start(bf16[96,256]{1,0:T(8,128)(2,1)S(1)} %shard_map.94.refs_0_), channel_id=1, source_target_pairs={{0,12},{4,8},{8,4},{12,0},{16,28},{20,24},{24,20},{28,16},{1,13},{... | collective-permute-start | bytes 147464 | tf_op jit(solution)/shard_map/ppermute | solution.py:492
  76.7 2.4 %collective-permute-start.24 = (bf16[96,256]{1,0:T(8,128)(2,1)S(1)}, bf16[96,256]{1,0:T(8,128)(2,1)S(1)}, u32[]{:S(2)}, u32[]{:S(2)}) collective-permute-start(bf16[96,256]{1,0:T(8,128)(2,1)S(1)} %shard_map.94.refs_0_), channel_id=1, source_target_pairs={{0,8},{4,12},{8,0},{12,4},{16,24},{20,28},{24,16},{28,20},{1,9},{5... | collective-permute-start | bytes 147464 | tf_op jit(solution)/shard_map/ppermute | solution.py:492
  79.1 1.9 %shard_map.87.main_ref = bf16[2,512,256]{2,1,0:T(8,128)(2,1)S(1)} custom-call(bf16[2,512,256]{2,1,0:T(8,128)(2,1)S(1)} %get-tuple-element.65.refs_0_.slope_ref, bf16[2,512,768]{2,1,0:T(8,128)(2,1)S(1)} %get-tuple-element.48.refs_1_, bf16[1,3,256,256]{3,2,1,0:T(8,128)(2,1)S(1)} %copy-done, ...), custom_call_target="tpu_custom_call", output_to_operand_aliasing={{}: (6, {})} | custom-call | tf_op jit(solution)/shard_map/pallas_call | solution.py:340
  81.0 0.6 collective-permute-done.24.refs_1_
  81.7 0.8 shard_map.96.refs_1_
  82.5 0.0 collective-permute-done.23.refs_0_
  82.5 0.7 shard_map.97
  83.3 0.0 collective-permute-done.14.far_ref
  83.3 0.9 %grad.1 = bf16[1,2,512,256]{3,2,1,0:T(8,128)(2,1)} custom-call(bf16[2,512,256]{2,1,0:T(8,128)(2,1)S(1)} %shard_map.87.main_ref, bf16[256,256]{1,0:T(8,128)(2,1)S(1)} %collective-permute-done.13.refs_0_.near_ref, bf16[768,256]{1,0:T(8,128)(2,1)S(1)} %collective-permute-done.14.far_ref), custom_call_target="tpu_custom_call" | custom-call | tf_op jit(solution)/shard_map/grad/pallas_call | solution.py:541
  (18 shorter events, 0.2 us)
Async XLA Ops:
  0.6 8.1 %copy-start.1 = (bf16[1,2,512,256]{3,2,1,0:T(8,128)(2,1)S(1)}, bf16[1,2,512,256]{3,2,1,0:T(8,128)(2,1)}, u32[]{:S(2)}) copy-start(bf16[1,2,512,256]{3,2,1,0:T(8,128)(2,1)} %x_ref.7) | copy-start | bytes 1572868
  0.6 8.1 %copy-start = (bf16[1,3,256,256]{3,2,1,0:T(8,128)(2,1)S(1)}, bf16[1,3,256,256]{3,2,1,0:T(8,128)(2,1)}, u32[]{:S(2)}) copy-start(bf16[1,3,256,256]{3,2,1,0:T(8,128)(2,1)} %refs_2_.17) | copy-start | bytes 1179652
  1.7 7.9 %collective-permute-start.1 = (bf16[2,128,256]{2,1,0:T(8,128)(2,1)S(1)}, bf16[2,128,256]{2,1,0:T(8,128)(2,1)S(1)}, u32[]{:S(2)}, u32[]{:S(2)}) collective-permute-start(bf16[2,128,256]{2,1,0:T(8,128)(2,1)S(1)} %get-tuple-element.42), channel_id=1, source_target_pairs={{0,1},{1,0},{2,3},{3,2},{4,8},{5,9},{6,10},{7,11},{8,4},{9,5},{10,... | collective-permute-start | bytes 393224 | tf_op jit(solution)/shard_map/ppermute | solution.py:559
  2.3 8.9 %collective-permute-start = (bf16[2,128,256]{2,1,0:T(8,128)(2,1)S(1)}, bf16[2,128,256]{2,1,0:T(8,128)(2,1)S(1)}, u32[]{:S(2)}, u32[]{:S(2)}) collective-permute-start(bf16[2,128,256]{2,1,0:T(8,128)(2,1)S(1)} %get-tuple-element.41), channel_id=1, source_target_pairs={{0,4},{1,5},{2,6},{3,7},{4,0},{5,1},{6,2},{7,3},{8,12},{9,13},{10,... | collective-permute-start | bytes 393224 | tf_op jit(solution)/shard_map/ppermute | solution.py:560
  11.2 1.0 %copy-start.2 = (bf16[2,512,256]{2,1,0:T(8,128)(2,1)S(1)}, bf16[2,512,256]{2,1,0:T(8,128)(2,1)}, u32[]{:S(2)}) copy-start(bf16[2,512,256]{2,1,0:T(8,128)(2,1)} %refs_3_.3) | copy-start | bytes 1572868
  12.3 9.2 %collective-permute-start.2 = (bf16[2,512,256]{2,1,0:T(8,128)(2,1)S(1)}, bf16[2,512,256]{2,1,0:T(8,128)(2,1)S(1)}, u32[]{:S(2)}, u32[]{:S(2)}) collective-permute-start(bf16[2,512,256]{2,1,0:T(8,128)(2,1)S(1)} %shard_map.81.refs_7_), channel_id=1, source_target_pairs={{0,1},{1,0},{2,3},{3,2},{4,5},{5,4},{6,7},{7,6},{8,9},{9,8},{10,11... | collective-permute-start | bytes 1572872 | tf_op jit(solution)/shard_map/ppermute | solution.py:569
  12.3 7.3 %collective-permute-start.3 = (bf16[2,128,256]{2,1,0:T(8,128)(2,1)S(1)}, bf16[2,128,256]{2,1,0:T(8,128)(2,1)S(1)}, u32[]{:S(2)}, u32[]{:S(2)}) collective-permute-start(bf16[2,128,256]{2,1,0:T(8,128)(2,1)S(1)} %get-tuple-element.50.refs_7_), channel_id=1, source_target_pairs={{3,6},{7,10},{11,14},{15,18},{19,22},{23,26},{27,30},{31,29},{5,1}... | collective-permute-start | bytes 393224 | tf_op jit(solution)/shard_map/ppermute | solution.py:569
  14.8 6.7 %collective-permute-start.4 = (bf16[2,128,256]{2,1,0:T(8,128)(2,1)S(1)}, bf16[2,128,256]{2,1,0:T(8,128)(2,1)S(1)}, u32[]{:S(2)}, u32[]{:S(2)}) collective-permute-start(bf16[2,128,256]{2,1,0:T(8,128)(2,1)S(1)} %get-tuple-element.51.refs_6_), channel_id=1, source_target_pairs={{31,26},{27,22},{23,18},{19,14},{15,10},{11,6},{7,2},{3,1},{25,29}... | collective-permute-start | bytes 393224 | tf_op jit(solution)/shard_map/ppermute | solution.py:569
  21.5 9.7 %collective-permute-start.5 = (bf16[512,256]{1,0:T(8,128)(2,1)S(1)}, bf16[512,256]{1,0:T(8,128)(2,1)S(1)}, u32[]{:S(2)}, u32[]{:S(2)}) collective-permute-start(bf16[512,256]{1,0:T(8,128)(2,1)S(1)} %get-tuple-element.52), channel_id=1, source_target_pairs={{0,3},{1,0},{2,1},{3,2},{4,7},{5,4},{6,5},{7,6},{8,11},{9,8},{10,9... | collective-permute-start | bytes 786440 | tf_op jit(solution)/shard_map/ppermute | solution.py:569
  22.1 9.3 %collective-permute-start.6 = (bf16[512,256]{1,0:T(8,128)(2,1)S(1)}, bf16[512,256]{1,0:T(8,128)(2,1)S(1)}, u32[]{:S(2)}, u32[]{:S(2)}) collective-permute-start(bf16[512,256]{1,0:T(8,128)(2,1)S(1)} %get-tuple-element.56), channel_id=1, source_target_pairs={{0,3},{1,0},{2,1},{3,2},{4,7},{5,4},{6,5},{7,6},{8,11},{9,8},{10,9... | collective-permute-start | bytes 786440 | tf_op jit(solution)/shard_map/ppermute | solution.py:569
  24.4 5.0 %collective-permute-start.7 = (bf16[2,128,256]{2,1,0:T(8,128)(2,1)S(1)}, bf16[2,128,256]{2,1,0:T(8,128)(2,1)S(1)}, u32[]{:S(2)}, u32[]{:S(2)}) collective-permute-start(bf16[2,128,256]{2,1,0:T(8,128)(2,1)S(1)} %get-tuple-element.57.refs_8_), channel_id=1, source_target_pairs={{2,5},{6,9},{10,13},{14,17},{18,21},{22,25},{26,29},{30,31},{7,3},... | collective-permute-start | bytes 393224 | tf_op jit(solution)/shard_map/ppermute | solution.py:569
  26.3 5.0 %collective-permute-start.8 = (bf16[2,128,256]{2,1,0:T(8,128)(2,1)S(1)}, bf16[2,128,256]{2,1,0:T(8,128)(2,1)S(1)}, u32[]{:S(2)}, u32[]{:S(2)}) collective-permute-start(bf16[2,128,256]{2,1,0:T(8,128)(2,1)S(1)} %get-tuple-element.58.refs_7_), channel_id=1, source_target_pairs={{30,25},{26,21},{22,17},{18,13},{14,9},{10,5},{6,1},{2,3},{27,31},... | collective-permute-start | bytes 393224 | tf_op jit(solution)/shard_map/ppermute | solution.py:569
  31.4 12.1 %collective-permute-start.9 = (bf16[2,512,256]{2,1,0:T(8,128)(2,1)S(1)}, bf16[2,512,256]{2,1,0:T(8,128)(2,1)S(1)}, u32[]{:S(2)}, u32[]{:S(2)}) collective-permute-start(bf16[2,512,256]{2,1,0:T(8,128)(2,1)S(1)} %shard_map.85.refs_6_), channel_id=1, source_target_pairs={{0,1},{1,0},{2,3},{3,2},{4,5},{5,4},{6,7},{7,6},{8,9},{9,8},{10,11... | collective-permute-start | bytes 1572872 | tf_op jit(solution)/shard_map/ppermute | solution.py:569
  36.8 4.4 %collective-permute-start.10 = (bf16[2,128,256]{2,1,0:T(8,128)(2,1)S(1)}, bf16[2,128,256]{2,1,0:T(8,128)(2,1)S(1)}, u32[]{:S(2)}, u32[]{:S(2)}) collective-permute-start(bf16[2,128,256]{2,1,0:T(8,128)(2,1)S(1)} %get-tuple-element.62.refs_7_), channel_id=1, source_target_pairs={{1,4},{5,8},{9,12},{13,16},{17,20},{21,24},{25,28},{29,31},{7,3},{... | collective-permute-start | bytes 393224 | tf_op jit(solution)/shard_map/ppermute | solution.py:569
  36.8 6.6 %collective-permute-start.11 = (bf16[2,128,256]{2,1,0:T(8,128)(2,1)S(1)}, bf16[2,128,256]{2,1,0:T(8,128)(2,1)S(1)}, u32[]{:S(2)}, u32[]{:S(2)}) collective-permute-start(bf16[2,128,256]{2,1,0:T(8,128)(2,1)S(1)} %get-tuple-element.63.refs_6_), channel_id=1, source_target_pairs={{29,24},{25,20},{21,16},{17,12},{13,8},{9,4},{5,0},{1,3},{27,31},{... | collective-permute-start | bytes 393224 | tf_op jit(solution)/shard_map/ppermute | solution.py:569
  44.5 1.4 %collective-permute-start.12 = (bf16[256,256]{1,0:T(8,128)(2,1)S(1)}, bf16[256,256]{1,0:T(8,128)(2,1)S(1)}, u32[]{:S(2)}, u32[]{:S(2)}) collective-permute-start(bf16[256,256]{1,0:T(8,128)(2,1)S(1)} %shard_map.89), channel_id=1, source_target_pairs={{0,1},{1,0},{2,3},{3,2},{4,5},{5,4},{6,7},{7,6},{8,9},{9,8},{10,11... | collective-permute-start | bytes 393224 | tf_op jit(solution)/shard_map/ppermute | solution.py:498
  46.0 5.0 %collective-permute-start.13 = (bf16[256,256]{1,0:T(8,128)(2,1)S(1)}, bf16[256,256]{1,0:T(8,128)(2,1)S(1)}, u32[]{:S(2)}, u32[]{:S(2)}) collective-permute-start(bf16[256,256]{1,0:T(8,128)(2,1)S(1)} %shard_map.90), channel_id=1, source_target_pairs={{0,4},{1,3},{2,6},{3,1},{4,0},{5,9},{6,2},{7,11},{8,12},{9,5},{10,... | collective-permute-start | bytes 393224 | tf_op jit(solution)/shard_map/ppermute | solution.py:502
  51.0 32.2 %collective-permute-start.14 = (bf16[768,256]{1,0:T(8,128)(2,1)S(1)}, bf16[768,256]{1,0:T(8,128)(2,1)S(1)}, u32[]{:S(2)}, u32[]{:S(2)}) collective-permute-start(bf16[768,256]{1,0:T(8,128)(2,1)S(1)} %shard_map.91), channel_id=1, source_target_pairs={{0,1},{1,0},{2,3},{3,2},{4,5},{5,4},{6,7},{7,6},{8,9},{9,8},{10,11... | collective-permute-start | bytes 1179656 | tf_op jit(solution)/shard_map/ppermute | solution.py:509
  51.8 6.4 %collective-permute-start.18 = (bf16[192,256]{1,0:T(8,128)(2,1)S(1)}, bf16[192,256]{1,0:T(8,128)(2,1)S(1)}, u32[]{:S(2)}, u32[]{:S(2)}) collective-permute-start(bf16[192,256]{1,0:T(8,128)(2,1)S(1)} %get-tuple-element.75), channel_id=1, source_target_pairs={{0,4},{4,0},{8,12},{12,8},{16,20},{20,16},{24,28},{28,24},{1,5},{5... | collective-permute-start | bytes 294920 | tf_op jit(solution)/shard_map/ppermute | solution.py:492
  54.3 7.9 %collective-permute-start.15 = (bf16[96,256]{1,0:T(8,128)(2,1)S(1)}, bf16[96,256]{1,0:T(8,128)(2,1)S(1)}, u32[]{:S(2)}, u32[]{:S(2)}) collective-permute-start(bf16[96,256]{1,0:T(8,128)(2,1)S(1)} %get-tuple-element.71), channel_id=1, source_target_pairs={{0,4},{4,0},{8,12},{12,8},{16,20},{20,16},{24,28},{28,24},{1,5},{5... | collective-permute-start | bytes 147464 | tf_op jit(solution)/shard_map/ppermute | solution.py:492
  54.3 10.1 %collective-permute-start.16 = (bf16[96,256]{1,0:T(8,128)(2,1)S(1)}, bf16[96,256]{1,0:T(8,128)(2,1)S(1)}, u32[]{:S(2)}, u32[]{:S(2)}) collective-permute-start(bf16[96,256]{1,0:T(8,128)(2,1)S(1)} %get-tuple-element.72), channel_id=1, source_target_pairs={{0,8},{4,12},{8,0},{12,4},{16,24},{20,28},{24,16},{28,20},{1,9},{5... | collective-permute-start | bytes 147464 | tf_op jit(solution)/shard_map/ppermute | solution.py:492
  58.1 6.3 %collective-permute-start.17 = (bf16[96,256]{1,0:T(8,128)(2,1)S(1)}, bf16[96,256]{1,0:T(8,128)(2,1)S(1)}, u32[]{:S(2)}, u32[]{:S(2)}) collective-permute-start(bf16[96,256]{1,0:T(8,128)(2,1)S(1)} %get-tuple-element.73), channel_id=1, source_target_pairs={{0,12},{4,8},{8,4},{12,0},{16,28},{20,24},{24,20},{28,16},{1,13},{... | collective-permute-start | bytes 147464 | tf_op jit(solution)/shard_map/ppermute | solution.py:492
  58.2 6.8 %collective-permute-start.19 = (bf16[96,256]{1,0:T(8,128)(2,1)S(1)}, bf16[96,256]{1,0:T(8,128)(2,1)S(1)}, u32[]{:S(2)}, u32[]{:S(2)}) collective-permute-start(bf16[96,256]{1,0:T(8,128)(2,1)S(1)} %get-tuple-element.76), channel_id=1, source_target_pairs={{0,16},{4,20},{8,24},{12,28},{16,0},{20,4},{24,8},{28,12},{1,17},{... | collective-permute-start | bytes 147464 | tf_op jit(solution)/shard_map/ppermute | solution.py:492
  62.2 5.9 %collective-permute-start.20 = (bf16[96,256]{1,0:T(8,128)(2,1)S(1)}, bf16[96,256]{1,0:T(8,128)(2,1)S(1)}, u32[]{:S(2)}, u32[]{:S(2)}) collective-permute-start(bf16[96,256]{1,0:T(8,128)(2,1)S(1)} %get-tuple-element.77), channel_id=1, source_target_pairs={{0,24},{4,28},{8,16},{12,20},{16,8},{20,12},{24,0},{28,4},{1,25},{... | collective-permute-start | bytes 147464 | tf_op jit(solution)/shard_map/ppermute | solution.py:492
  68.1 6.0 %collective-permute-start.22 = (bf16[96,256]{1,0:T(8,128)(2,1)S(1)}, bf16[96,256]{1,0:T(8,128)(2,1)S(1)}, u32[]{:S(2)}, u32[]{:S(2)}) collective-permute-start(bf16[96,256]{1,0:T(8,128)(2,1)S(1)} %shard_map.94.refs_0_), channel_id=1, source_target_pairs={{0,24},{4,28},{8,16},{12,20},{16,8},{20,12},{24,0},{28,4},{1,25},{... | collective-permute-start | bytes 147464 | tf_op jit(solution)/shard_map/ppermute | solution.py:492
  70.5 5.0 %collective-permute-start.21 = (bf16[96,256]{1,0:T(8,128)(2,1)S(1)}, bf16[96,256]{1,0:T(8,128)(2,1)S(1)}, u32[]{:S(2)}, u32[]{:S(2)}) collective-permute-start(bf16[96,256]{1,0:T(8,128)(2,1)S(1)} %shard_map.94.refs_0_), channel_id=1, source_target_pairs={{0,16},{4,20},{8,24},{12,28},{16,0},{20,4},{24,8},{28,12},{1,17},{... | collective-permute-start | bytes 147464 | tf_op jit(solution)/shard_map/ppermute | solution.py:492
  75.5 7.0 %collective-permute-start.23 = (bf16[288,256]{1,0:T(8,128)(2,1)S(1)}, bf16[288,256]{1,0:T(8,128)(2,1)S(1)}, u32[]{:S(2)}, u32[]{:S(2)}) collective-permute-start(bf16[288,256]{1,0:T(8,128)(2,1)S(1)} %shard_map.95), channel_id=1, source_target_pairs={{0,4},{4,0},{8,12},{12,8},{16,20},{20,16},{24,28},{28,24},{1,5},{5... | collective-permute-start | bytes 442376 | tf_op jit(solution)/shard_map/ppermute | solution.py:492
  75.6 5.4 %collective-permute-start.25 = (bf16[96,256]{1,0:T(8,128)(2,1)S(1)}, bf16[96,256]{1,0:T(8,128)(2,1)S(1)}, u32[]{:S(2)}, u32[]{:S(2)}) collective-permute-start(bf16[96,256]{1,0:T(8,128)(2,1)S(1)} %shard_map.94.refs_0_), channel_id=1, source_target_pairs={{0,12},{4,8},{8,4},{12,0},{16,28},{20,24},{24,20},{28,16},{1,13},{... | collective-permute-start | bytes 147464 | tf_op jit(solution)/shard_map/ppermute | solution.py:492
  76.7 5.0 %collective-permute-start.24 = (bf16[96,256]{1,0:T(8,128)(2,1)S(1)}, bf16[96,256]{1,0:T(8,128)(2,1)S(1)}, u32[]{:S(2)}, u32[]{:S(2)}) collective-permute-start(bf16[96,256]{1,0:T(8,128)(2,1)S(1)} %shard_map.94.refs_0_), channel_id=1, source_target_pairs={{0,8},{4,12},{8,0},{12,4},{16,24},{20,28},{24,16},{28,20},{1,9},{5... | collective-permute-start | bytes 147464 | tf_op jit(solution)/shard_map/ppermute | solution.py:492

commit v2 on v1

--- a/solution.py
+++ b/solution.py
@@ -61,22 +61,16 @@
     return [(s, (s - 1) % sections) for s in range(sections)]
 
 
-def slant_pairs(lats, sections, turn, upward):
-    last, low = lats - 1, turn - 1
-    ways = {(i, turn): (i + 1, low) for i in range(last)}
-    if sections > 2:
-        aside = (turn - 2) % sections if turn % 2 else turn + 1
-        ways[last, turn] = (last, aside)
-        ways.update({(i, aside): (i - 1, aside) for i in range(1, lats)})
-        ways[0, aside] = (0, low)
-        ways.update({(i, low): (i, turn) for i in range(lats)})
-        for i in range(lats):
-            for s in range(sections):
-                ways.setdefault((i, s), (i ^ 1, s))
-        assert len(set(ways.values())) == lats * sections
-    if not upward:
-        ways = {(last - i, s): (last - j, r) for (i, s), (j, r) in ways.items()}
-    return [(i * sections + s, j * sections + r) for (i, s), (j, r) in ways.items()]
+def mate_pairs(lats, sections, turn, side):
+    pairs = []
+    for i in range(lats):
+        j = i ^ 1 if side == 0 else (i + 1 if i % 2 else i - 1)
+        inside = 0 <= j < lats
+        if turn % 2:
+            pairs += [(i * sections + s, i * sections + (s ^ 1)) for s in range(sections) if s != turn]
+        if turn % 2 or inside:
+            pairs.append((i * sections + turn, (j if inside else i) * sections + turn - 1))
+    return pairs
 
 
 def cost(flops):
@@ -229,12 +223,14 @@
 
 
 PARTS = {
-    "edge": ("left", "right", "slope"),
+    "far": ("far", "slope"),
+    "near": ("near", "slope"),
+    "edge": ("near", "far", "slope"),
     "slope": ("slope", "done"),
-    "tips": ("left", "right"),
+    "tips": ("near", "far"),
     "bulk": ("out",),
     "head": ("slope", "done", "out", "sent0"),
-    "tail": ("left", "right", "slope", "done", "out", "sent1"),
+    "tail": ("near", "far", "slope", "done", "out", "sent1"),
 }
 MICROS = {"head": (0,), "tail": (1,)}
 
@@ -253,6 +249,7 @@
     outs, (stack_ref, term_ref) = dict(zip(PARTS[part], refs[-2 - len(PARTS[part]) :])), refs[-2:]
     (gp_ref, flip_ref, w_ref), rest = refs[:3], refs[3:]
     lat = lax.axis_index("lat")
+    odd = lat % 2 == 1
     rows = gp_ref.shape[1]
     size = GRP * BLK
     edge = HALO * BLK
@@ -267,23 +264,36 @@
         grad = (rest[m][at, :] if form == "micro" else rest[0][m, at, :]).astype(F32)
         if form == "whole":
             return grad
-        below_ref, above_ref = rest[MB : MB + 2] if form == "micro" else rest[1:3]
+        near_ref, far_ref = rest[MB : MB + 2] if form == "micro" else rest[1:3]
         parts = [grad[i * edge : (i + 1) * edge] for i in range(size // edge)]
         if g == 0:
-            parts[0] += jnp.where(lat > 0, below_ref[m].astype(F32), 0.0)
+            below = jnp.where(odd, near_ref[m], far_ref[m]).astype(F32)
+            parts[0] += jnp.where(lat > 0, below, 0.0)
         if g == groups - 1:
-            parts[-1] += jnp.where(lat < lats - 1, above_ref[m].astype(F32), 0.0)
+            above = jnp.where(odd, far_ref[m], near_ref[m]).astype(F32)
+            parts[-1] += jnp.where(lat < lats - 1, above, 0.0)
         return jnp.concatenate(parts, axis=0).astype(BF).astype(F32)
 
-    def tips():
-        rims = [slope_ref[m, at : at + edge, :] for m in range(MB) for at in (0, rows - edge)]
+    def tips(names):
+        deep = KB * edge
+        sides = [(name, above) for name, above in zip(names, (False, True)) if name]
+        rims = [slope_ref[m, (rows - edge) * up : (rows - edge) * up + edge, :] for m in range(MB) for _, up in sides]
         back_terms(jnp.concatenate(rims, axis=0), w_ref, stack_ref)
-        deep = KB * edge
         for m in range(MB):
-            low = stack_ref[2 * m * deep : (2 * m + 1) * deep, :]
-            outs["left"][m] = dot(flip_ref[0, :edge, :deep], low).astype(BF)
-            high = stack_ref[(2 * m + 1) * deep : (2 * m + 2) * deep, :]
-            outs["right"][m] = dot(flip_ref[groups - 1, size + edge :, deep:], high).astype(BF)
+            for i, (name, above) in enumerate(sides):
+                at = (m * len(sides) + i) * deep
+                band = flip_ref[groups - 1, size + edge :, deep:] if above else flip_ref[0, :edge, :deep]
+                outs[name][m] = dot(band, stack_ref[at : at + deep, :]).astype(BF)
+
+    def half(even_part):
+        above = not even_part if part == "far" else even_part
+        for m in range(MB):
+            mine = slice(rows - edge, rows) if above else slice(0, edge)
+            others = slice(edge, rows) if above else slice(0, rows - edge)
+            at = mine if part == "far" else others
+            grad = rest[0][m, at, :].astype(F32)
+            outs["slope"][m, at, :] = (grad * gp_ref[m, at, :]).astype(BF)
+        tips((None, part) if above else (part, None))
 
     def slopes():
         for m in micros:
@@ -317,13 +327,18 @@
 
     @pl.when(lax.axis_index("section") == turn)
     def _():
+        if part in ("far", "near"):
+            pl.when(odd)(lambda: half(False))
+            pl.when(jnp.logical_not(odd))(lambda: half(True))
+            return
         if "slope" in outs:
             slopes()
         if "out" in outs:
             for m in micros:
                 terms(m)
-        if "left" in outs:
-            tips()
+        if "near" in outs:
+            pl.when(odd)(lambda: tips(("near", "far")))
+            pl.when(jnp.logical_not(odd))(lambda: tips(("far", "near")))
 
 
 def step_call(turn, lats, part, grads, flip, weights, state):
@@ -334,7 +349,7 @@
     form = {1: "whole", 3: "summed", 4: "micro"}[len(grads)]
     factor = state["gp" if "slope" in names else "slope"]
     args = (factor, flip, weights) + grads + tuple(state[name] for name in known)
-    tall = {"left": edge, "right": edge, "done": 2 * edge}
+    tall = {"near": edge, "far": edge, "done": 2 * edge}
     shapes = {name: (mb, tall.get(name, rows), ch) for name in names}
     shapes.update({name: (rows, ch) for name in names if name.startswith("sent")})
     outs = pl.pallas_call(
@@ -384,11 +399,6 @@
     )(hid, slope)
 
 
-def lay_edges(even_ref, odd_ref):
-    odd = lax.axis_index("lat") % 2 == 1
-    return jnp.concatenate([jnp.where(odd, odd_ref[m], even_ref[m]) for m in range(MB)], axis=0)
-
-
 def cut_kernel(hid_ref, slope_ref, own_ref, one_ref, pair_ref, two_ref, three_ref, far_ref, acc_ref):
     weight_terms(hid_ref, slope_ref, acc_ref)
     me = lax.axis_index("lat")
@@ -413,10 +423,6 @@
     six_ref[...] = (far_ref[piece:, :] + pair_ref[piece:, :].astype(F32)).astype(BF)
 
 
-def give_kernel(left_ref, right_ref, out_ref):
-    out_ref[...] = lay_edges(left_ref, right_ref)
-
-
 def sum_kernel(own_ref, *refs):
     total = own_ref[...]
     for ref in refs[:-1]:
@@ -432,9 +438,11 @@
             at += value.shape[0]
 
 
-def rims_kernel(got_ref, left_ref, right_ref, out_ref):
+def rims_kernel(got_ref, near_ref, out_ref):
     second = lax.axis_index("section") % 2 == 1
-    out_ref[...] = jnp.where(second, got_ref[...], lay_edges(right_ref, left_ref))
+    edge = near_ref.shape[1]
+    for m in range(MB):
+        out_ref[m * edge : (m + 1) * edge, :] = jnp.where(second, got_ref[m], near_ref[m])
 
 
 def join_kernel(spots, piece, *refs):
@@ -479,10 +487,10 @@
 
 
 def reduce_weight(lats, sections, hid, state):
-    left, right, slope, done = (state[name] for name in ("left", "right", "slope", "done"))
+    near, far, slope, done = (state[name] for name in ("near", "far", "slope", "done"))
     ch = slope.shape[2]
     piece = KB * ch // lats
-    edges = MB * left.shape[1]
+    edges = MB * near.shape[1]
     swap = [(s, s ^ 1) for s in range(sections)]
 
     def vmem(rows, dtype=BF):
@@ -492,13 +500,12 @@
         return lax.ppermute(a, "lat", [(i, i ^ bits) for i in range(lats)])
 
     shapes = (vmem(piece, F32), vmem(piece), vmem(2 * piece), vmem(piece), vmem(piece), vmem(2 * piece, F32))
-    own, one, pair, two, three, far = small_call(cut_kernel, shapes, hid, slope, scratch=(vmem(KB * ch, F32),))
+    own, one, pair, two, three, half = small_call(cut_kernel, shapes, hid, slope, scratch=(vmem(KB * ch, F32),))
     pair, two, three, one = meet(pair, 1), meet(two, 2), meet(three, 3), meet(one, 1)
-    (give,) = small_call(give_kernel, (vmem(edges),), left, right)
-    got = lax.ppermute(give, "section", swap)
-    four, six = small_call(middle_kernel, (vmem(piece), vmem(piece)), far, pair)
+    got = lax.ppermute(far, "section", swap)
+    four, six = small_call(middle_kernel, (vmem(piece), vmem(piece)), half, pair)
     four, six = meet(four, 4), meet(six, 6)
-    (rims,) = small_call(rims_kernel, (vmem(edges),), got, left, right)
+    (rims,) = small_call(rims_kernel, (vmem(edges),), got, near)
     rims = lax.ppermute(rims, ("lat", "section"), edge_pairs(lats, sections))
     (mine,) = small_call(sum_kernel, (vmem(piece),), own, one, two, three, four, six)
     four, six = meet(mine, 4), meet(mine, 6)
@@ -552,8 +559,10 @@
     sections = lax.axis_size("section")
     lats = lax.axis_size("lat")
     both = ("lat", "section")
-    odd = lax.axis_index("lat") % 2
     sides = [near_pairs(lats, sections, side) for side in range(2)]
+
+    def send(array, pairs, axis=both):
+        return lax.ppermute(array, axis, pairs)
 
     far, near = rim_call(saved_input)
     far = lax.ppermute(far, both, sides[1])
@@ -561,41 +570,42 @@
     band, flip = band_call(block_index, block_mask, quad_values)
     hid, gp = hidden_call("inner", saved_input, band, weights)
     hid, gp = hidden_call("far", saved_input, band, weights, far, hid, gp)
-    hid, gp = hidden_call("near", saved_input, band, weights, near, hid, gp)
 
     state, grads = {"gp": gp}, (cotangent,)
-
-    def send(array, pairs, axis=both):
-        return lax.ppermute(array, axis, pairs)
-
     for turn in reversed(range(sections)):
-        if turn == 0:
+        if turn == sections - 1:
+            step_call(turn, lats, "far", grads, flip, weights, state)
+            hid, gp = hidden_call("near", saved_input, band, weights, near, hid, gp)
+            state["gp"] = gp
+            step_call(turn, lats, "near", grads, flip, weights, state)
+        elif turn == 0:
             step_call(turn, lats, "slope", grads, flip, weights, state)
             step_call(turn, lats, "tips", grads, flip, weights, state)
-            step_call(turn, lats, "bulk", grads, flip, weights, state)
-            continue
-        if turn % 2:
+        elif turn % 2:
             step_call(turn, lats, "edge", grads, flip, weights, state)
+        if turn % 2 or turn == 0:
             step_call(turn, lats, "bulk", grads, flip, weights, state)
             sent = {"main": state["out"]}
         else:
             step_call(turn, lats, "head", grads, flip, weights, state)
             step_call(turn, lats, "tail", grads, flip, weights, state)
             sent = {"main0": state["sent0"], "main1": state["sent1"]}
-        hop = hop_pairs(sections, turn)
-        grads = tuple(send(array, hop, "section") for array in sent.values())
-        low = send(state["right"], slant_pairs(lats, sections, turn, True))
-        high = send(state["left"], slant_pairs(lats, sections, turn, False))
-        grads += (low, high)
-
-    left, right, slope = (state[name] for name in PARTS["edge"])
+        if turn > 0:
+            hop = hop_pairs(sections, turn)
+            grads = tuple(send(array, hop, "section") for array in sent.values())
+            far = send(state["far"], mate_pairs(lats, sections, turn, 1))
+            near = send(state["near"], mate_pairs(lats, sections, turn, 0))
+            grads += (near, far)
+
+    near, far, slope = (state[name] for name in PARTS["edge"])
     channels = saved_input.shape[3]
     if lats == 8 and sections % 2 == 0:
         weight, near, far = reduce_weight(lats, sections, hid, state)
         grad = grad_call(lats, state["out"], near, far)
     else:
-        give = jnp.where(odd == 1, left, right), jnp.where(odd == 1, right, left)
-        near, far = (lax.ppermute(g, both, p).reshape(-1, channels) for g, p in zip(give, sides))
+        near, far = (
+            lax.ppermute(a, both, p).reshape(-1, channels) for a, p in zip((near, far), sides)
+        )
         weight = lax.psum(weight_call(hid, slope), "lat")
         grad = grad_call(lats, state["out"], near, far)
     return grad, weight.reshape(1, KB, channels, channels)

time: 84.4 us -> 83.1 us (0.985)
  waiting for transfers between devices: 31.8 us -> 24 us
  starting transfers between devices: 39.2 us -> 45.7 us
    ppermute x10, waiting for transfers between devices: 16.3 us -> 8.56 us  [send(): return lax.ppermute(array, axis, pairs)]
    ppermute x10, starting transfers between devices: 14.9 us -> 20.2 us  [send(): return lax.ppermute(array, axis, pairs)]
    ppermute x1, starting transfers between devices: 1.06 us -> 3.54 us  [reduce_weight(): rims = lax.ppermute(rims, ('lat', 'section'), edge_pairs(lats, sections))]
    ppermute x11, starting transfers between devices: 18.5 us -> 17 us  [meet(): return lax.ppermute(a, 'lat', [(i, i ^ bits) for i in range(lats)])]
    pallas_call x9 -> x10, Pallas kernels: 2.95 us -> 2.84 us  [step_call(): pl.pallas_call(functools.partial(step_kernel, turn, lats, part, form), ou...]
  transfers between devices with their start and end apart: 26 -> 26, of which waited for: 15 -> 14; matrix products, arithmetic and copies ran while one was open for 0% -> 0% of each run, Pallas kernels for 10% -> 10%
where the time goes in v2:
time: 83.1 us; the launch traced here: 82.9 us
  starting transfers between devices  45.7 us (55%)
  waiting for transfers between devices  24 us (29%)
  Pallas kernels  11.9 us (14%)
  between operations  0.88 us (1%)
    ppermute x10, starting transfers between devices, send(): return lax.ppermute(array, axis, pairs)  20.2 us
    ppermute x11, starting transfers between devices, meet(): return lax.ppermute(a, 'lat', [(i, i ^ bits) for i in range(lats)])  17 us
    ppermute x11, waiting for transfers between devices, meet(): return lax.ppermute(a, 'lat', [(i, i ^ bits) for i in range(lats)])  9.94 us
    ppermute x10, waiting for transfers between devices, send(): return lax.ppermute(array, axis, pairs)  8.56 us
    ppermute x1, starting transfers between devices, per_device(): near = lax.ppermute(near, both, sides[0])  4.02 us
    ppermute x1, waiting for transfers between devices, reduce_weight(): rims = lax.ppermute(rims, ('lat', 'section'), edge_pairs(lats, sections))  3.89 us
    ppermute x1, starting transfers between devices, reduce_weight(): rims = lax.ppermute(rims, ('lat', 'section'), edge_pairs(lats, sections))  3.54 us
    pallas_call x10, Pallas kernels, step_call(): pl.pallas_call(functools.partial(step_kernel, turn, lats, part, form), ou...  2.84 us
  transfers between devices with their start and end apart: 26, of which 14 were waited for; matrix products, arithmetic and copies ran while one was open for 0% of the time, Pallas kernels for 10%

profile of v2, /device:TPU:0, one launch (start us, length us, event | category | flops | bytes accessed | tf_op | source)
XLA Modules:
  0.0 82.9 jit_solution(11154606310846012094)
XLA Ops:
  0.6 1.1 %rim.1 = (bf16[2,128,256]{2,1,0:T(8,128)(2,1)S(1)}, bf16[2,128,256]{2,1,0:T(8,128)(2,1)S(1)}) custom-call(bf16[1,2,512,256]{3,2,1,0:T(8,128)(2,1)} %x_ref.7), custom_call_target="tpu_custom_call" | custom-call | tf_op jit(solution)/shard_map/rim/pallas_call | solution.py:214
  1.7 0.6 collective-permute-start.1
  2.3 4.0 %collective-permute-start = (bf16[2,128,256]{2,1,0:T(8,128)(2,1)S(1)}, bf16[2,128,256]{2,1,0:T(8,128)(2,1)S(1)}, u32[]{:S(2)}, u32[]{:S(2)}) collective-permute-start(bf16[2,128,256]{2,1,0:T(8,128)(2,1)S(1)} %get-tuple-element.42), channel_id=1, source_target_pairs={{0,4},{1,5},{2,6},{3,7},{4,0},{5,1},{6,2},{7,3},{8,12},{9,13},{10,... | collective-permute-start | bytes 393224 | tf_op jit(solution)/shard_map/ppermute | solution.py:569
  6.3 2.4 %band.1 = (bf16[2,768,512]{2,1,0:T(8,128)(2,1)S(1)}, bf16[2,512,768]{2,1,0:T(8,128)(2,1)S(1)}) custom-call(s32[8,5]{1,0:T(8,128)} %index_in.1, s32[8,5]{1,0:T(8,128)} %mask_in.1, bf16[3,8,5,64,64]{4,3,2,1,0:T(8,128)(2,1)} %quad_in.1), custom_call_target="tpu_custom_call" | custom-call | tf_op jit(solution)/shard_map/band/pallas_call | solution.py:125
  8.7 0.9 %shard_map.77 = (bf16[2,2,768,256]{3,2,1,0:T(8,128)(2,1)S(1)}, f32[2,512,256]{2,1,0:T(8,128)S(1)}) custom-call(bf16[1,2,512,256]{3,2,1,0:T(8,128)(2,1)S(1)} %copy-done.1, bf16[2,768,512]{2,1,0:T(8,128)(2,1)S(1)} %get-tuple-element.41.band_ref, bf16[1,3,256,256]{3,2,1,0:T(8,128)(2,1)S(1)} %copy-done), custom_call_target="tpu_custom_call" | custom-call | flops 1073741824 | bytes 4194304 | tf_op jit(solution)/shard_map/pallas_call | solution.py:186
  9.6 0.0 collective-permute-done.1.refs_0_
  9.6 0.0 copy-start.2
  9.7 0.7 shard_map.78
  10.4 0.3 copy-done.2
  10.7 0.5 collective-permute-done.refs_0_
  11.2 0.7 shard_map.79
  12.0 0.1 collective-permute-start.2
  12.1 0.5 collective-permute-start.3
  12.6 0.1 collective-permute-start.4
  12.6 1.5 %collective-permute-done.3.refs_4_ = bf16[2,128,256]{2,1,0:T(8,128)(2,1)S(1)} collective-permute-done((bf16[2,128,256]{2,1,0:T(8,128)(2,1)S(1)}, bf16[2,128,256]{2,1,0:T(8,128)(2,1)S(1)}, u32[]{:S(2)}, u32[]{:S(2)}) %collective-permute-start.3) | collective-permute-done | bytes 131104 | tf_op jit(solution)/shard_map/ppermute | solution.py:565
  14.2 0.2 collective-permute-done.4.refs_5_
  14.4 0.0 collective-permute-done.2.refs_3_
  14.4 7.2 %collective-permute-start.5 = (bf16[512,256]{1,0:T(8,128)(2,1)S(1)}, bf16[512,256]{1,0:T(8,128)(2,1)S(1)}, u32[]{:S(2)}, u32[]{:S(2)}) collective-permute-start(bf16[512,256]{1,0:T(8,128)(2,1)S(1)} %get-tuple-element.54), channel_id=1, source_target_pairs={{0,3},{1,0},{2,1},{3,2},{4,7},{5,4},{6,5},{7,6},{8,11},{9,8},{10,9... | collective-permute-start | bytes 786440 | tf_op jit(solution)/shard_map/ppermute | solution.py:565
  21.6 0.7 collective-permute-start.6
  22.3 0.7 collective-permute-start.7
  23.0 0.7 collective-permute-start.8
  23.6 0.0 collective-permute-done.8.refs_6_
  23.7 1.8 %collective-permute-done.5.refs_3_ = bf16[512,256]{1,0:T(8,128)(2,1)S(1)} collective-permute-done((bf16[512,256]{1,0:T(8,128)(2,1)S(1)}, bf16[512,256]{1,0:T(8,128)(2,1)S(1)}, u32[]{:S(2)}, u32[]{:S(2)}) %collective-permute-start.5) | collective-permute-done | bytes 262176 | tf_op jit(solution)/shard_map/ppermute | solution.py:565
  25.5 2.8 %collective-permute-done.6.refs_4_ = bf16[512,256]{1,0:T(8,128)(2,1)S(1)} collective-permute-done((bf16[512,256]{1,0:T(8,128)(2,1)S(1)}, bf16[512,256]{1,0:T(8,128)(2,1)S(1)}, u32[]{:S(2)}, u32[]{:S(2)}) %collective-permute-start.6) | collective-permute-done | bytes 262176 | tf_op jit(solution)/shard_map/ppermute | solution.py:565
  28.3 6.0 %collective-permute-start.9 = (bf16[2,512,256]{2,1,0:T(8,128)(2,1)S(1)}, bf16[2,512,256]{2,1,0:T(8,128)(2,1)S(1)}, u32[]{:S(2)}, u32[]{:S(2)}) collective-permute-start(bf16[2,512,256]{2,1,0:T(8,128)(2,1)S(1)} %shard_map.86.refs_6_), channel_id=1, source_target_pairs={{0,1},{1,0},{2,3},{3,2},{4,5},{5,4},{6,7},{7,6},{8,9},{9,8},{10,11... | collective-permute-start | bytes 1572872 | tf_op jit(solution)/shard_map/ppermute | solution.py:565
  34.3 0.1 collective-permute-start.10
  34.3 4.3 %collective-permute-start.11 = (bf16[2,128,256]{2,1,0:T(8,128)(2,1)S(1)}, bf16[2,128,256]{2,1,0:T(8,128)(2,1)S(1)}, u32[]{:S(2)}, u32[]{:S(2)}) collective-permute-start(bf16[2,128,256]{2,1,0:T(8,128)(2,1)S(1)} %get-tuple-element.65.refs_7_), channel_id=1, source_target_pairs={{0,1},{2,3},{3,2},{1,0},{4,5},{6,7},{7,6},{5,8},{8,9},{10,11},{11,... | collective-permute-start | bytes 393224 | tf_op jit(solution)/shard_map/ppermute | solution.py:565
  38.6 2.2 %collective-permute-done.10.refs_4_ = bf16[2,128,256]{2,1,0:T(8,128)(2,1)S(1)} collective-permute-done((bf16[2,128,256]{2,1,0:T(8,128)(2,1)S(1)}, bf16[2,128,256]{2,1,0:T(8,128)(2,1)S(1)}, u32[]{:S(2)}, u32[]{:S(2)}) %collective-permute-start.10) | collective-permute-done | bytes 131104 | tf_op jit(solution)/shard_map/ppermute | solution.py:565
  40.8 0.0 collective-permute-done.11.refs_5_
  40.8 0.0 collective-permute-done.9.refs_3_
  40.8 0.2 shard_map.87
  41.0 0.7 shard_map.89
  41.7 0.3 collective-permute-start.12
  42.0 1.1 %collective-permute-done.12.got_ref = bf16[2,128,256]{2,1,0:T(8,128)(2,1)S(1)} collective-permute-done((bf16[2,128,256]{2,1,0:T(8,128)(2,1)S(1)}, bf16[2,128,256]{2,1,0:T(8,128)(2,1)S(1)}, u32[]{:S(2)}, u32[]{:S(2)}) %collective-permute-start.12) | collective-permute-done | bytes 131104 | tf_op jit(solution)/shard_map/ppermute | solution.py:505
  43.2 3.5 %collective-permute-start.13 = (bf16[256,256]{1,0:T(8,128)(2,1)S(1)}, bf16[256,256]{1,0:T(8,128)(2,1)S(1)}, u32[]{:S(2)}, u32[]{:S(2)}) collective-permute-start(bf16[256,256]{1,0:T(8,128)(2,1)S(1)} %shard_map.90), channel_id=1, source_target_pairs={{0,4},{1,3},{2,6},{3,1},{4,0},{5,9},{6,2},{7,11},{8,12},{9,5},{10,... | collective-permute-start | bytes 393224 | tf_op jit(solution)/shard_map/ppermute | solution.py:509
  46.7 3.9 %collective-permute-done.13.refs_0_.near_ref = bf16[256,256]{1,0:T(8,128)(2,1)S(1)} collective-permute-done((bf16[256,256]{1,0:T(8,128)(2,1)S(1)}, bf16[256,256]{1,0:T(8,128)(2,1)S(1)}, u32[]{:S(2)}, u32[]{:S(2)}) %collective-permute-start.13) | collective-permute-done | bytes 131104 | tf_op jit(solution)/shard_map/ppermute | solution.py:509
  50.6 0.1 collective-permute-start.14
  50.7 0.7 shard_map.92
  51.4 2.5 %collective-permute-start.18 = (bf16[192,256]{1,0:T(8,128)(2,1)S(1)}, bf16[192,256]{1,0:T(8,128)(2,1)S(1)}, u32[]{:S(2)}, u32[]{:S(2)}) collective-permute-start(bf16[192,256]{1,0:T(8,128)(2,1)S(1)} %get-tuple-element.77), channel_id=1, source_target_pairs={{0,4},{4,0},{8,12},{12,8},{16,20},{20,16},{24,28},{28,24},{1,5},{5... | collective-permute-start | bytes 294920 | tf_op jit(solution)/shard_map/ppermute | solution.py:500
  53.9 0.1 collective-permute-start.15
  54.0 2.0 %collective-permute-start.16 = (bf16[96,256]{1,0:T(8,128)(2,1)S(1)}, bf16[96,256]{1,0:T(8,128)(2,1)S(1)}, u32[]{:S(2)}, u32[]{:S(2)}) collective-permute-start(bf16[96,256]{1,0:T(8,128)(2,1)S(1)} %get-tuple-element.74), channel_id=1, source_target_pairs={{0,8},{4,12},{8,0},{12,4},{16,24},{20,28},{24,16},{28,20},{1,9},{5... | collective-permute-start | bytes 147464 | tf_op jit(solution)/shard_map/ppermute | solution.py:500
  56.0 1.4 %collective-permute-start.17 = (bf16[96,256]{1,0:T(8,128)(2,1)S(1)}, bf16[96,256]{1,0:T(8,128)(2,1)S(1)}, u32[]{:S(2)}, u32[]{:S(2)}) collective-permute-start(bf16[96,256]{1,0:T(8,128)(2,1)S(1)} %get-tuple-element.75), channel_id=1, source_target_pairs={{0,12},{4,8},{8,4},{12,0},{16,28},{20,24},{24,20},{28,16},{1,13},{... | collective-permute-start | bytes 147464 | tf_op jit(solution)/shard_map/ppermute | solution.py:500
  57.4 0.2 collective-permute-done.18.pair_ref
  57.6 3.2 %collective-permute-start.19 = (bf16[96,256]{1,0:T(8,128)(2,1)S(1)}, bf16[96,256]{1,0:T(8,128)(2,1)S(1)}, u32[]{:S(2)}, u32[]{:S(2)}) collective-permute-start(bf16[96,256]{1,0:T(8,128)(2,1)S(1)} %get-tuple-element.78), channel_id=1, source_target_pairs={{0,16},{4,20},{8,24},{12,28},{16,0},{20,4},{24,8},{28,12},{1,17},{... | collective-permute-start | bytes 147464 | tf_op jit(solution)/shard_map/ppermute | solution.py:500
  60.8 0.0 collective-permute-done.15.refs_0_
  60.8 2.0 %collective-permute-start.20 = (bf16[96,256]{1,0:T(8,128)(2,1)S(1)}, bf16[96,256]{1,0:T(8,128)(2,1)S(1)}, u32[]{:S(2)}, u32[]{:S(2)}) collective-permute-start(bf16[96,256]{1,0:T(8,128)(2,1)S(1)} %get-tuple-element.79), channel_id=1, source_target_pairs={{0,24},{4,28},{8,16},{12,20},{16,8},{20,12},{24,0},{28,4},{1,25},{... | collective-permute-start | bytes 147464 | tf_op jit(solution)/shard_map/ppermute | solution.py:500
  62.8 0.0 collective-permute-done.16.refs_1_
  62.8 0.0 collective-permute-done.17.refs_2_
  62.8 0.1 collective-permute-done.19.refs_3_
  62.9 3.8 %collective-permute-done.20.refs_4_ = bf16[96,256]{1,0:T(8,128)(2,1)S(1)} collective-permute-done((bf16[96,256]{1,0:T(8,128)(2,1)S(1)}, bf16[96,256]{1,0:T(8,128)(2,1)S(1)}, u32[]{:S(2)}, u32[]{:S(2)}) %collective-permute-start.20) | collective-permute-done | bytes 49184 | tf_op jit(solution)/shard_map/ppermute | solution.py:500
  66.7 2.2 %collective-permute-start.22 = (bf16[96,256]{1,0:T(8,128)(2,1)S(1)}, bf16[96,256]{1,0:T(8,128)(2,1)S(1)}, u32[]{:S(2)}, u32[]{:S(2)}) collective-permute-start(bf16[96,256]{1,0:T(8,128)(2,1)S(1)} %shard_map.94.refs_0_), channel_id=1, source_target_pairs={{0,24},{4,28},{8,16},{12,20},{16,8},{20,12},{24,0},{28,4},{1,25},{... | collective-permute-start | bytes 147464 | tf_op jit(solution)/shard_map/ppermute | solution.py:500
  68.9 0.0 collective-permute-start.21
  68.9 3.8 %collective-permute-done.22.refs_2_.refs_4_ = bf16[96,256]{1,0:T(8,128)(2,1)S(1)} collective-permute-done((bf16[96,256]{1,0:T(8,128)(2,1)S(1)}, bf16[96,256]{1,0:T(8,128)(2,1)S(1)}, u32[]{:S(2)}, u32[]{:S(2)}) %collective-permute-start.22) | collective-permute-done | bytes 49184 | tf_op jit(solution)/shard_map/ppermute | solution.py:500
  72.7 1.2 %collective-permute-done.21.refs_1_.refs_3_ = bf16[96,256]{1,0:T(8,128)(2,1)S(1)} collective-permute-done((bf16[96,256]{1,0:T(8,128)(2,1)S(1)}, bf16[96,256]{1,0:T(8,128)(2,1)S(1)}, u32[]{:S(2)}, u32[]{:S(2)}) %collective-permute-start.21) | collective-permute-done | bytes 49184 | tf_op jit(solution)/shard_map/ppermute | solution.py:500
  73.9 1.4 %collective-permute-start.23 = (bf16[288,256]{1,0:T(8,128)(2,1)S(1)}, bf16[288,256]{1,0:T(8,128)(2,1)S(1)}, u32[]{:S(2)}, u32[]{:S(2)}) collective-permute-start(bf16[288,256]{1,0:T(8,128)(2,1)S(1)} %shard_map.95), channel_id=1, source_target_pairs={{0,4},{4,0},{8,12},{12,8},{16,20},{20,16},{24,28},{28,24},{1,5},{5... | collective-permute-start | bytes 442376 | tf_op jit(solution)/shard_map/ppermute | solution.py:500
  75.3 0.0 collective-permute-start.25
  75.3 2.1 %collective-permute-start.24 = (bf16[96,256]{1,0:T(8,128)(2,1)S(1)}, bf16[96,256]{1,0:T(8,128)(2,1)S(1)}, u32[]{:S(2)}, u32[]{:S(2)}) collective-permute-start(bf16[96,256]{1,0:T(8,128)(2,1)S(1)} %shard_map.94.refs_0_), channel_id=1, source_target_pairs={{0,8},{4,12},{8,0},{12,4},{16,24},{20,28},{24,16},{28,20},{1,9},{5... | collective-permute-start | bytes 147464 | tf_op jit(solution)/shard_map/ppermute | solution.py:500
  77.4 1.9 %shard_map.88.main_ref = bf16[2,512,256]{2,1,0:T(8,128)(2,1)S(1)} custom-call(bf16[2,512,256]{2,1,0:T(8,128)(2,1)S(1)} %get-tuple-element.67.refs_0_.slope_ref, bf16[2,512,768]{2,1,0:T(8,128)(2,1)S(1)} %get-tuple-element.49.refs_1_, bf16[1,3,256,256]{3,2,1,0:T(8,128)(2,1)S(1)} %copy-done, ...), custom_call_target="tpu_custom_call", output_to_operand_aliasing={{}: (6, {})} | custom-call | tf_op jit(solution)/shard_map/pallas_call | solution.py:355
  79.4 0.9 %collective-permute-done.25.refs_2_ = bf16[96,256]{1,0:T(8,128)(2,1)S(1)} collective-permute-done((bf16[96,256]{1,0:T(8,128)(2,1)S(1)}, bf16[96,256]{1,0:T(8,128)(2,1)S(1)}, u32[]{:S(2)}, u32[]{:S(2)}) %collective-permute-start.25) | collective-permute-done | bytes 49184 | tf_op jit(solution)/shard_map/ppermute | solution.py:500
  80.3 0.8 shard_map.96.refs_1_
  81.2 0.0 collective-permute-done.23.refs_0_
  81.2 0.7 shard_map.97
  81.9 0.0 collective-permute-done.14.far_ref
  81.9 0.9 %grad.1 = bf16[1,2,512,256]{3,2,1,0:T(8,128)(2,1)} custom-call(bf16[2,512,256]{2,1,0:T(8,128)(2,1)S(1)} %shard_map.88.main_ref, bf16[256,256]{1,0:T(8,128)(2,1)S(1)} %collective-permute-done.13.refs_0_.near_ref, bf16[768,256]{1,0:T(8,128)(2,1)S(1)} %collective-permute-done.14.far_ref), custom_call_target="tpu_custom_call" | custom-call | tf_op jit(solution)/shard_map/grad/pallas_call | solution.py:548
  (18 shorter events, 0.2 us)
Async XLA Ops:
  0.6 8.1 %copy-start.1 = (bf16[1,2,512,256]{3,2,1,0:T(8,128)(2,1)S(1)}, bf16[1,2,512,256]{3,2,1,0:T(8,128)(2,1)}, u32[]{:S(2)}) copy-start(bf16[1,2,512,256]{3,2,1,0:T(8,128)(2,1)} %x_ref.7) | copy-start | bytes 1572868
  0.6 8.1 %copy-start = (bf16[1,3,256,256]{3,2,1,0:T(8,128)(2,1)S(1)}, bf16[1,3,256,256]{3,2,1,0:T(8,128)(2,1)}, u32[]{:S(2)}) copy-start(bf16[1,3,256,256]{3,2,1,0:T(8,128)(2,1)} %refs_2_.19) | copy-start | bytes 1179652
  1.7 7.9 %collective-permute-start.1 = (bf16[2,128,256]{2,1,0:T(8,128)(2,1)S(1)}, bf16[2,128,256]{2,1,0:T(8,128)(2,1)S(1)}, u32[]{:S(2)}, u32[]{:S(2)}) collective-permute-start(bf16[2,128,256]{2,1,0:T(8,128)(2,1)S(1)} %get-tuple-element.43), channel_id=1, source_target_pairs={{0,1},{1,0},{2,3},{3,2},{4,8},{5,9},{6,10},{7,11},{8,4},{9,5},{10,... | collective-permute-start | bytes 393224 | tf_op jit(solution)/shard_map/ppermute | solution.py:568
  2.3 8.9 %collective-permute-start = (bf16[2,128,256]{2,1,0:T(8,128)(2,1)S(1)}, bf16[2,128,256]{2,1,0:T(8,128)(2,1)S(1)}, u32[]{:S(2)}, u32[]{:S(2)}) collective-permute-start(bf16[2,128,256]{2,1,0:T(8,128)(2,1)S(1)} %get-tuple-element.42), channel_id=1, source_target_pairs={{0,4},{1,5},{2,6},{3,7},{4,0},{5,1},{6,2},{7,3},{8,12},{9,13},{10,... | collective-permute-start | bytes 393224 | tf_op jit(solution)/shard_map/ppermute | solution.py:569
  9.6 1.0 %copy-start.2 = (bf16[2,512,256]{2,1,0:T(8,128)(2,1)S(1)}, bf16[2,512,256]{2,1,0:T(8,128)(2,1)}, u32[]{:S(2)}) copy-start(bf16[2,512,256]{2,1,0:T(8,128)(2,1)} %refs_3_.5) | copy-start | bytes 1572868
  12.0 2.4 %collective-permute-start.2 = (bf16[2,512,256]{2,1,0:T(8,128)(2,1)S(1)}, bf16[2,512,256]{2,1,0:T(8,128)(2,1)S(1)}, u32[]{:S(2)}, u32[]{:S(2)}) collective-permute-start(bf16[2,512,256]{2,1,0:T(8,128)(2,1)S(1)} %shard_map.82.refs_7_), channel_id=1, source_target_pairs={{0,1},{1,0},{2,3},{3,2},{4,5},{5,4},{6,7},{7,6},{8,9},{9,8},{10,11... | collective-permute-start | bytes 1572872 | tf_op jit(solution)/shard_map/ppermute | solution.py:565
  12.1 2.1 %collective-permute-start.3 = (bf16[2,128,256]{2,1,0:T(8,128)(2,1)S(1)}, bf16[2,128,256]{2,1,0:T(8,128)(2,1)S(1)}, u32[]{:S(2)}, u32[]{:S(2)}) collective-permute-start(bf16[2,128,256]{2,1,0:T(8,128)(2,1)S(1)} %get-tuple-element.52.refs_6_), channel_id=1, source_target_pairs={{0,1},{1,0},{2,3},{3,6},{4,5},{5,4},{6,7},{7,2},{8,9},{9,8},{10,11... | collective-permute-start | bytes 393224 | tf_op jit(solution)/shard_map/ppermute | solution.py:565
  12.6 1.8 %collective-permute-start.4 = (bf16[2,128,256]{2,1,0:T(8,128)(2,1)S(1)}, bf16[2,128,256]{2,1,0:T(8,128)(2,1)S(1)}, u32[]{:S(2)}, u32[]{:S(2)}) collective-permute-start(bf16[2,128,256]{2,1,0:T(8,128)(2,1)S(1)} %get-tuple-element.53.refs_7_), channel_id=1, source_target_pairs={{0,1},{1,0},{2,3},{3,2},{4,5},{5,4},{6,7},{7,10},{8,9},{9,8},{10,1... | collective-permute-start | bytes 393224 | tf_op jit(solution)/shard_map/ppermute | solution.py:565
  14.4 11.1 %collective-permute-start.5 = (bf16[512,256]{1,0:T(8,128)(2,1)S(1)}, bf16[512,256]{1,0:T(8,128)(2,1)S(1)}, u32[]{:S(2)}, u32[]{:S(2)}) collective-permute-start(bf16[512,256]{1,0:T(8,128)(2,1)S(1)} %get-tuple-element.54), channel_id=1, source_target_pairs={{0,3},{1,0},{2,1},{3,2},{4,7},{5,4},{6,5},{7,6},{8,11},{9,8},{10,9... | collective-permute-start | bytes 786440 | tf_op jit(solution)/shard_map/ppermute | solution.py:565
  21.6 6.7 %collective-permute-start.6 = (bf16[512,256]{1,0:T(8,128)(2,1)S(1)}, bf16[512,256]{1,0:T(8,128)(2,1)S(1)}, u32[]{:S(2)}, u32[]{:S(2)}) collective-permute-start(bf16[512,256]{1,0:T(8,128)(2,1)S(1)} %get-tuple-element.58), channel_id=1, source_target_pairs={{0,3},{1,0},{2,1},{3,2},{4,7},{5,4},{6,5},{7,6},{8,11},{9,8},{10,9... | collective-permute-start | bytes 786440 | tf_op jit(solution)/shard_map/ppermute | solution.py:565
  22.3 1.3 %collective-permute-start.7 = (bf16[2,128,256]{2,1,0:T(8,128)(2,1)S(1)}, bf16[2,128,256]{2,1,0:T(8,128)(2,1)S(1)}, u32[]{:S(2)}, u32[]{:S(2)}) collective-permute-start(bf16[2,128,256]{2,1,0:T(8,128)(2,1)S(1)} %get-tuple-element.59.refs_7_), channel_id=1, source_target_pairs={{2,5},{6,1},{10,13},{14,9},{18,21},{22,17},{26,29},{30,25}} | collective-permute-start | bytes 393224 | tf_op jit(solution)/shard_map/ppermute | solution.py:565
  23.0 0.7 collective-permute-start.8
  28.3 12.5 %collective-permute-start.9 = (bf16[2,512,256]{2,1,0:T(8,128)(2,1)S(1)}, bf16[2,512,256]{2,1,0:T(8,128)(2,1)S(1)}, u32[]{:S(2)}, u32[]{:S(2)}) collective-permute-start(bf16[2,512,256]{2,1,0:T(8,128)(2,1)S(1)} %shard_map.86.refs_6_), channel_id=1, source_target_pairs={{0,1},{1,0},{2,3},{3,2},{4,5},{5,4},{6,7},{7,6},{8,9},{9,8},{10,11... | collective-permute-start | bytes 1572872 | tf_op jit(solution)/shard_map/ppermute | solution.py:565
  34.3 6.6 %collective-permute-start.10 = (bf16[2,128,256]{2,1,0:T(8,128)(2,1)S(1)}, bf16[2,128,256]{2,1,0:T(8,128)(2,1)S(1)}, u32[]{:S(2)}, u32[]{:S(2)}) collective-permute-start(bf16[2,128,256]{2,1,0:T(8,128)(2,1)S(1)} %get-tuple-element.64.refs_6_), channel_id=1, source_target_pairs={{0,1},{2,3},{3,2},{1,4},{4,5},{6,7},{7,6},{5,0},{8,9},{10,11},{11,... | collective-permute-start | bytes 393224 | tf_op jit(solution)/shard_map/ppermute | solution.py:565
  34.3 6.5 %collective-permute-start.11 = (bf16[2,128,256]{2,1,0:T(8,128)(2,1)S(1)}, bf16[2,128,256]{2,1,0:T(8,128)(2,1)S(1)}, u32[]{:S(2)}, u32[]{:S(2)}) collective-permute-start(bf16[2,128,256]{2,1,0:T(8,128)(2,1)S(1)} %get-tuple-element.65.refs_7_), channel_id=1, source_target_pairs={{0,1},{2,3},{3,2},{1,0},{4,5},{6,7},{7,6},{5,8},{8,9},{10,11},{11,... | collective-permute-start | bytes 393224 | tf_op jit(solution)/shard_map/ppermute | solution.py:565
  41.7 1.4 %collective-permute-start.12 = (bf16[2,128,256]{2,1,0:T(8,128)(2,1)S(1)}, bf16[2,128,256]{2,1,0:T(8,128)(2,1)S(1)}, u32[]{:S(2)}, u32[]{:S(2)}) collective-permute-start(bf16[2,128,256]{2,1,0:T(8,128)(2,1)S(1)} %get-tuple-element.68), channel_id=1, source_target_pairs={{0,1},{1,0},{2,3},{3,2},{4,5},{5,4},{6,7},{7,6},{8,9},{9,8},{10,11... | collective-permute-start | bytes 393224 | tf_op jit(solution)/shard_map/ppermute | solution.py:505
  43.2 7.4 %collective-permute-start.13 = (bf16[256,256]{1,0:T(8,128)(2,1)S(1)}, bf16[256,256]{1,0:T(8,128)(2,1)S(1)}, u32[]{:S(2)}, u32[]{:S(2)}) collective-permute-start(bf16[256,256]{1,0:T(8,128)(2,1)S(1)} %shard_map.90), channel_id=1, source_target_pairs={{0,4},{1,3},{2,6},{3,1},{4,0},{5,9},{6,2},{7,11},{8,12},{9,5},{10,... | collective-permute-start | bytes 393224 | tf_op jit(solution)/shard_map/ppermute | solution.py:509
  50.6 31.3 %collective-permute-start.14 = (bf16[768,256]{1,0:T(8,128)(2,1)S(1)}, bf16[768,256]{1,0:T(8,128)(2,1)S(1)}, u32[]{:S(2)}, u32[]{:S(2)}) collective-permute-start(bf16[768,256]{1,0:T(8,128)(2,1)S(1)} %shard_map.91), channel_id=1, source_target_pairs={{0,1},{1,0},{2,3},{3,2},{4,5},{5,4},{6,7},{7,6},{8,9},{9,8},{10,11... | collective-permute-start | bytes 1179656 | tf_op jit(solution)/shard_map/ppermute | solution.py:516
  51.4 6.2 %collective-permute-start.18 = (bf16[192,256]{1,0:T(8,128)(2,1)S(1)}, bf16[192,256]{1,0:T(8,128)(2,1)S(1)}, u32[]{:S(2)}, u32[]{:S(2)}) collective-permute-start(bf16[192,256]{1,0:T(8,128)(2,1)S(1)} %get-tuple-element.77), channel_id=1, source_target_pairs={{0,4},{4,0},{8,12},{12,8},{16,20},{20,16},{24,28},{28,24},{1,5},{5... | collective-permute-start | bytes 294920 | tf_op jit(solution)/shard_map/ppermute | solution.py:500
  53.9 6.9 %collective-permute-start.15 = (bf16[96,256]{1,0:T(8,128)(2,1)S(1)}, bf16[96,256]{1,0:T(8,128)(2,1)S(1)}, u32[]{:S(2)}, u32[]{:S(2)}) collective-permute-start(bf16[96,256]{1,0:T(8,128)(2,1)S(1)} %get-tuple-element.73), channel_id=1, source_target_pairs={{0,4},{4,0},{8,12},{12,8},{16,20},{20,16},{24,28},{28,24},{1,5},{5... | collective-permute-start | bytes 147464 | tf_op jit(solution)/shard_map/ppermute | solution.py:500
  54.0 8.8 %collective-permute-start.16 = (bf16[96,256]{1,0:T(8,128)(2,1)S(1)}, bf16[96,256]{1,0:T(8,128)(2,1)S(1)}, u32[]{:S(2)}, u32[]{:S(2)}) collective-permute-start(bf16[96,256]{1,0:T(8,128)(2,1)S(1)} %get-tuple-element.74), channel_id=1, source_target_pairs={{0,8},{4,12},{8,0},{12,4},{16,24},{20,28},{24,16},{28,20},{1,9},{5... | collective-permute-start | bytes 147464 | tf_op jit(solution)/shard_map/ppermute | solution.py:500
  56.0 6.8 %collective-permute-start.17 = (bf16[96,256]{1,0:T(8,128)(2,1)S(1)}, bf16[96,256]{1,0:T(8,128)(2,1)S(1)}, u32[]{:S(2)}, u32[]{:S(2)}) collective-permute-start(bf16[96,256]{1,0:T(8,128)(2,1)S(1)} %get-tuple-element.75), channel_id=1, source_target_pairs={{0,12},{4,8},{8,4},{12,0},{16,28},{20,24},{24,20},{28,16},{1,13},{... | collective-permute-start | bytes 147464 | tf_op jit(solution)/shard_map/ppermute | solution.py:500
  57.6 5.3 %collective-permute-start.19 = (bf16[96,256]{1,0:T(8,128)(2,1)S(1)}, bf16[96,256]{1,0:T(8,128)(2,1)S(1)}, u32[]{:S(2)}, u32[]{:S(2)}) collective-permute-start(bf16[96,256]{1,0:T(8,128)(2,1)S(1)} %get-tuple-element.78), channel_id=1, source_target_pairs={{0,16},{4,20},{8,24},{12,28},{16,0},{20,4},{24,8},{28,12},{1,17},{... | collective-permute-start | bytes 147464 | tf_op jit(solution)/shard_map/ppermute | solution.py:500
  60.8 5.9 %collective-permute-start.20 = (bf16[96,256]{1,0:T(8,128)(2,1)S(1)}, bf16[96,256]{1,0:T(8,128)(2,1)S(1)}, u32[]{:S(2)}, u32[]{:S(2)}) collective-permute-start(bf16[96,256]{1,0:T(8,128)(2,1)S(1)} %get-tuple-element.79), channel_id=1, source_target_pairs={{0,24},{4,28},{8,16},{12,20},{16,8},{20,12},{24,0},{28,4},{1,25},{... | collective-permute-start | bytes 147464 | tf_op jit(solution)/shard_map/ppermute | solution.py:500
  66.7 6.0 %collective-permute-start.22 = (bf16[96,256]{1,0:T(8,128)(2,1)S(1)}, bf16[96,256]{1,0:T(8,128)(2,1)S(1)}, u32[]{:S(2)}, u32[]{:S(2)}) collective-permute-start(bf16[96,256]{1,0:T(8,128)(2,1)S(1)} %shard_map.94.refs_0_), channel_id=1, source_target_pairs={{0,24},{4,28},{8,16},{12,20},{16,8},{20,12},{24,0},{28,4},{1,25},{... | collective-permute-start | bytes 147464 | tf_op jit(solution)/shard_map/ppermute | solution.py:500
  68.9 5.0 %collective-permute-start.21 = (bf16[96,256]{1,0:T(8,128)(2,1)S(1)}, bf16[96,256]{1,0:T(8,128)(2,1)S(1)}, u32[]{:S(2)}, u32[]{:S(2)}) collective-permute-start(bf16[96,256]{1,0:T(8,128)(2,1)S(1)} %shard_map.94.refs_0_), channel_id=1, source_target_pairs={{0,16},{4,20},{8,24},{12,28},{16,0},{20,4},{24,8},{28,12},{1,17},{... | collective-permute-start | bytes 147464 | tf_op jit(solution)/shard_map/ppermute | solution.py:500
  73.9 7.3 %collective-permute-start.23 = (bf16[288,256]{1,0:T(8,128)(2,1)S(1)}, bf16[288,256]{1,0:T(8,128)(2,1)S(1)}, u32[]{:S(2)}, u32[]{:S(2)}) collective-permute-start(bf16[288,256]{1,0:T(8,128)(2,1)S(1)} %shard_map.95), channel_id=1, source_target_pairs={{0,4},{4,0},{8,12},{12,8},{16,20},{20,16},{24,28},{28,24},{1,5},{5... | collective-permute-start | bytes 442376 | tf_op jit(solution)/shard_map/ppermute | solution.py:500
  75.3 5.0 %collective-permute-start.25 = (bf16[96,256]{1,0:T(8,128)(2,1)S(1)}, bf16[96,256]{1,0:T(8,128)(2,1)S(1)}, u32[]{:S(2)}, u32[]{:S(2)}) collective-permute-start(bf16[96,256]{1,0:T(8,128)(2,1)S(1)} %shard_map.94.refs_0_), channel_id=1, source_target_pairs={{0,12},{4,8},{8,4},{12,0},{16,28},{20,24},{24,20},{28,16},{1,13},{... | collective-permute-start | bytes 147464 | tf_op jit(solution)/shard_map/ppermute | solution.py:500
  75.3 5.0 %collective-permute-start.24 = (bf16[96,256]{1,0:T(8,128)(2,1)S(1)}, bf16[96,256]{1,0:T(8,128)(2,1)S(1)}, u32[]{:S(2)}, u32[]{:S(2)}) collective-permute-start(bf16[96,256]{1,0:T(8,128)(2,1)S(1)} %shard_map.94.refs_0_), channel_id=1, source_target_pairs={{0,8},{4,12},{8,0},{12,4},{16,24},{20,28},{24,16},{28,20},{1,9},{5... | collective-permute-start | bytes 147464 | tf_op jit(solution)/shard_map/ppermute | solution.py:500

commit v3 on v2

--- a/solution.py
+++ b/solution.py
@@ -246,14 +246,13 @@
 
 
 def step_kernel(turn, lats, part, form, *refs):
-    outs, (stack_ref, term_ref) = dict(zip(PARTS[part], refs[-2 - len(PARTS[part]) :])), refs[-2:]
+    outs, stack_ref = dict(zip(PARTS[part], refs[-1 - len(PARTS[part]) :])), refs[-1]
     (gp_ref, flip_ref, w_ref), rest = refs[:3], refs[3:]
     lat = lax.axis_index("lat")
     odd = lat % 2 == 1
     rows = gp_ref.shape[1]
     size = GRP * BLK
     edge = HALO * BLK
-    lap = 2 * edge
     groups = rows // size
 
     micros = MICROS.get(part, range(MB))
@@ -274,16 +273,22 @@
             parts[-1] += jnp.where(lat < lats - 1, above, 0.0)
         return jnp.concatenate(parts, axis=0).astype(BF).astype(F32)
 
-    def tips(names):
+    def tips(sides):
         deep = KB * edge
-        sides = [(name, above) for name, above in zip(names, (False, True)) if name]
-        rims = [slope_ref[m, (rows - edge) * up : (rows - edge) * up + edge, :] for m in range(MB) for _, up in sides]
+        rims = [slope_ref[m, (rows - edge) * up : (rows - edge) * up + edge, :] for m in range(MB) for up in sides]
         back_terms(jnp.concatenate(rims, axis=0), w_ref, stack_ref)
+        found = []
+        for i, up in enumerate(list(sides) * MB):
+            band = flip_ref[groups - 1, size + edge :, deep:] if up else flip_ref[0, :edge, :deep]
+            found.append(dot(band, stack_ref[i * deep : (i + 1) * deep, :]).astype(BF))
+        return found
+
+    def both_tips():
+        found = tips((0, 1))
         for m in range(MB):
-            for i, (name, above) in enumerate(sides):
-                at = (m * len(sides) + i) * deep
-                band = flip_ref[groups - 1, size + edge :, deep:] if above else flip_ref[0, :edge, :deep]
-                outs[name][m] = dot(band, stack_ref[at : at + deep, :]).astype(BF)
+            below, above = found[2 * m : 2 * m + 2]
+            outs["near"][m] = jnp.where(odd, below, above)
+            outs["far"][m] = jnp.where(odd, above, below)
 
     def half(even_part):
         above = not even_part if part == "far" else even_part
@@ -293,7 +298,8 @@
             at = mine if part == "far" else others
             grad = rest[0][m, at, :].astype(F32)
             outs["slope"][m, at, :] = (grad * gp_ref[m, at, :]).astype(BF)
-        tips((None, part) if above else (part, None))
+        for m, found in enumerate(tips((int(above),))):
+            outs[part][m] = found
 
     def slopes():
         for m in micros:
@@ -307,23 +313,26 @@
                     outs["done"][m, edge:, :] = grad[size - edge :].astype(BF)
 
     def terms(m):
+        deep = KB * size
         for g in range(groups):
-            grad = grad_of(m, g)
-            back_terms(slope_ref[m, g * size : (g + 1) * size, :], w_ref, stack_ref)
-            term = dot(flip_ref[g], stack_ref[: KB * size, :])
-            low = g * size
-            if g == 0:
-                term_ref[low + edge : low + lap, :] = term[edge:lap] + grad[: lap - edge]
-            else:
-                term_ref[low : low + lap, :] += term[:lap]
-                term_ref[low + edge : low + lap, :] += grad[: lap - edge]
-            term_ref[low + lap : low + size + edge, :] = term[lap : size + edge] + grad[lap - edge :]
-            if g < groups - 1:
-                term_ref[low + size + edge : low + size + lap, :] = term[size + edge :]
-        out = term_ref[edge : edge + rows, :].astype(BF)
-        outs["out"][m] = out
-        if part in MICROS:
-            outs[f"sent{m}"][...] = out
+            stack = stack_ref.at[pl.ds(g * deep, deep)]
+            back_terms(slope_ref[m, g * size : (g + 1) * size, :], w_ref, stack)
+        sums = [None] * (rows // edge)
+        for g in range(groups):
+            first = max(2 * g - 1, 0)
+            last = min(2 * g + 3, len(sums))
+            low = (first - (2 * g - 1)) * edge
+            term = dot(flip_ref[g, low : low + (last - first) * edge, :], stack_ref[g * deep : (g + 1) * deep, :])
+            for i in range(first, last):
+                new = term[(i - first) * edge : (i - first + 1) * edge]
+                sums[i] = new if sums[i] is None else sums[i] + new
+        for i, value in enumerate(sums):
+            at = slice(i * edge, (i + 1) * edge)
+            grad = grad_of(m, i // 2)[(i % 2) * edge : (i % 2 + 1) * edge]
+            out = (value + grad).astype(BF)
+            outs["out"][m, at, :] = out
+            if part in MICROS:
+                outs[f"sent{m}"][at, :] = out
 
     @pl.when(lax.axis_index("section") == turn)
     def _():
@@ -337,8 +346,7 @@
             for m in micros:
                 terms(m)
         if "near" in outs:
-            pl.when(odd)(lambda: tips(("near", "far")))
-            pl.when(jnp.logical_not(odd))(lambda: tips(("far", "near")))
+            both_tips()
 
 
 def step_call(turn, lats, part, grads, flip, weights, state):
@@ -361,8 +369,7 @@
             len(args) - len(known) + i: names.index(name) for i, name in enumerate(known)
         },
         scratch_shapes=[
-            pltpu.VMEM((KB * max(GRP * BLK, 2 * MB * edge), ch), BF),
-            pltpu.VMEM((rows + 2 * edge, ch), F32),
+            pltpu.VMEM((KB * max(rows, 2 * MB * edge), ch), BF),
         ],
         compiler_params=params(),
     )(*args)

time: 83.1 us -> 81 us (0.975)
  starting transfers between devices: 45.7 us -> 42.9 us
  waiting for transfers between devices: 24 us -> 25.4 us
    ppermute x10, starting transfers between devices: 20.2 us -> 17.6 us  [send(): return lax.ppermute(array, axis, pairs)]
  transfers between devices with their start and end apart: 26 -> 26, of which waited for: 14 -> 14; matrix products, arithmetic and copies ran while one was open for 0% -> 0% of each run, Pallas kernels for 10% -> 9%
where the time goes in v3:
time: 81 us; the launch traced here: 80.8 us
  starting transfers between devices  42.9 us (53%)
  waiting for transfers between devices  25.4 us (31%)
  Pallas kernels  11.4 us (14%)
  between operations  0.88 us (1%)
    ppermute x10, starting transfers between devices, send(): return lax.ppermute(array, axis, pairs)  17.6 us
    ppermute x11, starting transfers between devices, meet(): return lax.ppermute(a, 'lat', [(i, i ^ bits) for i in range(lats)])  17 us
    ppermute x11, waiting for transfers between devices, meet(): return lax.ppermute(a, 'lat', [(i, i ^ bits) for i in range(lats)])  10.6 us
    ppermute x10, waiting for transfers between devices, send(): return lax.ppermute(array, axis, pairs)  9.01 us
    ppermute x1, starting transfers between devices, per_device(): near = lax.ppermute(near, both, sides[0])  4.02 us
    ppermute x1, waiting for transfers between devices, reduce_weight(): rims = lax.ppermute(rims, ('lat', 'section'), edge_pairs(lats, sections))  3.89 us
    ppermute x1, starting transfers between devices, reduce_weight(): rims = lax.ppermute(rims, ('lat', 'section'), edge_pairs(lats, sections))  3.54 us
    pallas_call x3, Pallas kernels, hidden_call(): pl.pallas_call(functools.partial(hidden_kernel, part), out_shape=(pltpu.V...  2.39 us
  transfers between devices with their start and end apart: 26, of which 14 were waited for; matrix products, arithmetic and copies ran while one was open for 0% of the time, Pallas kernels for 9%

profile of v3, /device:TPU:0, one launch (start us, length us, event | category | flops | bytes accessed | tf_op | source)
XLA Modules:
  0.0 80.8 jit_solution(1725553834366029333)
XLA Ops:
  0.6 1.1 %rim.1 = (bf16[2,128,256]{2,1,0:T(8,128)(2,1)S(1)}, bf16[2,128,256]{2,1,0:T(8,128)(2,1)S(1)}) custom-call(bf16[1,2,512,256]{3,2,1,0:T(8,128)(2,1)} %x_ref.7), custom_call_target="tpu_custom_call" | custom-call | tf_op jit(solution)/shard_map/rim/pallas_call | solution.py:214
  1.7 0.6 collective-permute-start.1
  2.3 4.0 %collective-permute-start = (bf16[2,128,256]{2,1,0:T(8,128)(2,1)S(1)}, bf16[2,128,256]{2,1,0:T(8,128)(2,1)S(1)}, u32[]{:S(2)}, u32[]{:S(2)}) collective-permute-start(bf16[2,128,256]{2,1,0:T(8,128)(2,1)S(1)} %get-tuple-element.42), channel_id=1, source_target_pairs={{0,4},{1,5},{2,6},{3,7},{4,0},{5,1},{6,2},{7,3},{8,12},{9,13},{10,... | collective-permute-start | bytes 393224 | tf_op jit(solution)/shard_map/ppermute | solution.py:576
  6.3 2.4 %band.1 = (bf16[2,768,512]{2,1,0:T(8,128)(2,1)S(1)}, bf16[2,512,768]{2,1,0:T(8,128)(2,1)S(1)}) custom-call(s32[8,5]{1,0:T(8,128)} %index_in.1, s32[8,5]{1,0:T(8,128)} %mask_in.1, bf16[3,8,5,64,64]{4,3,2,1,0:T(8,128)(2,1)} %quad_in.1), custom_call_target="tpu_custom_call" | custom-call | tf_op jit(solution)/shard_map/band/pallas_call | solution.py:125
  8.7 0.9 %shard_map.77 = (bf16[2,2,768,256]{3,2,1,0:T(8,128)(2,1)S(1)}, f32[2,512,256]{2,1,0:T(8,128)S(1)}) custom-call(bf16[1,2,512,256]{3,2,1,0:T(8,128)(2,1)S(1)} %copy-done.1, bf16[2,768,512]{2,1,0:T(8,128)(2,1)S(1)} %get-tuple-element.41.band_ref, bf16[1,3,256,256]{3,2,1,0:T(8,128)(2,1)S(1)} %copy-done), custom_call_target="tpu_custom_call" | custom-call | flops 1073741824 | bytes 4194304 | tf_op jit(solution)/shard_map/pallas_call | solution.py:186
  9.6 0.0 collective-permute-done.1.refs_0_
  9.6 0.0 copy-start.2
  9.7 0.7 shard_map.78
  10.4 0.3 copy-done.2
  10.7 0.5 collective-permute-done.refs_0_
  11.2 0.7 shard_map.79
  12.0 0.1 collective-permute-start.2
  12.1 0.5 collective-permute-start.3
  12.6 0.1 collective-permute-start.4
  12.6 1.5 %collective-permute-done.3.refs_4_ = bf16[2,128,256]{2,1,0:T(8,128)(2,1)S(1)} collective-permute-done((bf16[2,128,256]{2,1,0:T(8,128)(2,1)S(1)}, bf16[2,128,256]{2,1,0:T(8,128)(2,1)S(1)}, u32[]{:S(2)}, u32[]{:S(2)}) %collective-permute-start.3) | collective-permute-done | bytes 131104 | tf_op jit(solution)/shard_map/ppermute | solution.py:572
  14.2 0.2 collective-permute-done.4.refs_5_
  14.4 0.0 collective-permute-done.2.refs_3_
  14.4 6.5 %collective-permute-start.5 = (bf16[512,256]{1,0:T(8,128)(2,1)S(1)}, bf16[512,256]{1,0:T(8,128)(2,1)S(1)}, u32[]{:S(2)}, u32[]{:S(2)}) collective-permute-start(bf16[512,256]{1,0:T(8,128)(2,1)S(1)} %get-tuple-element.54), channel_id=1, source_target_pairs={{0,3},{1,0},{2,1},{3,2},{4,7},{5,4},{6,5},{7,6},{8,11},{9,8},{10,9... | collective-permute-start | bytes 786440 | tf_op jit(solution)/shard_map/ppermute | solution.py:572
  20.9 0.2 collective-permute-start.6
  21.1 0.7 collective-permute-start.7
  21.8 0.7 collective-permute-start.8
  22.5 0.0 collective-permute-done.7.refs_5_
  22.5 0.0 collective-permute-done.8.refs_6_
  22.5 2.3 %collective-permute-done.5.refs_3_ = bf16[512,256]{1,0:T(8,128)(2,1)S(1)} collective-permute-done((bf16[512,256]{1,0:T(8,128)(2,1)S(1)}, bf16[512,256]{1,0:T(8,128)(2,1)S(1)}, u32[]{:S(2)}, u32[]{:S(2)}) %collective-permute-start.5) | collective-permute-done | bytes 262176 | tf_op jit(solution)/shard_map/ppermute | solution.py:572
  24.8 2.8 %collective-permute-done.6.refs_4_ = bf16[512,256]{1,0:T(8,128)(2,1)S(1)} collective-permute-done((bf16[512,256]{1,0:T(8,128)(2,1)S(1)}, bf16[512,256]{1,0:T(8,128)(2,1)S(1)}, u32[]{:S(2)}, u32[]{:S(2)}) %collective-permute-start.6) | collective-permute-done | bytes 262176 | tf_op jit(solution)/shard_map/ppermute | solution.py:572
  27.6 3.8 %collective-permute-start.9 = (bf16[2,512,256]{2,1,0:T(8,128)(2,1)S(1)}, bf16[2,512,256]{2,1,0:T(8,128)(2,1)S(1)}, u32[]{:S(2)}, u32[]{:S(2)}) collective-permute-start(bf16[2,512,256]{2,1,0:T(8,128)(2,1)S(1)} %shard_map.86.refs_6_), channel_id=1, source_target_pairs={{0,1},{1,0},{2,3},{3,2},{4,5},{5,4},{6,7},{7,6},{8,9},{9,8},{10,11... | collective-permute-start | bytes 1572872 | tf_op jit(solution)/shard_map/ppermute | solution.py:572
  31.4 0.1 collective-permute-start.10
  31.5 4.9 %collective-permute-start.11 = (bf16[2,128,256]{2,1,0:T(8,128)(2,1)S(1)}, bf16[2,128,256]{2,1,0:T(8,128)(2,1)S(1)}, u32[]{:S(2)}, u32[]{:S(2)}) collective-permute-start(bf16[2,128,256]{2,1,0:T(8,128)(2,1)S(1)} %get-tuple-element.65.refs_7_), channel_id=1, source_target_pairs={{0,1},{2,3},{3,2},{1,0},{4,5},{6,7},{7,6},{5,8},{8,9},{10,11},{11,... | collective-permute-start | bytes 393224 | tf_op jit(solution)/shard_map/ppermute | solution.py:572
  36.4 2.2 %collective-permute-done.10.refs_4_ = bf16[2,128,256]{2,1,0:T(8,128)(2,1)S(1)} collective-permute-done((bf16[2,128,256]{2,1,0:T(8,128)(2,1)S(1)}, bf16[2,128,256]{2,1,0:T(8,128)(2,1)S(1)}, u32[]{:S(2)}, u32[]{:S(2)}) %collective-permute-start.10) | collective-permute-done | bytes 131104 | tf_op jit(solution)/shard_map/ppermute | solution.py:572
  38.6 0.0 collective-permute-done.11.refs_5_
  38.6 0.0 collective-permute-done.9.refs_3_
  38.6 0.2 shard_map.87
  38.8 0.9 %shard_map.89 = (bf16[2,128,256]{2,1,0:T(8,128)(2,1)S(1)}, bf16[2,128,256]{2,1,0:T(8,128)(2,1)S(1)}) custom-call(bf16[2,512,256]{2,1,0:T(8,128)(2,1)S(1)} %get-tuple-element.67.refs_0_.slope_ref, bf16[2,512,768]{2,1,0:T(8,128)(2,1)S(1)} %get-tuple-element.49.refs_1_, ...), custom_call_target="tpu_custom_call", output_to_operand_aliasing={{0}: (6, {}), {1}: (7, {})} | custom-call | tf_op jit(solution)/shard_map/pallas_call | solution.py:363
  39.7 0.1 collective-permute-start.12
  39.8 1.3 %collective-permute-done.12.got_ref = bf16[2,128,256]{2,1,0:T(8,128)(2,1)S(1)} collective-permute-done((bf16[2,128,256]{2,1,0:T(8,128)(2,1)S(1)}, bf16[2,128,256]{2,1,0:T(8,128)(2,1)S(1)}, u32[]{:S(2)}, u32[]{:S(2)}) %collective-permute-start.12) | collective-permute-done | bytes 131104 | tf_op jit(solution)/shard_map/ppermute | solution.py:512
  41.1 3.5 %collective-permute-start.13 = (bf16[256,256]{1,0:T(8,128)(2,1)S(1)}, bf16[256,256]{1,0:T(8,128)(2,1)S(1)}, u32[]{:S(2)}, u32[]{:S(2)}) collective-permute-start(bf16[256,256]{1,0:T(8,128)(2,1)S(1)} %shard_map.90), channel_id=1, source_target_pairs={{0,4},{1,3},{2,6},{3,1},{4,0},{5,9},{6,2},{7,11},{8,12},{9,5},{10,... | collective-permute-start | bytes 393224 | tf_op jit(solution)/shard_map/ppermute | solution.py:516
  44.7 3.9 %collective-permute-done.13.refs_0_.near_ref = bf16[256,256]{1,0:T(8,128)(2,1)S(1)} collective-permute-done((bf16[256,256]{1,0:T(8,128)(2,1)S(1)}, bf16[256,256]{1,0:T(8,128)(2,1)S(1)}, u32[]{:S(2)}, u32[]{:S(2)}) %collective-permute-start.13) | collective-permute-done | bytes 131104 | tf_op jit(solution)/shard_map/ppermute | solution.py:516
  48.6 0.1 collective-permute-start.14
  48.7 0.7 shard_map.92
  49.3 2.5 %collective-permute-start.18 = (bf16[192,256]{1,0:T(8,128)(2,1)S(1)}, bf16[192,256]{1,0:T(8,128)(2,1)S(1)}, u32[]{:S(2)}, u32[]{:S(2)}) collective-permute-start(bf16[192,256]{1,0:T(8,128)(2,1)S(1)} %get-tuple-element.77), channel_id=1, source_target_pairs={{0,4},{4,0},{8,12},{12,8},{16,20},{20,16},{24,28},{28,24},{1,5},{5... | collective-permute-start | bytes 294920 | tf_op jit(solution)/shard_map/ppermute | solution.py:507
  51.9 0.1 collective-permute-start.15
  51.9 2.0 %collective-permute-start.16 = (bf16[96,256]{1,0:T(8,128)(2,1)S(1)}, bf16[96,256]{1,0:T(8,128)(2,1)S(1)}, u32[]{:S(2)}, u32[]{:S(2)}) collective-permute-start(bf16[96,256]{1,0:T(8,128)(2,1)S(1)} %get-tuple-element.74), channel_id=1, source_target_pairs={{0,8},{4,12},{8,0},{12,4},{16,24},{20,28},{24,16},{28,20},{1,9},{5... | collective-permute-start | bytes 147464 | tf_op jit(solution)/shard_map/ppermute | solution.py:507
  54.0 1.4 %collective-permute-start.17 = (bf16[96,256]{1,0:T(8,128)(2,1)S(1)}, bf16[96,256]{1,0:T(8,128)(2,1)S(1)}, u32[]{:S(2)}, u32[]{:S(2)}) collective-permute-start(bf16[96,256]{1,0:T(8,128)(2,1)S(1)} %get-tuple-element.75), channel_id=1, source_target_pairs={{0,12},{4,8},{8,4},{12,0},{16,28},{20,24},{24,20},{28,16},{1,13},{... | collective-permute-start | bytes 147464 | tf_op jit(solution)/shard_map/ppermute | solution.py:507
  55.4 0.2 collective-permute-done.18.pair_ref
  55.5 3.2 %collective-permute-start.19 = (bf16[96,256]{1,0:T(8,128)(2,1)S(1)}, bf16[96,256]{1,0:T(8,128)(2,1)S(1)}, u32[]{:S(2)}, u32[]{:S(2)}) collective-permute-start(bf16[96,256]{1,0:T(8,128)(2,1)S(1)} %get-tuple-element.78), channel_id=1, source_target_pairs={{0,16},{4,20},{8,24},{12,28},{16,0},{20,4},{24,8},{28,12},{1,17},{... | collective-permute-start | bytes 147464 | tf_op jit(solution)/shard_map/ppermute | solution.py:507
  58.7 0.0 collective-permute-done.15.refs_0_
  58.7 2.0 %collective-permute-start.20 = (bf16[96,256]{1,0:T(8,128)(2,1)S(1)}, bf16[96,256]{1,0:T(8,128)(2,1)S(1)}, u32[]{:S(2)}, u32[]{:S(2)}) collective-permute-start(bf16[96,256]{1,0:T(8,128)(2,1)S(1)} %get-tuple-element.79), channel_id=1, source_target_pairs={{0,24},{4,28},{8,16},{12,20},{16,8},{20,12},{24,0},{28,4},{1,25},{... | collective-permute-start | bytes 147464 | tf_op jit(solution)/shard_map/ppermute | solution.py:507
  60.8 0.1 collective-permute-done.19.refs_3_
  60.9 3.8 %collective-permute-done.20.refs_4_ = bf16[96,256]{1,0:T(8,128)(2,1)S(1)} collective-permute-done((bf16[96,256]{1,0:T(8,128)(2,1)S(1)}, bf16[96,256]{1,0:T(8,128)(2,1)S(1)}, u32[]{:S(2)}, u32[]{:S(2)}) %collective-permute-start.20) | collective-permute-done | bytes 49184 | tf_op jit(solution)/shard_map/ppermute | solution.py:507
  64.7 2.2 %collective-permute-start.22 = (bf16[96,256]{1,0:T(8,128)(2,1)S(1)}, bf16[96,256]{1,0:T(8,128)(2,1)S(1)}, u32[]{:S(2)}, u32[]{:S(2)}) collective-permute-start(bf16[96,256]{1,0:T(8,128)(2,1)S(1)} %shard_map.94.refs_0_), channel_id=1, source_target_pairs={{0,24},{4,28},{8,16},{12,20},{16,8},{20,12},{24,0},{28,4},{1,25},{... | collective-permute-start | bytes 147464 | tf_op jit(solution)/shard_map/ppermute | solution.py:507
  66.9 0.0 collective-permute-start.21
  66.9 3.8 %collective-permute-done.22.refs_2_.refs_4_ = bf16[96,256]{1,0:T(8,128)(2,1)S(1)} collective-permute-done((bf16[96,256]{1,0:T(8,128)(2,1)S(1)}, bf16[96,256]{1,0:T(8,128)(2,1)S(1)}, u32[]{:S(2)}, u32[]{:S(2)}) %collective-permute-start.22) | collective-permute-done | bytes 49184 | tf_op jit(solution)/shard_map/ppermute | solution.py:507
  70.6 1.2 %collective-permute-done.21.refs_1_.refs_3_ = bf16[96,256]{1,0:T(8,128)(2,1)S(1)} collective-permute-done((bf16[96,256]{1,0:T(8,128)(2,1)S(1)}, bf16[96,256]{1,0:T(8,128)(2,1)S(1)}, u32[]{:S(2)}, u32[]{:S(2)}) %collective-permute-start.21) | collective-permute-done | bytes 49184 | tf_op jit(solution)/shard_map/ppermute | solution.py:507
  71.9 1.4 %collective-permute-start.23 = (bf16[288,256]{1,0:T(8,128)(2,1)S(1)}, bf16[288,256]{1,0:T(8,128)(2,1)S(1)}, u32[]{:S(2)}, u32[]{:S(2)}) collective-permute-start(bf16[288,256]{1,0:T(8,128)(2,1)S(1)} %shard_map.95), channel_id=1, source_target_pairs={{0,4},{4,0},{8,12},{12,8},{16,20},{20,16},{24,28},{28,24},{1,5},{5... | collective-permute-start | bytes 442376 | tf_op jit(solution)/shard_map/ppermute | solution.py:507
  73.3 0.0 collective-permute-start.25
  73.3 2.1 %collective-permute-start.24 = (bf16[96,256]{1,0:T(8,128)(2,1)S(1)}, bf16[96,256]{1,0:T(8,128)(2,1)S(1)}, u32[]{:S(2)}, u32[]{:S(2)}) collective-permute-start(bf16[96,256]{1,0:T(8,128)(2,1)S(1)} %shard_map.94.refs_0_), channel_id=1, source_target_pairs={{0,8},{4,12},{8,0},{12,4},{16,24},{20,28},{24,16},{28,20},{1,9},{5... | collective-permute-start | bytes 147464 | tf_op jit(solution)/shard_map/ppermute | solution.py:507
  75.4 1.2 %shard_map.88.main_ref = bf16[2,512,256]{2,1,0:T(8,128)(2,1)S(1)} custom-call(bf16[2,512,256]{2,1,0:T(8,128)(2,1)S(1)} %get-tuple-element.67.refs_0_.slope_ref, bf16[2,512,768]{2,1,0:T(8,128)(2,1)S(1)} %get-tuple-element.49.refs_1_, bf16[1,3,256,256]{3,2,1,0:T(8,128)(2,1)S(1)} %copy-done, ...), custom_call_target="tpu_custom_call", output_to_operand_aliasing={{}: (6, {})} | custom-call | tf_op jit(solution)/shard_map/pallas_call | solution.py:363
  76.6 1.6 %collective-permute-done.25.refs_2_ = bf16[96,256]{1,0:T(8,128)(2,1)S(1)} collective-permute-done((bf16[96,256]{1,0:T(8,128)(2,1)S(1)}, bf16[96,256]{1,0:T(8,128)(2,1)S(1)}, u32[]{:S(2)}, u32[]{:S(2)}) %collective-permute-start.25) | collective-permute-done | bytes 49184 | tf_op jit(solution)/shard_map/ppermute | solution.py:507
  78.3 0.0 collective-permute-done.24.refs_1_
  78.3 0.8 %shard_map.96.refs_1_ = f32[768,256]{1,0:T(8,128)} custom-call(bf16[96,256]{1,0:T(8,128)(2,1)S(1)} %shard_map.94.refs_0_, bf16[96,256]{1,0:T(8,128)(2,1)S(1)} %collective-permute-done.24.refs_1_, bf16[96,256]{1,0:T(8,128)(2,1)S(1)} %collective-permute-done.25.refs_2_, bf16[96,256]{1,0:T(8,128)(2,1)S(1)} %collective-permute-done.21.refs_1_.refs_3_, ...), custom_call_target="tpu_custom_call" | custom-call | tf_op jit(solution)/shard_map/pallas_call | solution.py:471
  79.1 0.0 collective-permute-done.23.refs_0_
  79.1 0.7 shard_map.97
  79.9 0.0 collective-permute-done.14.far_ref
  79.9 0.9 %grad.1 = bf16[1,2,512,256]{3,2,1,0:T(8,128)(2,1)} custom-call(bf16[2,512,256]{2,1,0:T(8,128)(2,1)S(1)} %shard_map.88.main_ref, bf16[256,256]{1,0:T(8,128)(2,1)S(1)} %collective-permute-done.13.refs_0_.near_ref, bf16[768,256]{1,0:T(8,128)(2,1)S(1)} %collective-permute-done.14.far_ref), custom_call_target="tpu_custom_call" | custom-call | tf_op jit(solution)/shard_map/grad/pallas_call | solution.py:555
  (18 shorter events, 0.2 us)
Async XLA Ops:
  0.6 8.1 %copy-start.1 = (bf16[1,2,512,256]{3,2,1,0:T(8,128)(2,1)S(1)}, bf16[1,2,512,256]{3,2,1,0:T(8,128)(2,1)}, u32[]{:S(2)}) copy-start(bf16[1,2,512,256]{3,2,1,0:T(8,128)(2,1)} %x_ref.7) | copy-start | bytes 1572868
  0.6 8.1 %copy-start = (bf16[1,3,256,256]{3,2,1,0:T(8,128)(2,1)S(1)}, bf16[1,3,256,256]{3,2,1,0:T(8,128)(2,1)}, u32[]{:S(2)}) copy-start(bf16[1,3,256,256]{3,2,1,0:T(8,128)(2,1)} %refs_2_.19) | copy-start | bytes 1179652
  1.7 7.9 %collective-permute-start.1 = (bf16[2,128,256]{2,1,0:T(8,128)(2,1)S(1)}, bf16[2,128,256]{2,1,0:T(8,128)(2,1)S(1)}, u32[]{:S(2)}, u32[]{:S(2)}) collective-permute-start(bf16[2,128,256]{2,1,0:T(8,128)(2,1)S(1)} %get-tuple-element.43), channel_id=1, source_target_pairs={{0,1},{1,0},{2,3},{3,2},{4,8},{5,9},{6,10},{7,11},{8,4},{9,5},{10,... | collective-permute-start | bytes 393224 | tf_op jit(solution)/shard_map/ppermute | solution.py:575
  2.3 8.9 %collective-permute-start = (bf16[2,128,256]{2,1,0:T(8,128)(2,1)S(1)}, bf16[2,128,256]{2,1,0:T(8,128)(2,1)S(1)}, u32[]{:S(2)}, u32[]{:S(2)}) collective-permute-start(bf16[2,128,256]{2,1,0:T(8,128)(2,1)S(1)} %get-tuple-element.42), channel_id=1, source_target_pairs={{0,4},{1,5},{2,6},{3,7},{4,0},{5,1},{6,2},{7,3},{8,12},{9,13},{10,... | collective-permute-start | bytes 393224 | tf_op jit(solution)/shard_map/ppermute | solution.py:576
  9.6 1.0 %copy-start.2 = (bf16[2,512,256]{2,1,0:T(8,128)(2,1)S(1)}, bf16[2,512,256]{2,1,0:T(8,128)(2,1)}, u32[]{:S(2)}) copy-start(bf16[2,512,256]{2,1,0:T(8,128)(2,1)} %refs_3_.5) | copy-start | bytes 1572868
  12.0 2.4 %collective-permute-start.2 = (bf16[2,512,256]{2,1,0:T(8,128)(2,1)S(1)}, bf16[2,512,256]{2,1,0:T(8,128)(2,1)S(1)}, u32[]{:S(2)}, u32[]{:S(2)}) collective-permute-start(bf16[2,512,256]{2,1,0:T(8,128)(2,1)S(1)} %shard_map.82.refs_7_), channel_id=1, source_target_pairs={{0,1},{1,0},{2,3},{3,2},{4,5},{5,4},{6,7},{7,6},{8,9},{9,8},{10,11... | collective-permute-start | bytes 1572872 | tf_op jit(solution)/shard_map/ppermute | solution.py:572
  12.1 2.1 %collective-permute-start.3 = (bf16[2,128,256]{2,1,0:T(8,128)(2,1)S(1)}, bf16[2,128,256]{2,1,0:T(8,128)(2,1)S(1)}, u32[]{:S(2)}, u32[]{:S(2)}) collective-permute-start(bf16[2,128,256]{2,1,0:T(8,128)(2,1)S(1)} %get-tuple-element.52.refs_6_), channel_id=1, source_target_pairs={{0,1},{1,0},{2,3},{3,6},{4,5},{5,4},{6,7},{7,2},{8,9},{9,8},{10,11... | collective-permute-start | bytes 393224 | tf_op jit(solution)/shard_map/ppermute | solution.py:572
  12.6 1.8 %collective-permute-start.4 = (bf16[2,128,256]{2,1,0:T(8,128)(2,1)S(1)}, bf16[2,128,256]{2,1,0:T(8,128)(2,1)S(1)}, u32[]{:S(2)}, u32[]{:S(2)}) collective-permute-start(bf16[2,128,256]{2,1,0:T(8,128)(2,1)S(1)} %get-tuple-element.53.refs_7_), channel_id=1, source_target_pairs={{0,1},{1,0},{2,3},{3,2},{4,5},{5,4},{6,7},{7,10},{8,9},{9,8},{10,1... | collective-permute-start | bytes 393224 | tf_op jit(solution)/shard_map/ppermute | solution.py:572
  14.4 10.4 %collective-permute-start.5 = (bf16[512,256]{1,0:T(8,128)(2,1)S(1)}, bf16[512,256]{1,0:T(8,128)(2,1)S(1)}, u32[]{:S(2)}, u32[]{:S(2)}) collective-permute-start(bf16[512,256]{1,0:T(8,128)(2,1)S(1)} %get-tuple-element.54), channel_id=1, source_target_pairs={{0,3},{1,0},{2,1},{3,2},{4,7},{5,4},{6,5},{7,6},{8,11},{9,8},{10,9... | collective-permute-start | bytes 786440 | tf_op jit(solution)/shard_map/ppermute | solution.py:572
  20.9 6.7 %collective-permute-start.6 = (bf16[512,256]{1,0:T(8,128)(2,1)S(1)}, bf16[512,256]{1,0:T(8,128)(2,1)S(1)}, u32[]{:S(2)}, u32[]{:S(2)}) collective-permute-start(bf16[512,256]{1,0:T(8,128)(2,1)S(1)} %get-tuple-element.58), channel_id=1, source_target_pairs={{0,3},{1,0},{2,1},{3,2},{4,7},{5,4},{6,5},{7,6},{8,11},{9,8},{10,9... | collective-permute-start | bytes 786440 | tf_op jit(solution)/shard_map/ppermute | solution.py:572
  21.1 1.3 %collective-permute-start.7 = (bf16[2,128,256]{2,1,0:T(8,128)(2,1)S(1)}, bf16[2,128,256]{2,1,0:T(8,128)(2,1)S(1)}, u32[]{:S(2)}, u32[]{:S(2)}) collective-permute-start(bf16[2,128,256]{2,1,0:T(8,128)(2,1)S(1)} %get-tuple-element.59.refs_7_), channel_id=1, source_target_pairs={{2,5},{6,1},{10,13},{14,9},{18,21},{22,17},{26,29},{30,25}} | collective-permute-start | bytes 393224 | tf_op jit(solution)/shard_map/ppermute | solution.py:572
  21.8 0.7 collective-permute-start.8
  27.6 11.1 %collective-permute-start.9 = (bf16[2,512,256]{2,1,0:T(8,128)(2,1)S(1)}, bf16[2,512,256]{2,1,0:T(8,128)(2,1)S(1)}, u32[]{:S(2)}, u32[]{:S(2)}) collective-permute-start(bf16[2,512,256]{2,1,0:T(8,128)(2,1)S(1)} %shard_map.86.refs_6_), channel_id=1, source_target_pairs={{0,1},{1,0},{2,3},{3,2},{4,5},{5,4},{6,7},{7,6},{8,9},{9,8},{10,11... | collective-permute-start | bytes 1572872 | tf_op jit(solution)/shard_map/ppermute | solution.py:572
  31.4 7.2 %collective-permute-start.10 = (bf16[2,128,256]{2,1,0:T(8,128)(2,1)S(1)}, bf16[2,128,256]{2,1,0:T(8,128)(2,1)S(1)}, u32[]{:S(2)}, u32[]{:S(2)}) collective-permute-start(bf16[2,128,256]{2,1,0:T(8,128)(2,1)S(1)} %get-tuple-element.64.refs_6_), channel_id=1, source_target_pairs={{0,1},{2,3},{3,2},{1,4},{4,5},{6,7},{7,6},{5,0},{8,9},{10,11},{11,... | collective-permute-start | bytes 393224 | tf_op jit(solution)/shard_map/ppermute | solution.py:572
  31.5 7.1 %collective-permute-start.11 = (bf16[2,128,256]{2,1,0:T(8,128)(2,1)S(1)}, bf16[2,128,256]{2,1,0:T(8,128)(2,1)S(1)}, u32[]{:S(2)}, u32[]{:S(2)}) collective-permute-start(bf16[2,128,256]{2,1,0:T(8,128)(2,1)S(1)} %get-tuple-element.65.refs_7_), channel_id=1, source_target_pairs={{0,1},{2,3},{3,2},{1,0},{4,5},{6,7},{7,6},{5,8},{8,9},{10,11},{11,... | collective-permute-start | bytes 393224 | tf_op jit(solution)/shard_map/ppermute | solution.py:572
  39.7 1.4 %collective-permute-start.12 = (bf16[2,128,256]{2,1,0:T(8,128)(2,1)S(1)}, bf16[2,128,256]{2,1,0:T(8,128)(2,1)S(1)}, u32[]{:S(2)}, u32[]{:S(2)}) collective-permute-start(bf16[2,128,256]{2,1,0:T(8,128)(2,1)S(1)} %get-tuple-element.68), channel_id=1, source_target_pairs={{0,1},{1,0},{2,3},{3,2},{4,5},{5,4},{6,7},{7,6},{8,9},{9,8},{10,11... | collective-permute-start | bytes 393224 | tf_op jit(solution)/shard_map/ppermute | solution.py:512
  41.1 7.4 %collective-permute-start.13 = (bf16[256,256]{1,0:T(8,128)(2,1)S(1)}, bf16[256,256]{1,0:T(8,128)(2,1)S(1)}, u32[]{:S(2)}, u32[]{:S(2)}) collective-permute-start(bf16[256,256]{1,0:T(8,128)(2,1)S(1)} %shard_map.90), channel_id=1, source_target_pairs={{0,4},{1,3},{2,6},{3,1},{4,0},{5,9},{6,2},{7,11},{8,12},{9,5},{10,... | collective-permute-start | bytes 393224 | tf_op jit(solution)/shard_map/ppermute | solution.py:516
  48.6 31.3 %collective-permute-start.14 = (bf16[768,256]{1,0:T(8,128)(2,1)S(1)}, bf16[768,256]{1,0:T(8,128)(2,1)S(1)}, u32[]{:S(2)}, u32[]{:S(2)}) collective-permute-start(bf16[768,256]{1,0:T(8,128)(2,1)S(1)} %shard_map.91), channel_id=1, source_target_pairs={{0,1},{1,0},{2,3},{3,2},{4,5},{5,4},{6,7},{7,6},{8,9},{9,8},{10,11... | collective-permute-start | bytes 1179656 | tf_op jit(solution)/shard_map/ppermute | solution.py:523
  49.3 6.2 %collective-permute-start.18 = (bf16[192,256]{1,0:T(8,128)(2,1)S(1)}, bf16[192,256]{1,0:T(8,128)(2,1)S(1)}, u32[]{:S(2)}, u32[]{:S(2)}) collective-permute-start(bf16[192,256]{1,0:T(8,128)(2,1)S(1)} %get-tuple-element.77), channel_id=1, source_target_pairs={{0,4},{4,0},{8,12},{12,8},{16,20},{20,16},{24,28},{28,24},{1,5},{5... | collective-permute-start | bytes 294920 | tf_op jit(solution)/shard_map/ppermute | solution.py:507
  51.9 6.9 %collective-permute-start.15 = (bf16[96,256]{1,0:T(8,128)(2,1)S(1)}, bf16[96,256]{1,0:T(8,128)(2,1)S(1)}, u32[]{:S(2)}, u32[]{:S(2)}) collective-permute-start(bf16[96,256]{1,0:T(8,128)(2,1)S(1)} %get-tuple-element.73), channel_id=1, source_target_pairs={{0,4},{4,0},{8,12},{12,8},{16,20},{20,16},{24,28},{28,24},{1,5},{5... | collective-permute-start | bytes 147464 | tf_op jit(solution)/shard_map/ppermute | solution.py:507
  51.9 8.8 %collective-permute-start.16 = (bf16[96,256]{1,0:T(8,128)(2,1)S(1)}, bf16[96,256]{1,0:T(8,128)(2,1)S(1)}, u32[]{:S(2)}, u32[]{:S(2)}) collective-permute-start(bf16[96,256]{1,0:T(8,128)(2,1)S(1)} %get-tuple-element.74), channel_id=1, source_target_pairs={{0,8},{4,12},{8,0},{12,4},{16,24},{20,28},{24,16},{28,20},{1,9},{5... | collective-permute-start | bytes 147464 | tf_op jit(solution)/shard_map/ppermute | solution.py:507
  54.0 6.8 %collective-permute-start.17 = (bf16[96,256]{1,0:T(8,128)(2,1)S(1)}, bf16[96,256]{1,0:T(8,128)(2,1)S(1)}, u32[]{:S(2)}, u32[]{:S(2)}) collective-permute-start(bf16[96,256]{1,0:T(8,128)(2,1)S(1)} %get-tuple-element.75), channel_id=1, source_target_pairs={{0,12},{4,8},{8,4},{12,0},{16,28},{20,24},{24,20},{28,16},{1,13},{... | collective-permute-start | bytes 147464 | tf_op jit(solution)/shard_map/ppermute | solution.py:507
  55.5 5.3 %collective-permute-start.19 = (bf16[96,256]{1,0:T(8,128)(2,1)S(1)}, bf16[96,256]{1,0:T(8,128)(2,1)S(1)}, u32[]{:S(2)}, u32[]{:S(2)}) collective-permute-start(bf16[96,256]{1,0:T(8,128)(2,1)S(1)} %get-tuple-element.78), channel_id=1, source_target_pairs={{0,16},{4,20},{8,24},{12,28},{16,0},{20,4},{24,8},{28,12},{1,17},{... | collective-permute-start | bytes 147464 | tf_op jit(solution)/shard_map/ppermute | solution.py:507
  58.7 5.9 %collective-permute-start.20 = (bf16[96,256]{1,0:T(8,128)(2,1)S(1)}, bf16[96,256]{1,0:T(8,128)(2,1)S(1)}, u32[]{:S(2)}, u32[]{:S(2)}) collective-permute-start(bf16[96,256]{1,0:T(8,128)(2,1)S(1)} %get-tuple-element.79), channel_id=1, source_target_pairs={{0,24},{4,28},{8,16},{12,20},{16,8},{20,12},{24,0},{28,4},{1,25},{... | collective-permute-start | bytes 147464 | tf_op jit(solution)/shard_map/ppermute | solution.py:507
  64.7 6.0 %collective-permute-start.22 = (bf16[96,256]{1,0:T(8,128)(2,1)S(1)}, bf16[96,256]{1,0:T(8,128)(2,1)S(1)}, u32[]{:S(2)}, u32[]{:S(2)}) collective-permute-start(bf16[96,256]{1,0:T(8,128)(2,1)S(1)} %shard_map.94.refs_0_), channel_id=1, source_target_pairs={{0,24},{4,28},{8,16},{12,20},{16,8},{20,12},{24,0},{28,4},{1,25},{... | collective-permute-start | bytes 147464 | tf_op jit(solution)/shard_map/ppermute | solution.py:507
  66.9 5.0 %collective-permute-start.21 = (bf16[96,256]{1,0:T(8,128)(2,1)S(1)}, bf16[96,256]{1,0:T(8,128)(2,1)S(1)}, u32[]{:S(2)}, u32[]{:S(2)}) collective-permute-start(bf16[96,256]{1,0:T(8,128)(2,1)S(1)} %shard_map.94.refs_0_), channel_id=1, source_target_pairs={{0,16},{4,20},{8,24},{12,28},{16,0},{20,4},{24,8},{28,12},{1,17},{... | collective-permute-start | bytes 147464 | tf_op jit(solution)/shard_map/ppermute | solution.py:507
  71.9 7.3 %collective-permute-start.23 = (bf16[288,256]{1,0:T(8,128)(2,1)S(1)}, bf16[288,256]{1,0:T(8,128)(2,1)S(1)}, u32[]{:S(2)}, u32[]{:S(2)}) collective-permute-start(bf16[288,256]{1,0:T(8,128)(2,1)S(1)} %shard_map.95), channel_id=1, source_target_pairs={{0,4},{4,0},{8,12},{12,8},{16,20},{20,16},{24,28},{28,24},{1,5},{5... | collective-permute-start | bytes 442376 | tf_op jit(solution)/shard_map/ppermute | solution.py:507
  73.3 5.0 %collective-permute-start.25 = (bf16[96,256]{1,0:T(8,128)(2,1)S(1)}, bf16[96,256]{1,0:T(8,128)(2,1)S(1)}, u32[]{:S(2)}, u32[]{:S(2)}) collective-permute-start(bf16[96,256]{1,0:T(8,128)(2,1)S(1)} %shard_map.94.refs_0_), channel_id=1, source_target_pairs={{0,12},{4,8},{8,4},{12,0},{16,28},{20,24},{24,20},{28,16},{1,13},{... | collective-permute-start | bytes 147464 | tf_op jit(solution)/shard_map/ppermute | solution.py:507
  73.3 5.0 %collective-permute-start.24 = (bf16[96,256]{1,0:T(8,128)(2,1)S(1)}, bf16[96,256]{1,0:T(8,128)(2,1)S(1)}, u32[]{:S(2)}, u32[]{:S(2)}) collective-permute-start(bf16[96,256]{1,0:T(8,128)(2,1)S(1)} %shard_map.94.refs_0_), channel_id=1, source_target_pairs={{0,8},{4,12},{8,0},{12,4},{16,24},{20,28},{24,16},{28,20},{1,9},{5... | collective-permute-start | bytes 147464 | tf_op jit(solution)/shard_map/ppermute | solution.py:507

commit v4 on v3

--- a/solution.py
+++ b/solution.py
@@ -67,7 +67,11 @@
         j = i ^ 1 if side == 0 else (i + 1 if i % 2 else i - 1)
         inside = 0 <= j < lats
         if turn % 2:
-            pairs += [(i * sections + s, i * sections + (s ^ 1)) for s in range(sections) if s != turn]
+            p, q = (turn - 3) % sections, (turn - 2) % sections
+            ways = {s: s ^ 1 for s in range(sections) if s != turn}
+            if sections > 2:
+                ways.update({turn - 1: p, p: q, q: turn})
+            pairs += [(i * sections + s, i * sections + r) for s, r in ways.items()]
         if turn % 2 or inside:
             pairs.append((i * sections + turn, (j if inside else i) * sections + turn - 1))
     return pairs

time: 81 us -> 81 us (level)
  starting transfers between devices: 42.9 us -> 35.4 us
  waiting for transfers between devices: 25.4 us -> 32.9 us
    ppermute x10, waiting for transfers between devices: 9.01 us -> 16.8 us  [send(): return lax.ppermute(array, axis, pairs)]
    ppermute x10, starting transfers between devices: 17.6 us -> 9.79 us  [send(): return lax.ppermute(array, axis, pairs)]
where the time goes in v4:
time: 81 us; the launch traced here: 80.8 us
  starting transfers between devices  35.4 us (44%)
  waiting for transfers between devices  32.9 us (41%)
  Pallas kernels  11.4 us (14%)
  between operations  0.88 us (1%)
    ppermute x11, starting transfers between devices, meet(): return lax.ppermute(a, 'lat', [(i, i ^ bits) for i in range(lats)])  17 us
    ppermute x10, waiting for transfers between devices, send(): return lax.ppermute(array, axis, pairs)  16.8 us
    ppermute x11, waiting for transfers between devices, meet(): return lax.ppermute(a, 'lat', [(i, i ^ bits) for i in range(lats)])  10.6 us
    ppermute x10, starting transfers between devices, send(): return lax.ppermute(array, axis, pairs)  9.79 us
    ppermute x1, starting transfers between devices, per_device(): near = lax.ppermute(near, both, sides[0])  4.02 us
    ppermute x1, waiting for transfers between devices, reduce_weight(): rims = lax.ppermute(rims, ('lat', 'section'), edge_pairs(lats, sections))  3.89 us
    ppermute x1, starting transfers between devices, reduce_weight(): rims = lax.ppermute(rims, ('lat', 'section'), edge_pairs(lats, sections))  3.4 us
    pallas_call x3, Pallas kernels, hidden_call(): pl.pallas_call(functools.partial(hidden_kernel, part), out_shape=(pltpu.V...  2.39 us
  transfers between devices with their start and end apart: 26, of which 14 were waited for; matrix products, arithmetic and copies ran while one was open for 0% of the time, Pallas kernels for 9%

profile of v4, /device:TPU:0, one launch (start us, length us, event | category | flops | bytes accessed | tf_op | source)
XLA Modules:
  0.0 80.8 jit_solution(16434478202274027341)
XLA Ops:
  0.6 1.1 %rim.1 = (bf16[2,128,256]{2,1,0:T(8,128)(2,1)S(1)}, bf16[2,128,256]{2,1,0:T(8,128)(2,1)S(1)}) custom-call(bf16[1,2,512,256]{3,2,1,0:T(8,128)(2,1)} %x_ref.7), custom_call_target="tpu_custom_call" | custom-call | tf_op jit(solution)/shard_map/rim/pallas_call | solution.py:218
  1.7 0.6 collective-permute-start.1
  2.3 4.0 %collective-permute-start = (bf16[2,128,256]{2,1,0:T(8,128)(2,1)S(1)}, bf16[2,128,256]{2,1,0:T(8,128)(2,1)S(1)}, u32[]{:S(2)}, u32[]{:S(2)}) collective-permute-start(bf16[2,128,256]{2,1,0:T(8,128)(2,1)S(1)} %get-tuple-element.42), channel_id=1, source_target_pairs={{0,4},{1,5},{2,6},{3,7},{4,0},{5,1},{6,2},{7,3},{8,12},{9,13},{10,... | collective-permute-start | bytes 393224 | tf_op jit(solution)/shard_map/ppermute | solution.py:580
  6.3 2.4 %band.1 = (bf16[2,768,512]{2,1,0:T(8,128)(2,1)S(1)}, bf16[2,512,768]{2,1,0:T(8,128)(2,1)S(1)}) custom-call(s32[8,5]{1,0:T(8,128)} %index_in.1, s32[8,5]{1,0:T(8,128)} %mask_in.1, bf16[3,8,5,64,64]{4,3,2,1,0:T(8,128)(2,1)} %quad_in.1), custom_call_target="tpu_custom_call" | custom-call | tf_op jit(solution)/shard_map/band/pallas_call | solution.py:129
  8.7 0.9 %shard_map.77 = (bf16[2,2,768,256]{3,2,1,0:T(8,128)(2,1)S(1)}, f32[2,512,256]{2,1,0:T(8,128)S(1)}) custom-call(bf16[1,2,512,256]{3,2,1,0:T(8,128)(2,1)S(1)} %copy-done.1, bf16[2,768,512]{2,1,0:T(8,128)(2,1)S(1)} %get-tuple-element.41.band_ref, bf16[1,3,256,256]{3,2,1,0:T(8,128)(2,1)S(1)} %copy-done), custom_call_target="tpu_custom_call" | custom-call | flops 1073741824 | bytes 4194304 | tf_op jit(solution)/shard_map/pallas_call | solution.py:190
  9.6 0.0 collective-permute-done.1.refs_0_
  9.6 0.0 copy-start.2
  9.7 0.7 shard_map.78
  10.4 0.3 copy-done.2
  10.7 0.5 collective-permute-done.refs_0_
  11.2 0.7 shard_map.79
  12.0 0.1 collective-permute-start.2
  12.1 0.5 collective-permute-start.3
  12.6 2.6 %collective-permute-start.4 = (bf16[2,128,256]{2,1,0:T(8,128)(2,1)S(1)}, bf16[2,128,256]{2,1,0:T(8,128)(2,1)S(1)}, u32[]{:S(2)}, u32[]{:S(2)}) collective-permute-start(bf16[2,128,256]{2,1,0:T(8,128)(2,1)S(1)} %get-tuple-element.53.refs_7_), channel_id=1, source_target_pairs={{0,1},{1,3},{2,0},{3,2},{4,5},{5,7},{6,4},{7,10},{8,9},{9,11},{10,... | collective-permute-start | bytes 393224 | tf_op jit(solution)/shard_map/ppermute | solution.py:576
  15.1 3.1 %collective-permute-done.3.refs_4_ = bf16[2,128,256]{2,1,0:T(8,128)(2,1)S(1)} collective-permute-done((bf16[2,128,256]{2,1,0:T(8,128)(2,1)S(1)}, bf16[2,128,256]{2,1,0:T(8,128)(2,1)S(1)}, u32[]{:S(2)}, u32[]{:S(2)}) %collective-permute-start.3) | collective-permute-done | bytes 131104 | tf_op jit(solution)/shard_map/ppermute | solution.py:576
  18.3 1.4 %collective-permute-done.4.refs_5_ = bf16[2,128,256]{2,1,0:T(8,128)(2,1)S(1)} collective-permute-done((bf16[2,128,256]{2,1,0:T(8,128)(2,1)S(1)}, bf16[2,128,256]{2,1,0:T(8,128)(2,1)S(1)}, u32[]{:S(2)}, u32[]{:S(2)}) %collective-permute-start.4) | collective-permute-done | bytes 131104 | tf_op jit(solution)/shard_map/ppermute | solution.py:576
  19.7 0.0 collective-permute-done.2.refs_3_
  19.7 1.7 %collective-permute-start.5 = (bf16[512,256]{1,0:T(8,128)(2,1)S(1)}, bf16[512,256]{1,0:T(8,128)(2,1)S(1)}, u32[]{:S(2)}, u32[]{:S(2)}) collective-permute-start(bf16[512,256]{1,0:T(8,128)(2,1)S(1)} %get-tuple-element.54), channel_id=1, source_target_pairs={{0,3},{1,0},{2,1},{3,2},{4,7},{5,4},{6,5},{7,6},{8,11},{9,8},{10,9... | collective-permute-start | bytes 786440 | tf_op jit(solution)/shard_map/ppermute | solution.py:576
  21.4 0.1 collective-permute-start.6
  21.4 0.7 collective-permute-start.7
  22.1 0.7 collective-permute-start.8
  22.8 0.0 collective-permute-done.7.refs_5_
  22.8 0.0 collective-permute-done.8.refs_6_
  22.8 2.5 %collective-permute-done.5.refs_3_ = bf16[512,256]{1,0:T(8,128)(2,1)S(1)} collective-permute-done((bf16[512,256]{1,0:T(8,128)(2,1)S(1)}, bf16[512,256]{1,0:T(8,128)(2,1)S(1)}, u32[]{:S(2)}, u32[]{:S(2)}) %collective-permute-start.5) | collective-permute-done | bytes 262176 | tf_op jit(solution)/shard_map/ppermute | solution.py:576
  25.3 2.8 %collective-permute-done.6.refs_4_ = bf16[512,256]{1,0:T(8,128)(2,1)S(1)} collective-permute-done((bf16[512,256]{1,0:T(8,128)(2,1)S(1)}, bf16[512,256]{1,0:T(8,128)(2,1)S(1)}, u32[]{:S(2)}, u32[]{:S(2)}) %collective-permute-start.6) | collective-permute-done | bytes 262176 | tf_op jit(solution)/shard_map/ppermute | solution.py:576
  28.1 3.6 %collective-permute-start.9 = (bf16[2,512,256]{2,1,0:T(8,128)(2,1)S(1)}, bf16[2,512,256]{2,1,0:T(8,128)(2,1)S(1)}, u32[]{:S(2)}, u32[]{:S(2)}) collective-permute-start(bf16[2,512,256]{2,1,0:T(8,128)(2,1)S(1)} %shard_map.86.refs_6_), channel_id=1, source_target_pairs={{0,1},{1,0},{2,3},{3,2},{4,5},{5,4},{6,7},{7,6},{8,9},{9,8},{10,11... | collective-permute-start | bytes 1572872 | tf_op jit(solution)/shard_map/ppermute | solution.py:576
  31.6 0.0 collective-permute-start.10
  31.6 0.0 collective-permute-start.11
  31.7 7.0 %collective-permute-done.10.refs_4_ = bf16[2,128,256]{2,1,0:T(8,128)(2,1)S(1)} collective-permute-done((bf16[2,128,256]{2,1,0:T(8,128)(2,1)S(1)}, bf16[2,128,256]{2,1,0:T(8,128)(2,1)S(1)}, u32[]{:S(2)}, u32[]{:S(2)}) %collective-permute-start.10) | collective-permute-done | bytes 131104 | tf_op jit(solution)/shard_map/ppermute | solution.py:576
  38.6 0.0 collective-permute-done.11.refs_5_
  38.6 0.0 collective-permute-done.9.refs_3_
  38.6 0.2 shard_map.87
  38.8 0.9 %shard_map.89 = (bf16[2,128,256]{2,1,0:T(8,128)(2,1)S(1)}, bf16[2,128,256]{2,1,0:T(8,128)(2,1)S(1)}) custom-call(bf16[2,512,256]{2,1,0:T(8,128)(2,1)S(1)} %get-tuple-element.67.refs_0_.slope_ref, bf16[2,512,768]{2,1,0:T(8,128)(2,1)S(1)} %get-tuple-element.49.refs_1_, ...), custom_call_target="tpu_custom_call", output_to_operand_aliasing={{0}: (6, {}), {1}: (7, {})} | custom-call | tf_op jit(solution)/shard_map/pallas_call | solution.py:367
  39.7 0.6 collective-permute-start.12
  40.2 1.0 %collective-permute-done.12.got_ref = bf16[2,128,256]{2,1,0:T(8,128)(2,1)S(1)} collective-permute-done((bf16[2,128,256]{2,1,0:T(8,128)(2,1)S(1)}, bf16[2,128,256]{2,1,0:T(8,128)(2,1)S(1)}, u32[]{:S(2)}, u32[]{:S(2)}) %collective-permute-start.12) | collective-permute-done | bytes 131104 | tf_op jit(solution)/shard_map/ppermute | solution.py:516
  41.3 3.4 %collective-permute-start.13 = (bf16[256,256]{1,0:T(8,128)(2,1)S(1)}, bf16[256,256]{1,0:T(8,128)(2,1)S(1)}, u32[]{:S(2)}, u32[]{:S(2)}) collective-permute-start(bf16[256,256]{1,0:T(8,128)(2,1)S(1)} %shard_map.90), channel_id=1, source_target_pairs={{0,4},{1,3},{2,6},{3,1},{4,0},{5,9},{6,2},{7,11},{8,12},{9,5},{10,... | collective-permute-start | bytes 393224 | tf_op jit(solution)/shard_map/ppermute | solution.py:520
  44.7 3.9 %collective-permute-done.13.refs_0_.near_ref = bf16[256,256]{1,0:T(8,128)(2,1)S(1)} collective-permute-done((bf16[256,256]{1,0:T(8,128)(2,1)S(1)}, bf16[256,256]{1,0:T(8,128)(2,1)S(1)}, u32[]{:S(2)}, u32[]{:S(2)}) %collective-permute-start.13) | collective-permute-done | bytes 131104 | tf_op jit(solution)/shard_map/ppermute | solution.py:520
  48.6 0.1 collective-permute-start.14
  48.7 0.7 shard_map.92
  49.3 2.5 %collective-permute-start.18 = (bf16[192,256]{1,0:T(8,128)(2,1)S(1)}, bf16[192,256]{1,0:T(8,128)(2,1)S(1)}, u32[]{:S(2)}, u32[]{:S(2)}) collective-permute-start(bf16[192,256]{1,0:T(8,128)(2,1)S(1)} %get-tuple-element.77), channel_id=1, source_target_pairs={{0,4},{4,0},{8,12},{12,8},{16,20},{20,16},{24,28},{28,24},{1,5},{5... | collective-permute-start | bytes 294920 | tf_op jit(solution)/shard_map/ppermute | solution.py:511
  51.9 0.1 collective-permute-start.15
  51.9 2.0 %collective-permute-start.16 = (bf16[96,256]{1,0:T(8,128)(2,1)S(1)}, bf16[96,256]{1,0:T(8,128)(2,1)S(1)}, u32[]{:S(2)}, u32[]{:S(2)}) collective-permute-start(bf16[96,256]{1,0:T(8,128)(2,1)S(1)} %get-tuple-element.74), channel_id=1, source_target_pairs={{0,8},{4,12},{8,0},{12,4},{16,24},{20,28},{24,16},{28,20},{1,9},{5... | collective-permute-start | bytes 147464 | tf_op jit(solution)/shard_map/ppermute | solution.py:511
  54.0 1.4 %collective-permute-start.17 = (bf16[96,256]{1,0:T(8,128)(2,1)S(1)}, bf16[96,256]{1,0:T(8,128)(2,1)S(1)}, u32[]{:S(2)}, u32[]{:S(2)}) collective-permute-start(bf16[96,256]{1,0:T(8,128)(2,1)S(1)} %get-tuple-element.75), channel_id=1, source_target_pairs={{0,12},{4,8},{8,4},{12,0},{16,28},{20,24},{24,20},{28,16},{1,13},{... | collective-permute-start | bytes 147464 | tf_op jit(solution)/shard_map/ppermute | solution.py:511
  55.4 0.2 collective-permute-done.18.pair_ref
  55.5 3.2 %collective-permute-start.19 = (bf16[96,256]{1,0:T(8,128)(2,1)S(1)}, bf16[96,256]{1,0:T(8,128)(2,1)S(1)}, u32[]{:S(2)}, u32[]{:S(2)}) collective-permute-start(bf16[96,256]{1,0:T(8,128)(2,1)S(1)} %get-tuple-element.78), channel_id=1, source_target_pairs={{0,16},{4,20},{8,24},{12,28},{16,0},{20,4},{24,8},{28,12},{1,17},{... | collective-permute-start | bytes 147464 | tf_op jit(solution)/shard_map/ppermute | solution.py:511
  58.7 0.0 collective-permute-done.15.refs_0_
  58.7 2.0 %collective-permute-start.20 = (bf16[96,256]{1,0:T(8,128)(2,1)S(1)}, bf16[96,256]{1,0:T(8,128)(2,1)S(1)}, u32[]{:S(2)}, u32[]{:S(2)}) collective-permute-start(bf16[96,256]{1,0:T(8,128)(2,1)S(1)} %get-tuple-element.79), channel_id=1, source_target_pairs={{0,24},{4,28},{8,16},{12,20},{16,8},{20,12},{24,0},{28,4},{1,25},{... | collective-permute-start | bytes 147464 | tf_op jit(solution)/shard_map/ppermute | solution.py:511
  60.8 0.1 collective-permute-done.19.refs_3_
  60.9 3.8 %collective-permute-done.20.refs_4_ = bf16[96,256]{1,0:T(8,128)(2,1)S(1)} collective-permute-done((bf16[96,256]{1,0:T(8,128)(2,1)S(1)}, bf16[96,256]{1,0:T(8,128)(2,1)S(1)}, u32[]{:S(2)}, u32[]{:S(2)}) %collective-permute-start.20) | collective-permute-done | bytes 49184 | tf_op jit(solution)/shard_map/ppermute | solution.py:511
  64.7 2.2 %collective-permute-start.22 = (bf16[96,256]{1,0:T(8,128)(2,1)S(1)}, bf16[96,256]{1,0:T(8,128)(2,1)S(1)}, u32[]{:S(2)}, u32[]{:S(2)}) collective-permute-start(bf16[96,256]{1,0:T(8,128)(2,1)S(1)} %shard_map.94.refs_0_), channel_id=1, source_target_pairs={{0,24},{4,28},{8,16},{12,20},{16,8},{20,12},{24,0},{28,4},{1,25},{... | collective-permute-start | bytes 147464 | tf_op jit(solution)/shard_map/ppermute | solution.py:511
  66.9 0.0 collective-permute-start.21
  66.9 3.8 %collective-permute-done.22.refs_2_.refs_4_ = bf16[96,256]{1,0:T(8,128)(2,1)S(1)} collective-permute-done((bf16[96,256]{1,0:T(8,128)(2,1)S(1)}, bf16[96,256]{1,0:T(8,128)(2,1)S(1)}, u32[]{:S(2)}, u32[]{:S(2)}) %collective-permute-start.22) | collective-permute-done | bytes 49184 | tf_op jit(solution)/shard_map/ppermute | solution.py:511
  70.6 1.2 %collective-permute-done.21.refs_1_.refs_3_ = bf16[96,256]{1,0:T(8,128)(2,1)S(1)} collective-permute-done((bf16[96,256]{1,0:T(8,128)(2,1)S(1)}, bf16[96,256]{1,0:T(8,128)(2,1)S(1)}, u32[]{:S(2)}, u32[]{:S(2)}) %collective-permute-start.21) | collective-permute-done | bytes 49184 | tf_op jit(solution)/shard_map/ppermute | solution.py:511
  71.9 1.4 %collective-permute-start.23 = (bf16[288,256]{1,0:T(8,128)(2,1)S(1)}, bf16[288,256]{1,0:T(8,128)(2,1)S(1)}, u32[]{:S(2)}, u32[]{:S(2)}) collective-permute-start(bf16[288,256]{1,0:T(8,128)(2,1)S(1)} %shard_map.95), channel_id=1, source_target_pairs={{0,4},{4,0},{8,12},{12,8},{16,20},{20,16},{24,28},{28,24},{1,5},{5... | collective-permute-start | bytes 442376 | tf_op jit(solution)/shard_map/ppermute | solution.py:511
  73.3 0.0 collective-permute-start.25
  73.3 2.1 %collective-permute-start.24 = (bf16[96,256]{1,0:T(8,128)(2,1)S(1)}, bf16[96,256]{1,0:T(8,128)(2,1)S(1)}, u32[]{:S(2)}, u32[]{:S(2)}) collective-permute-start(bf16[96,256]{1,0:T(8,128)(2,1)S(1)} %shard_map.94.refs_0_), channel_id=1, source_target_pairs={{0,8},{4,12},{8,0},{12,4},{16,24},{20,28},{24,16},{28,20},{1,9},{5... | collective-permute-start | bytes 147464 | tf_op jit(solution)/shard_map/ppermute | solution.py:511
  75.4 1.2 %shard_map.88.main_ref = bf16[2,512,256]{2,1,0:T(8,128)(2,1)S(1)} custom-call(bf16[2,512,256]{2,1,0:T(8,128)(2,1)S(1)} %get-tuple-element.67.refs_0_.slope_ref, bf16[2,512,768]{2,1,0:T(8,128)(2,1)S(1)} %get-tuple-element.49.refs_1_, bf16[1,3,256,256]{3,2,1,0:T(8,128)(2,1)S(1)} %copy-done, ...), custom_call_target="tpu_custom_call", output_to_operand_aliasing={{}: (6, {})} | custom-call | tf_op jit(solution)/shard_map/pallas_call | solution.py:367
  76.6 1.6 %collective-permute-done.25.refs_2_ = bf16[96,256]{1,0:T(8,128)(2,1)S(1)} collective-permute-done((bf16[96,256]{1,0:T(8,128)(2,1)S(1)}, bf16[96,256]{1,0:T(8,128)(2,1)S(1)}, u32[]{:S(2)}, u32[]{:S(2)}) %collective-permute-start.25) | collective-permute-done | bytes 49184 | tf_op jit(solution)/shard_map/ppermute | solution.py:511
  78.3 0.0 collective-permute-done.24.refs_1_
  78.3 0.8 %shard_map.96.refs_1_ = f32[768,256]{1,0:T(8,128)} custom-call(bf16[96,256]{1,0:T(8,128)(2,1)S(1)} %shard_map.94.refs_0_, bf16[96,256]{1,0:T(8,128)(2,1)S(1)} %collective-permute-done.24.refs_1_, bf16[96,256]{1,0:T(8,128)(2,1)S(1)} %collective-permute-done.25.refs_2_, bf16[96,256]{1,0:T(8,128)(2,1)S(1)} %collective-permute-done.21.refs_1_.refs_3_, ...), custom_call_target="tpu_custom_call" | custom-call | tf_op jit(solution)/shard_map/pallas_call | solution.py:475
  79.1 0.0 collective-permute-done.23.refs_0_
  79.1 0.7 shard_map.97
  79.9 0.0 collective-permute-done.14.far_ref
  79.9 0.9 %grad.1 = bf16[1,2,512,256]{3,2,1,0:T(8,128)(2,1)} custom-call(bf16[2,512,256]{2,1,0:T(8,128)(2,1)S(1)} %shard_map.88.main_ref, bf16[256,256]{1,0:T(8,128)(2,1)S(1)} %collective-permute-done.13.refs_0_.near_ref, bf16[768,256]{1,0:T(8,128)(2,1)S(1)} %collective-permute-done.14.far_ref), custom_call_target="tpu_custom_call" | custom-call | tf_op jit(solution)/shard_map/grad/pallas_call | solution.py:559
  (18 shorter events, 0.2 us)
Async XLA Ops:
  0.6 8.1 %copy-start.1 = (bf16[1,2,512,256]{3,2,1,0:T(8,128)(2,1)S(1)}, bf16[1,2,512,256]{3,2,1,0:T(8,128)(2,1)}, u32[]{:S(2)}) copy-start(bf16[1,2,512,256]{3,2,1,0:T(8,128)(2,1)} %x_ref.7) | copy-start | bytes 1572868
  0.6 8.1 %copy-start = (bf16[1,3,256,256]{3,2,1,0:T(8,128)(2,1)S(1)}, bf16[1,3,256,256]{3,2,1,0:T(8,128)(2,1)}, u32[]{:S(2)}) copy-start(bf16[1,3,256,256]{3,2,1,0:T(8,128)(2,1)} %refs_2_.19) | copy-start | bytes 1179652
  1.7 7.9 %collective-permute-start.1 = (bf16[2,128,256]{2,1,0:T(8,128)(2,1)S(1)}, bf16[2,128,256]{2,1,0:T(8,128)(2,1)S(1)}, u32[]{:S(2)}, u32[]{:S(2)}) collective-permute-start(bf16[2,128,256]{2,1,0:T(8,128)(2,1)S(1)} %get-tuple-element.43), channel_id=1, source_target_pairs={{0,1},{1,0},{2,3},{3,2},{4,8},{5,9},{6,10},{7,11},{8,4},{9,5},{10,... | collective-permute-start | bytes 393224 | tf_op jit(solution)/shard_map/ppermute | solution.py:579
  2.3 8.9 %collective-permute-start = (bf16[2,128,256]{2,1,0:T(8,128)(2,1)S(1)}, bf16[2,128,256]{2,1,0:T(8,128)(2,1)S(1)}, u32[]{:S(2)}, u32[]{:S(2)}) collective-permute-start(bf16[2,128,256]{2,1,0:T(8,128)(2,1)S(1)} %get-tuple-element.42), channel_id=1, source_target_pairs={{0,4},{1,5},{2,6},{3,7},{4,0},{5,1},{6,2},{7,3},{8,12},{9,13},{10,... | collective-permute-start | bytes 393224 | tf_op jit(solution)/shard_map/ppermute | solution.py:580
  9.6 1.0 %copy-start.2 = (bf16[2,512,256]{2,1,0:T(8,128)(2,1)S(1)}, bf16[2,512,256]{2,1,0:T(8,128)(2,1)}, u32[]{:S(2)}) copy-start(bf16[2,512,256]{2,1,0:T(8,128)(2,1)} %refs_3_.5) | copy-start | bytes 1572868
  12.0 7.7 %collective-permute-start.2 = (bf16[2,512,256]{2,1,0:T(8,128)(2,1)S(1)}, bf16[2,512,256]{2,1,0:T(8,128)(2,1)S(1)}, u32[]{:S(2)}, u32[]{:S(2)}) collective-permute-start(bf16[2,512,256]{2,1,0:T(8,128)(2,1)S(1)} %shard_map.82.refs_7_), channel_id=1, source_target_pairs={{0,1},{1,0},{2,3},{3,2},{4,5},{5,4},{6,7},{7,6},{8,9},{9,8},{10,11... | collective-permute-start | bytes 1572872 | tf_op jit(solution)/shard_map/ppermute | solution.py:576
  12.1 6.2 %collective-permute-start.3 = (bf16[2,128,256]{2,1,0:T(8,128)(2,1)S(1)}, bf16[2,128,256]{2,1,0:T(8,128)(2,1)S(1)}, u32[]{:S(2)}, u32[]{:S(2)}) collective-permute-start(bf16[2,128,256]{2,1,0:T(8,128)(2,1)S(1)} %get-tuple-element.52.refs_6_), channel_id=1, source_target_pairs={{0,1},{1,3},{2,0},{3,6},{4,5},{5,7},{6,4},{7,2},{8,9},{9,11},{10,8... | collective-permute-start | bytes 393224 | tf_op jit(solution)/shard_map/ppermute | solution.py:576
  12.6 7.1 %collective-permute-start.4 = (bf16[2,128,256]{2,1,0:T(8,128)(2,1)S(1)}, bf16[2,128,256]{2,1,0:T(8,128)(2,1)S(1)}, u32[]{:S(2)}, u32[]{:S(2)}) collective-permute-start(bf16[2,128,256]{2,1,0:T(8,128)(2,1)S(1)} %get-tuple-element.53.refs_7_), channel_id=1, source_target_pairs={{0,1},{1,3},{2,0},{3,2},{4,5},{5,7},{6,4},{7,10},{8,9},{9,11},{10,... | collective-permute-start | bytes 393224 | tf_op jit(solution)/shard_map/ppermute | solution.py:576
  19.7 5.6 %collective-permute-start.5 = (bf16[512,256]{1,0:T(8,128)(2,1)S(1)}, bf16[512,256]{1,0:T(8,128)(2,1)S(1)}, u32[]{:S(2)}, u32[]{:S(2)}) collective-permute-start(bf16[512,256]{1,0:T(8,128)(2,1)S(1)} %get-tuple-element.54), channel_id=1, source_target_pairs={{0,3},{1,0},{2,1},{3,2},{4,7},{5,4},{6,5},{7,6},{8,11},{9,8},{10,9... | collective-permute-start | bytes 786440 | tf_op jit(solution)/shard_map/ppermute | solution.py:576
  21.4 6.7 %collective-permute-start.6 = (bf16[512,256]{1,0:T(8,128)(2,1)S(1)}, bf16[512,256]{1,0:T(8,128)(2,1)S(1)}, u32[]{:S(2)}, u32[]{:S(2)}) collective-permute-start(bf16[512,256]{1,0:T(8,128)(2,1)S(1)} %get-tuple-element.58), channel_id=1, source_target_pairs={{0,3},{1,0},{2,1},{3,2},{4,7},{5,4},{6,5},{7,6},{8,11},{9,8},{10,9... | collective-permute-start | bytes 786440 | tf_op jit(solution)/shard_map/ppermute | solution.py:576
  21.4 1.3 %collective-permute-start.7 = (bf16[2,128,256]{2,1,0:T(8,128)(2,1)S(1)}, bf16[2,128,256]{2,1,0:T(8,128)(2,1)S(1)}, u32[]{:S(2)}, u32[]{:S(2)}) collective-permute-start(bf16[2,128,256]{2,1,0:T(8,128)(2,1)S(1)} %get-tuple-element.59.refs_7_), channel_id=1, source_target_pairs={{2,5},{6,1},{10,13},{14,9},{18,21},{22,17},{26,29},{30,25}} | collective-permute-start | bytes 393224 | tf_op jit(solution)/shard_map/ppermute | solution.py:576
  22.1 0.7 collective-permute-start.8
  28.1 10.6 %collective-permute-start.9 = (bf16[2,512,256]{2,1,0:T(8,128)(2,1)S(1)}, bf16[2,512,256]{2,1,0:T(8,128)(2,1)S(1)}, u32[]{:S(2)}, u32[]{:S(2)}) collective-permute-start(bf16[2,512,256]{2,1,0:T(8,128)(2,1)S(1)} %shard_map.86.refs_6_), channel_id=1, source_target_pairs={{0,1},{1,0},{2,3},{3,2},{4,5},{5,4},{6,7},{7,6},{8,9},{9,8},{10,11... | collective-permute-start | bytes 1572872 | tf_op jit(solution)/shard_map/ppermute | solution.py:576
  31.6 7.0 %collective-permute-start.10 = (bf16[2,128,256]{2,1,0:T(8,128)(2,1)S(1)}, bf16[2,128,256]{2,1,0:T(8,128)(2,1)S(1)}, u32[]{:S(2)}, u32[]{:S(2)}) collective-permute-start(bf16[2,128,256]{2,1,0:T(8,128)(2,1)S(1)} %get-tuple-element.64.refs_6_), channel_id=1, source_target_pairs={{0,2},{2,3},{3,1},{1,4},{4,6},{6,7},{7,5},{5,0},{8,10},{10,11},{11... | collective-permute-start | bytes 393224 | tf_op jit(solution)/shard_map/ppermute | solution.py:576
  31.6 7.0 %collective-permute-start.11 = (bf16[2,128,256]{2,1,0:T(8,128)(2,1)S(1)}, bf16[2,128,256]{2,1,0:T(8,128)(2,1)S(1)}, u32[]{:S(2)}, u32[]{:S(2)}) collective-permute-start(bf16[2,128,256]{2,1,0:T(8,128)(2,1)S(1)} %get-tuple-element.65.refs_7_), channel_id=1, source_target_pairs={{0,2},{2,3},{3,1},{1,0},{4,6},{6,7},{7,5},{5,8},{8,10},{10,11},{11... | collective-permute-start | bytes 393224 | tf_op jit(solution)/shard_map/ppermute | solution.py:576
  39.7 1.5 %collective-permute-start.12 = (bf16[2,128,256]{2,1,0:T(8,128)(2,1)S(1)}, bf16[2,128,256]{2,1,0:T(8,128)(2,1)S(1)}, u32[]{:S(2)}, u32[]{:S(2)}) collective-permute-start(bf16[2,128,256]{2,1,0:T(8,128)(2,1)S(1)} %get-tuple-element.68), channel_id=1, source_target_pairs={{0,1},{1,0},{2,3},{3,2},{4,5},{5,4},{6,7},{7,6},{8,9},{9,8},{10,11... | collective-permute-start | bytes 393224 | tf_op jit(solution)/shard_map/ppermute | solution.py:516
  41.3 7.3 %collective-permute-start.13 = (bf16[256,256]{1,0:T(8,128)(2,1)S(1)}, bf16[256,256]{1,0:T(8,128)(2,1)S(1)}, u32[]{:S(2)}, u32[]{:S(2)}) collective-permute-start(bf16[256,256]{1,0:T(8,128)(2,1)S(1)} %shard_map.90), channel_id=1, source_target_pairs={{0,4},{1,3},{2,6},{3,1},{4,0},{5,9},{6,2},{7,11},{8,12},{9,5},{10,... | collective-permute-start | bytes 393224 | tf_op jit(solution)/shard_map/ppermute | solution.py:520
  48.6 31.3 %collective-permute-start.14 = (bf16[768,256]{1,0:T(8,128)(2,1)S(1)}, bf16[768,256]{1,0:T(8,128)(2,1)S(1)}, u32[]{:S(2)}, u32[]{:S(2)}) collective-permute-start(bf16[768,256]{1,0:T(8,128)(2,1)S(1)} %shard_map.91), channel_id=1, source_target_pairs={{0,1},{1,0},{2,3},{3,2},{4,5},{5,4},{6,7},{7,6},{8,9},{9,8},{10,11... | collective-permute-start | bytes 1179656 | tf_op jit(solution)/shard_map/ppermute | solution.py:527
  49.3 6.2 %collective-permute-start.18 = (bf16[192,256]{1,0:T(8,128)(2,1)S(1)}, bf16[192,256]{1,0:T(8,128)(2,1)S(1)}, u32[]{:S(2)}, u32[]{:S(2)}) collective-permute-start(bf16[192,256]{1,0:T(8,128)(2,1)S(1)} %get-tuple-element.77), channel_id=1, source_target_pairs={{0,4},{4,0},{8,12},{12,8},{16,20},{20,16},{24,28},{28,24},{1,5},{5... | collective-permute-start | bytes 294920 | tf_op jit(solution)/shard_map/ppermute | solution.py:511
  51.9 6.9 %collective-permute-start.15 = (bf16[96,256]{1,0:T(8,128)(2,1)S(1)}, bf16[96,256]{1,0:T(8,128)(2,1)S(1)}, u32[]{:S(2)}, u32[]{:S(2)}) collective-permute-start(bf16[96,256]{1,0:T(8,128)(2,1)S(1)} %get-tuple-element.73), channel_id=1, source_target_pairs={{0,4},{4,0},{8,12},{12,8},{16,20},{20,16},{24,28},{28,24},{1,5},{5... | collective-permute-start | bytes 147464 | tf_op jit(solution)/shard_map/ppermute | solution.py:511
  51.9 8.8 %collective-permute-start.16 = (bf16[96,256]{1,0:T(8,128)(2,1)S(1)}, bf16[96,256]{1,0:T(8,128)(2,1)S(1)}, u32[]{:S(2)}, u32[]{:S(2)}) collective-permute-start(bf16[96,256]{1,0:T(8,128)(2,1)S(1)} %get-tuple-element.74), channel_id=1, source_target_pairs={{0,8},{4,12},{8,0},{12,4},{16,24},{20,28},{24,16},{28,20},{1,9},{5... | collective-permute-start | bytes 147464 | tf_op jit(solution)/shard_map/ppermute | solution.py:511
  54.0 6.8 %collective-permute-start.17 = (bf16[96,256]{1,0:T(8,128)(2,1)S(1)}, bf16[96,256]{1,0:T(8,128)(2,1)S(1)}, u32[]{:S(2)}, u32[]{:S(2)}) collective-permute-start(bf16[96,256]{1,0:T(8,128)(2,1)S(1)} %get-tuple-element.75), channel_id=1, source_target_pairs={{0,12},{4,8},{8,4},{12,0},{16,28},{20,24},{24,20},{28,16},{1,13},{... | collective-permute-start | bytes 147464 | tf_op jit(solution)/shard_map/ppermute | solution.py:511
  55.5 5.3 %collective-permute-start.19 = (bf16[96,256]{1,0:T(8,128)(2,1)S(1)}, bf16[96,256]{1,0:T(8,128)(2,1)S(1)}, u32[]{:S(2)}, u32[]{:S(2)}) collective-permute-start(bf16[96,256]{1,0:T(8,128)(2,1)S(1)} %get-tuple-element.78), channel_id=1, source_target_pairs={{0,16},{4,20},{8,24},{12,28},{16,0},{20,4},{24,8},{28,12},{1,17},{... | collective-permute-start | bytes 147464 | tf_op jit(solution)/shard_map/ppermute | solution.py:511
  58.7 5.9 %collective-permute-start.20 = (bf16[96,256]{1,0:T(8,128)(2,1)S(1)}, bf16[96,256]{1,0:T(8,128)(2,1)S(1)}, u32[]{:S(2)}, u32[]{:S(2)}) collective-permute-start(bf16[96,256]{1,0:T(8,128)(2,1)S(1)} %get-tuple-element.79), channel_id=1, source_target_pairs={{0,24},{4,28},{8,16},{12,20},{16,8},{20,12},{24,0},{28,4},{1,25},{... | collective-permute-start | bytes 147464 | tf_op jit(solution)/shard_map/ppermute | solution.py:511
  64.7 6.0 %collective-permute-start.22 = (bf16[96,256]{1,0:T(8,128)(2,1)S(1)}, bf16[96,256]{1,0:T(8,128)(2,1)S(1)}, u32[]{:S(2)}, u32[]{:S(2)}) collective-permute-start(bf16[96,256]{1,0:T(8,128)(2,1)S(1)} %shard_map.94.refs_0_), channel_id=1, source_target_pairs={{0,24},{4,28},{8,16},{12,20},{16,8},{20,12},{24,0},{28,4},{1,25},{... | collective-permute-start | bytes 147464 | tf_op jit(solution)/shard_map/ppermute | solution.py:511
  66.9 5.0 %collective-permute-start.21 = (bf16[96,256]{1,0:T(8,128)(2,1)S(1)}, bf16[96,256]{1,0:T(8,128)(2,1)S(1)}, u32[]{:S(2)}, u32[]{:S(2)}) collective-permute-start(bf16[96,256]{1,0:T(8,128)(2,1)S(1)} %shard_map.94.refs_0_), channel_id=1, source_target_pairs={{0,16},{4,20},{8,24},{12,28},{16,0},{20,4},{24,8},{28,12},{1,17},{... | collective-permute-start | bytes 147464 | tf_op jit(solution)/shard_map/ppermute | solution.py:511
  71.9 7.3 %collective-permute-start.23 = (bf16[288,256]{1,0:T(8,128)(2,1)S(1)}, bf16[288,256]{1,0:T(8,128)(2,1)S(1)}, u32[]{:S(2)}, u32[]{:S(2)}) collective-permute-start(bf16[288,256]{1,0:T(8,128)(2,1)S(1)} %shard_map.95), channel_id=1, source_target_pairs={{0,4},{4,0},{8,12},{12,8},{16,20},{20,16},{24,28},{28,24},{1,5},{5... | collective-permute-start | bytes 442376 | tf_op jit(solution)/shard_map/ppermute | solution.py:511
  73.3 5.0 %collective-permute-start.25 = (bf16[96,256]{1,0:T(8,128)(2,1)S(1)}, bf16[96,256]{1,0:T(8,128)(2,1)S(1)}, u32[]{:S(2)}, u32[]{:S(2)}) collective-permute-start(bf16[96,256]{1,0:T(8,128)(2,1)S(1)} %shard_map.94.refs_0_), channel_id=1, source_target_pairs={{0,12},{4,8},{8,4},{12,0},{16,28},{20,24},{24,20},{28,16},{1,13},{... | collective-permute-start | bytes 147464 | tf_op jit(solution)/shard_map/ppermute | solution.py:511
  73.3 5.0 %collective-permute-start.24 = (bf16[96,256]{1,0:T(8,128)(2,1)S(1)}, bf16[96,256]{1,0:T(8,128)(2,1)S(1)}, u32[]{:S(2)}, u32[]{:S(2)}) collective-permute-start(bf16[96,256]{1,0:T(8,128)(2,1)S(1)} %shard_map.94.refs_0_), channel_id=1, source_target_pairs={{0,8},{4,12},{8,0},{12,4},{16,24},{20,28},{24,16},{28,20},{1,9},{5... | collective-permute-start | bytes 147464 | tf_op jit(solution)/shard_map/ppermute | solution.py:511

commit v5 on v4

--- a/solution.py
+++ b/solution.py
@@ -72,7 +72,11 @@
             if sections > 2:
                 ways.update({turn - 1: p, p: q, q: turn})
             pairs += [(i * sections + s, i * sections + r) for s, r in ways.items()]
-        if turn % 2 or inside:
+        elif sections > 2:
+            ways = {s: s ^ 1 for s in range(sections) if s != turn}
+            ways.update({turn - 1: turn - 2, turn - 2: turn + 1, turn + 1: turn})
+            pairs += [(i * sections + s, i * sections + r) for s, r in ways.items()]
+        if sections > 2 or turn % 2 or inside:
             pairs.append((i * sections + turn, (j if inside else i) * sections + turn - 1))
     return pairs
 

time: 81 us -> 81 us (level)
  waiting for transfers between devices: 32.9 us -> 34.2 us
  starting transfers between devices: 35.4 us -> 34.1 us
    ppermute x10, waiting for transfers between devices: 16.8 us -> 18.2 us  [send(): return lax.ppermute(array, axis, pairs)]
    ppermute x10, starting transfers between devices: 9.79 us -> 8.45 us  [send(): return lax.ppermute(array, axis, pairs)]
where the time goes in v5:
time: 81 us; the launch traced here: 80.8 us
  waiting for transfers between devices  34.2 us (42%)
  starting transfers between devices  34.1 us (42%)
  Pallas kernels  11.4 us (14%)
  between operations  0.85 us (1%)
    ppermute x10, waiting for transfers between devices, send(): return lax.ppermute(array, axis, pairs)  18.2 us
    ppermute x11, starting transfers between devices, meet(): return lax.ppermute(a, 'lat', [(i, i ^ bits) for i in range(lats)])  17 us
    ppermute x11, waiting for transfers between devices, meet(): return lax.ppermute(a, 'lat', [(i, i ^ bits) for i in range(lats)])  10.6 us
    ppermute x10, starting transfers between devices, send(): return lax.ppermute(array, axis, pairs)  8.45 us
    ppermute x1, starting transfers between devices, per_device(): near = lax.ppermute(near, both, sides[0])  4.02 us
    ppermute x1, waiting for transfers between devices, reduce_weight(): rims = lax.ppermute(rims, ('lat', 'section'), edge_pairs(lats, sections))  3.89 us
    ppermute x1, starting transfers between devices, reduce_weight(): rims = lax.ppermute(rims, ('lat', 'section'), edge_pairs(lats, sections))  3.4 us
    pallas_call x3, Pallas kernels, hidden_call(): pl.pallas_call(functools.partial(hidden_kernel, part), out_shape=(pltpu.V...  2.39 us
  transfers between devices with their start and end apart: 26, of which 14 were waited for; matrix products, arithmetic and copies ran while one was open for 0% of the time, Pallas kernels for 9%

profile of v5, /device:TPU:0, one launch (start us, length us, event | category | flops | bytes accessed | tf_op | source)
XLA Modules:
  0.0 80.8 jit_solution(3986173678138288140)
XLA Ops:
  0.6 1.1 %rim.1 = (bf16[2,128,256]{2,1,0:T(8,128)(2,1)S(1)}, bf16[2,128,256]{2,1,0:T(8,128)(2,1)S(1)}) custom-call(bf16[1,2,512,256]{3,2,1,0:T(8,128)(2,1)} %x_ref.7), custom_call_target="tpu_custom_call" | custom-call | tf_op jit(solution)/shard_map/rim/pallas_call | solution.py:222
  1.7 0.6 collective-permute-start.1
  2.3 4.0 %collective-permute-start = (bf16[2,128,256]{2,1,0:T(8,128)(2,1)S(1)}, bf16[2,128,256]{2,1,0:T(8,128)(2,1)S(1)}, u32[]{:S(2)}, u32[]{:S(2)}) collective-permute-start(bf16[2,128,256]{2,1,0:T(8,128)(2,1)S(1)} %get-tuple-element.42), channel_id=1, source_target_pairs={{0,4},{1,5},{2,6},{3,7},{4,0},{5,1},{6,2},{7,3},{8,12},{9,13},{10,... | collective-permute-start | bytes 393224 | tf_op jit(solution)/shard_map/ppermute | solution.py:584
  6.3 2.4 %band.1 = (bf16[2,768,512]{2,1,0:T(8,128)(2,1)S(1)}, bf16[2,512,768]{2,1,0:T(8,128)(2,1)S(1)}) custom-call(s32[8,5]{1,0:T(8,128)} %index_in.1, s32[8,5]{1,0:T(8,128)} %mask_in.1, bf16[3,8,5,64,64]{4,3,2,1,0:T(8,128)(2,1)} %quad_in.1), custom_call_target="tpu_custom_call" | custom-call | tf_op jit(solution)/shard_map/band/pallas_call | solution.py:133
  8.7 0.9 %shard_map.77 = (bf16[2,2,768,256]{3,2,1,0:T(8,128)(2,1)S(1)}, f32[2,512,256]{2,1,0:T(8,128)S(1)}) custom-call(bf16[1,2,512,256]{3,2,1,0:T(8,128)(2,1)S(1)} %copy-done.1, bf16[2,768,512]{2,1,0:T(8,128)(2,1)S(1)} %get-tuple-element.41.band_ref, bf16[1,3,256,256]{3,2,1,0:T(8,128)(2,1)S(1)} %copy-done), custom_call_target="tpu_custom_call" | custom-call | flops 1073741824 | bytes 4194304 | tf_op jit(solution)/shard_map/pallas_call | solution.py:194
  9.6 0.0 collective-permute-done.1.refs_0_
  9.6 0.0 copy-start.2
  9.7 0.7 shard_map.78
  10.4 0.3 copy-done.2
  10.7 0.5 collective-permute-done.refs_0_
  11.2 0.7 shard_map.79
  12.0 0.1 collective-permute-start.2
  12.1 0.5 collective-permute-start.3
  12.6 2.6 %collective-permute-start.4 = (bf16[2,128,256]{2,1,0:T(8,128)(2,1)S(1)}, bf16[2,128,256]{2,1,0:T(8,128)(2,1)S(1)}, u32[]{:S(2)}, u32[]{:S(2)}) collective-permute-start(bf16[2,128,256]{2,1,0:T(8,128)(2,1)S(1)} %get-tuple-element.53.refs_7_), channel_id=1, source_target_pairs={{0,1},{1,3},{2,0},{3,2},{4,5},{5,7},{6,4},{7,10},{8,9},{9,11},{10,... | collective-permute-start | bytes 393224 | tf_op jit(solution)/shard_map/ppermute | solution.py:580
  15.1 3.1 %collective-permute-done.3.refs_4_ = bf16[2,128,256]{2,1,0:T(8,128)(2,1)S(1)} collective-permute-done((bf16[2,128,256]{2,1,0:T(8,128)(2,1)S(1)}, bf16[2,128,256]{2,1,0:T(8,128)(2,1)S(1)}, u32[]{:S(2)}, u32[]{:S(2)}) %collective-permute-start.3) | collective-permute-done | bytes 131104 | tf_op jit(solution)/shard_map/ppermute | solution.py:580
  18.3 1.4 %collective-permute-done.4.refs_5_ = bf16[2,128,256]{2,1,0:T(8,128)(2,1)S(1)} collective-permute-done((bf16[2,128,256]{2,1,0:T(8,128)(2,1)S(1)}, bf16[2,128,256]{2,1,0:T(8,128)(2,1)S(1)}, u32[]{:S(2)}, u32[]{:S(2)}) %collective-permute-start.4) | collective-permute-done | bytes 131104 | tf_op jit(solution)/shard_map/ppermute | solution.py:580
  19.7 0.0 collective-permute-done.2.refs_3_
  19.7 1.7 %collective-permute-start.5 = (bf16[512,256]{1,0:T(8,128)(2,1)S(1)}, bf16[512,256]{1,0:T(8,128)(2,1)S(1)}, u32[]{:S(2)}, u32[]{:S(2)}) collective-permute-start(bf16[512,256]{1,0:T(8,128)(2,1)S(1)} %get-tuple-element.54), channel_id=1, source_target_pairs={{0,3},{1,0},{2,1},{3,2},{4,7},{5,4},{6,5},{7,6},{8,11},{9,8},{10,9... | collective-permute-start | bytes 786440 | tf_op jit(solution)/shard_map/ppermute | solution.py:580
  21.4 0.1 collective-permute-start.6
  21.4 1.0 %collective-permute-start.7 = (bf16[2,128,256]{2,1,0:T(8,128)(2,1)S(1)}, bf16[2,128,256]{2,1,0:T(8,128)(2,1)S(1)}, u32[]{:S(2)}, u32[]{:S(2)}) collective-permute-start(bf16[2,128,256]{2,1,0:T(8,128)(2,1)S(1)} %get-tuple-element.59.refs_7_), channel_id=1, source_target_pairs={{0,3},{1,0},{3,2},{2,5},{4,7},{5,4},{7,6},{6,1},{8,11},{9,8},{11,1... | collective-permute-start | bytes 393224 | tf_op jit(solution)/shard_map/ppermute | solution.py:580
  22.5 0.1 collective-permute-start.8
  22.6 6.9 %collective-permute-done.7.refs_5_ = bf16[2,128,256]{2,1,0:T(8,128)(2,1)S(1)} collective-permute-done((bf16[2,128,256]{2,1,0:T(8,128)(2,1)S(1)}, bf16[2,128,256]{2,1,0:T(8,128)(2,1)S(1)}, u32[]{:S(2)}, u32[]{:S(2)}) %collective-permute-start.7) | collective-permute-done | bytes 131104 | tf_op jit(solution)/shard_map/ppermute | solution.py:580
  29.5 1.4 %collective-permute-done.8.refs_6_ = bf16[2,128,256]{2,1,0:T(8,128)(2,1)S(1)} collective-permute-done((bf16[2,128,256]{2,1,0:T(8,128)(2,1)S(1)}, bf16[2,128,256]{2,1,0:T(8,128)(2,1)S(1)}, u32[]{:S(2)}, u32[]{:S(2)}) %collective-permute-start.8) | collective-permute-done | bytes 131104 | tf_op jit(solution)/shard_map/ppermute | solution.py:580
  30.9 0.0 collective-permute-done.5.refs_3_
  30.9 0.0 collective-permute-done.6.refs_4_
  30.9 2.2 %collective-permute-start.9 = (bf16[2,512,256]{2,1,0:T(8,128)(2,1)S(1)}, bf16[2,512,256]{2,1,0:T(8,128)(2,1)S(1)}, u32[]{:S(2)}, u32[]{:S(2)}) collective-permute-start(bf16[2,512,256]{2,1,0:T(8,128)(2,1)S(1)} %shard_map.86.refs_6_), channel_id=1, source_target_pairs={{0,1},{1,0},{2,3},{3,2},{4,5},{5,4},{6,7},{7,6},{8,9},{9,8},{10,11... | collective-permute-start | bytes 1572872 | tf_op jit(solution)/shard_map/ppermute | solution.py:580
  33.1 0.2 collective-permute-start.10
  33.3 0.1 collective-permute-start.11
  33.3 5.3 %collective-permute-done.10.refs_4_ = bf16[2,128,256]{2,1,0:T(8,128)(2,1)S(1)} collective-permute-done((bf16[2,128,256]{2,1,0:T(8,128)(2,1)S(1)}, bf16[2,128,256]{2,1,0:T(8,128)(2,1)S(1)}, u32[]{:S(2)}, u32[]{:S(2)}) %collective-permute-start.10) | collective-permute-done | bytes 131104 | tf_op jit(solution)/shard_map/ppermute | solution.py:580
  38.6 0.0 collective-permute-done.11.refs_5_
  38.6 0.0 collective-permute-done.9.refs_3_
  38.6 0.2 shard_map.87
  38.8 0.9 %shard_map.89 = (bf16[2,128,256]{2,1,0:T(8,128)(2,1)S(1)}, bf16[2,128,256]{2,1,0:T(8,128)(2,1)S(1)}) custom-call(bf16[2,512,256]{2,1,0:T(8,128)(2,1)S(1)} %get-tuple-element.67.refs_0_.slope_ref, bf16[2,512,768]{2,1,0:T(8,128)(2,1)S(1)} %get-tuple-element.49.refs_1_, ...), custom_call_target="tpu_custom_call", output_to_operand_aliasing={{0}: (6, {}), {1}: (7, {})} | custom-call | tf_op jit(solution)/shard_map/pallas_call | solution.py:371
  39.7 0.6 collective-permute-start.12
  40.2 1.0 %collective-permute-done.12.got_ref = bf16[2,128,256]{2,1,0:T(8,128)(2,1)S(1)} collective-permute-done((bf16[2,128,256]{2,1,0:T(8,128)(2,1)S(1)}, bf16[2,128,256]{2,1,0:T(8,128)(2,1)S(1)}, u32[]{:S(2)}, u32[]{:S(2)}) %collective-permute-start.12) | collective-permute-done | bytes 131104 | tf_op jit(solution)/shard_map/ppermute | solution.py:520
  41.3 3.4 %collective-permute-start.13 = (bf16[256,256]{1,0:T(8,128)(2,1)S(1)}, bf16[256,256]{1,0:T(8,128)(2,1)S(1)}, u32[]{:S(2)}, u32[]{:S(2)}) collective-permute-start(bf16[256,256]{1,0:T(8,128)(2,1)S(1)} %shard_map.90), channel_id=1, source_target_pairs={{0,4},{1,3},{2,6},{3,1},{4,0},{5,9},{6,2},{7,11},{8,12},{9,5},{10,... | collective-permute-start | bytes 393224 | tf_op jit(solution)/shard_map/ppermute | solution.py:524
  44.7 3.9 %collective-permute-done.13.refs_0_.near_ref = bf16[256,256]{1,0:T(8,128)(2,1)S(1)} collective-permute-done((bf16[256,256]{1,0:T(8,128)(2,1)S(1)}, bf16[256,256]{1,0:T(8,128)(2,1)S(1)}, u32[]{:S(2)}, u32[]{:S(2)}) %collective-permute-start.13) | collective-permute-done | bytes 131104 | tf_op jit(solution)/shard_map/ppermute | solution.py:524
  48.6 0.1 collective-permute-start.14
  48.7 0.7 shard_map.92
  49.3 2.5 %collective-permute-start.18 = (bf16[192,256]{1,0:T(8,128)(2,1)S(1)}, bf16[192,256]{1,0:T(8,128)(2,1)S(1)}, u32[]{:S(2)}, u32[]{:S(2)}) collective-permute-start(bf16[192,256]{1,0:T(8,128)(2,1)S(1)} %get-tuple-element.77), channel_id=1, source_target_pairs={{0,4},{4,0},{8,12},{12,8},{16,20},{20,16},{24,28},{28,24},{1,5},{5... | collective-permute-start | bytes 294920 | tf_op jit(solution)/shard_map/ppermute | solution.py:515
  51.9 0.1 collective-permute-start.15
  51.9 2.0 %collective-permute-start.16 = (bf16[96,256]{1,0:T(8,128)(2,1)S(1)}, bf16[96,256]{1,0:T(8,128)(2,1)S(1)}, u32[]{:S(2)}, u32[]{:S(2)}) collective-permute-start(bf16[96,256]{1,0:T(8,128)(2,1)S(1)} %get-tuple-element.74), channel_id=1, source_target_pairs={{0,8},{4,12},{8,0},{12,4},{16,24},{20,28},{24,16},{28,20},{1,9},{5... | collective-permute-start | bytes 147464 | tf_op jit(solution)/shard_map/ppermute | solution.py:515
  54.0 1.4 %collective-permute-start.17 = (bf16[96,256]{1,0:T(8,128)(2,1)S(1)}, bf16[96,256]{1,0:T(8,128)(2,1)S(1)}, u32[]{:S(2)}, u32[]{:S(2)}) collective-permute-start(bf16[96,256]{1,0:T(8,128)(2,1)S(1)} %get-tuple-element.75), channel_id=1, source_target_pairs={{0,12},{4,8},{8,4},{12,0},{16,28},{20,24},{24,20},{28,16},{1,13},{... | collective-permute-start | bytes 147464 | tf_op jit(solution)/shard_map/ppermute | solution.py:515
  55.4 0.2 collective-permute-done.18.pair_ref
  55.5 3.2 %collective-permute-start.19 = (bf16[96,256]{1,0:T(8,128)(2,1)S(1)}, bf16[96,256]{1,0:T(8,128)(2,1)S(1)}, u32[]{:S(2)}, u32[]{:S(2)}) collective-permute-start(bf16[96,256]{1,0:T(8,128)(2,1)S(1)} %get-tuple-element.78), channel_id=1, source_target_pairs={{0,16},{4,20},{8,24},{12,28},{16,0},{20,4},{24,8},{28,12},{1,17},{... | collective-permute-start | bytes 147464 | tf_op jit(solution)/shard_map/ppermute | solution.py:515
  58.7 2.0 %collective-permute-start.20 = (bf16[96,256]{1,0:T(8,128)(2,1)S(1)}, bf16[96,256]{1,0:T(8,128)(2,1)S(1)}, u32[]{:S(2)}, u32[]{:S(2)}) collective-permute-start(bf16[96,256]{1,0:T(8,128)(2,1)S(1)} %get-tuple-element.79), channel_id=1, source_target_pairs={{0,24},{4,28},{8,16},{12,20},{16,8},{20,12},{24,0},{28,4},{1,25},{... | collective-permute-start | bytes 147464 | tf_op jit(solution)/shard_map/ppermute | solution.py:515
  60.8 0.0 collective-permute-done.16.refs_1_
  60.8 0.0 collective-permute-done.17.refs_2_
  60.8 0.1 collective-permute-done.19.refs_3_
  60.9 3.8 %collective-permute-done.20.refs_4_ = bf16[96,256]{1,0:T(8,128)(2,1)S(1)} collective-permute-done((bf16[96,256]{1,0:T(8,128)(2,1)S(1)}, bf16[96,256]{1,0:T(8,128)(2,1)S(1)}, u32[]{:S(2)}, u32[]{:S(2)}) %collective-permute-start.20) | collective-permute-done | bytes 49184 | tf_op jit(solution)/shard_map/ppermute | solution.py:515
  64.7 2.2 %collective-permute-start.22 = (bf16[96,256]{1,0:T(8,128)(2,1)S(1)}, bf16[96,256]{1,0:T(8,128)(2,1)S(1)}, u32[]{:S(2)}, u32[]{:S(2)}) collective-permute-start(bf16[96,256]{1,0:T(8,128)(2,1)S(1)} %shard_map.94.refs_0_), channel_id=1, source_target_pairs={{0,24},{4,28},{8,16},{12,20},{16,8},{20,12},{24,0},{28,4},{1,25},{... | collective-permute-start | bytes 147464 | tf_op jit(solution)/shard_map/ppermute | solution.py:515
  66.8 0.0 collective-permute-start.21
  66.9 3.8 %collective-permute-done.22.refs_2_.refs_4_ = bf16[96,256]{1,0:T(8,128)(2,1)S(1)} collective-permute-done((bf16[96,256]{1,0:T(8,128)(2,1)S(1)}, bf16[96,256]{1,0:T(8,128)(2,1)S(1)}, u32[]{:S(2)}, u32[]{:S(2)}) %collective-permute-start.22) | collective-permute-done | bytes 49184 | tf_op jit(solution)/shard_map/ppermute | solution.py:515
  70.6 1.2 %collective-permute-done.21.refs_1_.refs_3_ = bf16[96,256]{1,0:T(8,128)(2,1)S(1)} collective-permute-done((bf16[96,256]{1,0:T(8,128)(2,1)S(1)}, bf16[96,256]{1,0:T(8,128)(2,1)S(1)}, u32[]{:S(2)}, u32[]{:S(2)}) %collective-permute-start.21) | collective-permute-done | bytes 49184 | tf_op jit(solution)/shard_map/ppermute | solution.py:515
  71.9 1.4 %collective-permute-start.23 = (bf16[288,256]{1,0:T(8,128)(2,1)S(1)}, bf16[288,256]{1,0:T(8,128)(2,1)S(1)}, u32[]{:S(2)}, u32[]{:S(2)}) collective-permute-start(bf16[288,256]{1,0:T(8,128)(2,1)S(1)} %shard_map.95), channel_id=1, source_target_pairs={{0,4},{4,0},{8,12},{12,8},{16,20},{20,16},{24,28},{28,24},{1,5},{5... | collective-permute-start | bytes 442376 | tf_op jit(solution)/shard_map/ppermute | solution.py:515
  73.3 0.0 collective-permute-start.25
  73.3 2.1 %collective-permute-start.24 = (bf16[96,256]{1,0:T(8,128)(2,1)S(1)}, bf16[96,256]{1,0:T(8,128)(2,1)S(1)}, u32[]{:S(2)}, u32[]{:S(2)}) collective-permute-start(bf16[96,256]{1,0:T(8,128)(2,1)S(1)} %shard_map.94.refs_0_), channel_id=1, source_target_pairs={{0,8},{4,12},{8,0},{12,4},{16,24},{20,28},{24,16},{28,20},{1,9},{5... | collective-permute-start | bytes 147464 | tf_op jit(solution)/shard_map/ppermute | solution.py:515
  75.4 1.2 %shard_map.88.main_ref = bf16[2,512,256]{2,1,0:T(8,128)(2,1)S(1)} custom-call(bf16[2,512,256]{2,1,0:T(8,128)(2,1)S(1)} %get-tuple-element.67.refs_0_.slope_ref, bf16[2,512,768]{2,1,0:T(8,128)(2,1)S(1)} %get-tuple-element.49.refs_1_, bf16[1,3,256,256]{3,2,1,0:T(8,128)(2,1)S(1)} %copy-done, ...), custom_call_target="tpu_custom_call", output_to_operand_aliasing={{}: (6, {})} | custom-call | tf_op jit(solution)/shard_map/pallas_call | solution.py:371
  76.6 1.6 %collective-permute-done.25.refs_2_ = bf16[96,256]{1,0:T(8,128)(2,1)S(1)} collective-permute-done((bf16[96,256]{1,0:T(8,128)(2,1)S(1)}, bf16[96,256]{1,0:T(8,128)(2,1)S(1)}, u32[]{:S(2)}, u32[]{:S(2)}) %collective-permute-start.25) | collective-permute-done | bytes 49184 | tf_op jit(solution)/shard_map/ppermute | solution.py:515
  78.3 0.8 %shard_map.96.refs_1_ = f32[768,256]{1,0:T(8,128)} custom-call(bf16[96,256]{1,0:T(8,128)(2,1)S(1)} %shard_map.94.refs_0_, bf16[96,256]{1,0:T(8,128)(2,1)S(1)} %collective-permute-done.24.refs_1_, bf16[96,256]{1,0:T(8,128)(2,1)S(1)} %collective-permute-done.25.refs_2_, bf16[96,256]{1,0:T(8,128)(2,1)S(1)} %collective-permute-done.21.refs_1_.refs_3_, ...), custom_call_target="tpu_custom_call" | custom-call | tf_op jit(solution)/shard_map/pallas_call | solution.py:479
  79.1 0.0 collective-permute-done.23.refs_0_
  79.1 0.7 shard_map.97
  79.9 0.0 collective-permute-done.14.far_ref
  79.9 0.9 %grad.1 = bf16[1,2,512,256]{3,2,1,0:T(8,128)(2,1)} custom-call(bf16[2,512,256]{2,1,0:T(8,128)(2,1)S(1)} %shard_map.88.main_ref, bf16[256,256]{1,0:T(8,128)(2,1)S(1)} %collective-permute-done.13.refs_0_.near_ref, bf16[768,256]{1,0:T(8,128)(2,1)S(1)} %collective-permute-done.14.far_ref), custom_call_target="tpu_custom_call" | custom-call | tf_op jit(solution)/shard_map/grad/pallas_call | solution.py:563
  (18 shorter events, 0.2 us)
Async XLA Ops:
  0.6 8.1 %copy-start.1 = (bf16[1,2,512,256]{3,2,1,0:T(8,128)(2,1)S(1)}, bf16[1,2,512,256]{3,2,1,0:T(8,128)(2,1)}, u32[]{:S(2)}) copy-start(bf16[1,2,512,256]{3,2,1,0:T(8,128)(2,1)} %x_ref.7) | copy-start | bytes 1572868
  0.6 8.1 %copy-start = (bf16[1,3,256,256]{3,2,1,0:T(8,128)(2,1)S(1)}, bf16[1,3,256,256]{3,2,1,0:T(8,128)(2,1)}, u32[]{:S(2)}) copy-start(bf16[1,3,256,256]{3,2,1,0:T(8,128)(2,1)} %refs_2_.19) | copy-start | bytes 1179652
  1.7 7.9 %collective-permute-start.1 = (bf16[2,128,256]{2,1,0:T(8,128)(2,1)S(1)}, bf16[2,128,256]{2,1,0:T(8,128)(2,1)S(1)}, u32[]{:S(2)}, u32[]{:S(2)}) collective-permute-start(bf16[2,128,256]{2,1,0:T(8,128)(2,1)S(1)} %get-tuple-element.43), channel_id=1, source_target_pairs={{0,1},{1,0},{2,3},{3,2},{4,8},{5,9},{6,10},{7,11},{8,4},{9,5},{10,... | collective-permute-start | bytes 393224 | tf_op jit(solution)/shard_map/ppermute | solution.py:583
  2.3 8.9 %collective-permute-start = (bf16[2,128,256]{2,1,0:T(8,128)(2,1)S(1)}, bf16[2,128,256]{2,1,0:T(8,128)(2,1)S(1)}, u32[]{:S(2)}, u32[]{:S(2)}) collective-permute-start(bf16[2,128,256]{2,1,0:T(8,128)(2,1)S(1)} %get-tuple-element.42), channel_id=1, source_target_pairs={{0,4},{1,5},{2,6},{3,7},{4,0},{5,1},{6,2},{7,3},{8,12},{9,13},{10,... | collective-permute-start | bytes 393224 | tf_op jit(solution)/shard_map/ppermute | solution.py:584
  9.6 1.0 %copy-start.2 = (bf16[2,512,256]{2,1,0:T(8,128)(2,1)S(1)}, bf16[2,512,256]{2,1,0:T(8,128)(2,1)}, u32[]{:S(2)}) copy-start(bf16[2,512,256]{2,1,0:T(8,128)(2,1)} %refs_3_.5) | copy-start | bytes 1572868
  12.0 7.7 %collective-permute-start.2 = (bf16[2,512,256]{2,1,0:T(8,128)(2,1)S(1)}, bf16[2,512,256]{2,1,0:T(8,128)(2,1)S(1)}, u32[]{:S(2)}, u32[]{:S(2)}) collective-permute-start(bf16[2,512,256]{2,1,0:T(8,128)(2,1)S(1)} %shard_map.82.refs_7_), channel_id=1, source_target_pairs={{0,1},{1,0},{2,3},{3,2},{4,5},{5,4},{6,7},{7,6},{8,9},{9,8},{10,11... | collective-permute-start | bytes 1572872 | tf_op jit(solution)/shard_map/ppermute | solution.py:580
  12.1 6.2 %collective-permute-start.3 = (bf16[2,128,256]{2,1,0:T(8,128)(2,1)S(1)}, bf16[2,128,256]{2,1,0:T(8,128)(2,1)S(1)}, u32[]{:S(2)}, u32[]{:S(2)}) collective-permute-start(bf16[2,128,256]{2,1,0:T(8,128)(2,1)S(1)} %get-tuple-element.52.refs_6_), channel_id=1, source_target_pairs={{0,1},{1,3},{2,0},{3,6},{4,5},{5,7},{6,4},{7,2},{8,9},{9,11},{10,8... | collective-permute-start | bytes 393224 | tf_op jit(solution)/shard_map/ppermute | solution.py:580
  12.6 7.1 %collective-permute-start.4 = (bf16[2,128,256]{2,1,0:T(8,128)(2,1)S(1)}, bf16[2,128,256]{2,1,0:T(8,128)(2,1)S(1)}, u32[]{:S(2)}, u32[]{:S(2)}) collective-permute-start(bf16[2,128,256]{2,1,0:T(8,128)(2,1)S(1)} %get-tuple-element.53.refs_7_), channel_id=1, source_target_pairs={{0,1},{1,3},{2,0},{3,2},{4,5},{5,7},{6,4},{7,10},{8,9},{9,11},{10,... | collective-permute-start | bytes 393224 | tf_op jit(solution)/shard_map/ppermute | solution.py:580
  19.7 11.2 %collective-permute-start.5 = (bf16[512,256]{1,0:T(8,128)(2,1)S(1)}, bf16[512,256]{1,0:T(8,128)(2,1)S(1)}, u32[]{:S(2)}, u32[]{:S(2)}) collective-permute-start(bf16[512,256]{1,0:T(8,128)(2,1)S(1)} %get-tuple-element.54), channel_id=1, source_target_pairs={{0,3},{1,0},{2,1},{3,2},{4,7},{5,4},{6,5},{7,6},{8,11},{9,8},{10,9... | collective-permute-start | bytes 786440 | tf_op jit(solution)/shard_map/ppermute | solution.py:580
  21.4 9.5 %collective-permute-start.6 = (bf16[512,256]{1,0:T(8,128)(2,1)S(1)}, bf16[512,256]{1,0:T(8,128)(2,1)S(1)}, u32[]{:S(2)}, u32[]{:S(2)}) collective-permute-start(bf16[512,256]{1,0:T(8,128)(2,1)S(1)} %get-tuple-element.58), channel_id=1, source_target_pairs={{0,3},{1,0},{2,1},{3,2},{4,7},{5,4},{6,5},{7,6},{8,11},{9,8},{10,9... | collective-permute-start | bytes 786440 | tf_op jit(solution)/shard_map/ppermute | solution.py:580
  21.4 8.0 %collective-permute-start.7 = (bf16[2,128,256]{2,1,0:T(8,128)(2,1)S(1)}, bf16[2,128,256]{2,1,0:T(8,128)(2,1)S(1)}, u32[]{:S(2)}, u32[]{:S(2)}) collective-permute-start(bf16[2,128,256]{2,1,0:T(8,128)(2,1)S(1)} %get-tuple-element.59.refs_7_), channel_id=1, source_target_pairs={{0,3},{1,0},{3,2},{2,5},{4,7},{5,4},{7,6},{6,1},{8,11},{9,8},{11,1... | collective-permute-start | bytes 393224 | tf_op jit(solution)/shard_map/ppermute | solution.py:580
  22.5 8.4 %collective-permute-start.8 = (bf16[2,128,256]{2,1,0:T(8,128)(2,1)S(1)}, bf16[2,128,256]{2,1,0:T(8,128)(2,1)S(1)}, u32[]{:S(2)}, u32[]{:S(2)}) collective-permute-start(bf16[2,128,256]{2,1,0:T(8,128)(2,1)S(1)} %get-tuple-element.60.refs_8_), channel_id=1, source_target_pairs={{0,3},{1,0},{3,2},{2,1},{4,7},{5,4},{7,6},{6,9},{8,11},{9,8},{11,1... | collective-permute-start | bytes 393224 | tf_op jit(solution)/shard_map/ppermute | solution.py:580
  30.9 7.8 %collective-permute-start.9 = (bf16[2,512,256]{2,1,0:T(8,128)(2,1)S(1)}, bf16[2,512,256]{2,1,0:T(8,128)(2,1)S(1)}, u32[]{:S(2)}, u32[]{:S(2)}) collective-permute-start(bf16[2,512,256]{2,1,0:T(8,128)(2,1)S(1)} %shard_map.86.refs_6_), channel_id=1, source_target_pairs={{0,1},{1,0},{2,3},{3,2},{4,5},{5,4},{6,7},{7,6},{8,9},{9,8},{10,11... | collective-permute-start | bytes 1572872 | tf_op jit(solution)/shard_map/ppermute | solution.py:580
  33.1 5.6 %collective-permute-start.10 = (bf16[2,128,256]{2,1,0:T(8,128)(2,1)S(1)}, bf16[2,128,256]{2,1,0:T(8,128)(2,1)S(1)}, u32[]{:S(2)}, u32[]{:S(2)}) collective-permute-start(bf16[2,128,256]{2,1,0:T(8,128)(2,1)S(1)} %get-tuple-element.64.refs_6_), channel_id=1, source_target_pairs={{0,2},{2,3},{3,1},{1,4},{4,6},{6,7},{7,5},{5,0},{8,10},{10,11},{11... | collective-permute-start | bytes 393224 | tf_op jit(solution)/shard_map/ppermute | solution.py:580
  33.3 5.4 %collective-permute-start.11 = (bf16[2,128,256]{2,1,0:T(8,128)(2,1)S(1)}, bf16[2,128,256]{2,1,0:T(8,128)(2,1)S(1)}, u32[]{:S(2)}, u32[]{:S(2)}) collective-permute-start(bf16[2,128,256]{2,1,0:T(8,128)(2,1)S(1)} %get-tuple-element.65.refs_7_), channel_id=1, source_target_pairs={{0,2},{2,3},{3,1},{1,0},{4,6},{6,7},{7,5},{5,8},{8,10},{10,11},{11... | collective-permute-start | bytes 393224 | tf_op jit(solution)/shard_map/ppermute | solution.py:580
  39.7 1.5 %collective-permute-start.12 = (bf16[2,128,256]{2,1,0:T(8,128)(2,1)S(1)}, bf16[2,128,256]{2,1,0:T(8,128)(2,1)S(1)}, u32[]{:S(2)}, u32[]{:S(2)}) collective-permute-start(bf16[2,128,256]{2,1,0:T(8,128)(2,1)S(1)} %get-tuple-element.68), channel_id=1, source_target_pairs={{0,1},{1,0},{2,3},{3,2},{4,5},{5,4},{6,7},{7,6},{8,9},{9,8},{10,11... | collective-permute-start | bytes 393224 | tf_op jit(solution)/shard_map/ppermute | solution.py:520
  41.3 7.3 %collective-permute-start.13 = (bf16[256,256]{1,0:T(8,128)(2,1)S(1)}, bf16[256,256]{1,0:T(8,128)(2,1)S(1)}, u32[]{:S(2)}, u32[]{:S(2)}) collective-permute-start(bf16[256,256]{1,0:T(8,128)(2,1)S(1)} %shard_map.90), channel_id=1, source_target_pairs={{0,4},{1,3},{2,6},{3,1},{4,0},{5,9},{6,2},{7,11},{8,12},{9,5},{10,... | collective-permute-start | bytes 393224 | tf_op jit(solution)/shard_map/ppermute | solution.py:524
  48.6 31.3 %collective-permute-start.14 = (bf16[768,256]{1,0:T(8,128)(2,1)S(1)}, bf16[768,256]{1,0:T(8,128)(2,1)S(1)}, u32[]{:S(2)}, u32[]{:S(2)}) collective-permute-start(bf16[768,256]{1,0:T(8,128)(2,1)S(1)} %shard_map.91), channel_id=1, source_target_pairs={{0,1},{1,0},{2,3},{3,2},{4,5},{5,4},{6,7},{7,6},{8,9},{9,8},{10,11... | collective-permute-start | bytes 1179656 | tf_op jit(solution)/shard_map/ppermute | solution.py:531
  49.3 6.2 %collective-permute-start.18 = (bf16[192,256]{1,0:T(8,128)(2,1)S(1)}, bf16[192,256]{1,0:T(8,128)(2,1)S(1)}, u32[]{:S(2)}, u32[]{:S(2)}) collective-permute-start(bf16[192,256]{1,0:T(8,128)(2,1)S(1)} %get-tuple-element.77), channel_id=1, source_target_pairs={{0,4},{4,0},{8,12},{12,8},{16,20},{20,16},{24,28},{28,24},{1,5},{5... | collective-permute-start | bytes 294920 | tf_op jit(solution)/shard_map/ppermute | solution.py:515
  51.9 6.9 %collective-permute-start.15 = (bf16[96,256]{1,0:T(8,128)(2,1)S(1)}, bf16[96,256]{1,0:T(8,128)(2,1)S(1)}, u32[]{:S(2)}, u32[]{:S(2)}) collective-permute-start(bf16[96,256]{1,0:T(8,128)(2,1)S(1)} %get-tuple-element.73), channel_id=1, source_target_pairs={{0,4},{4,0},{8,12},{12,8},{16,20},{20,16},{24,28},{28,24},{1,5},{5... | collective-permute-start | bytes 147464 | tf_op jit(solution)/shard_map/ppermute | solution.py:515
  51.9 8.8 %collective-permute-start.16 = (bf16[96,256]{1,0:T(8,128)(2,1)S(1)}, bf16[96,256]{1,0:T(8,128)(2,1)S(1)}, u32[]{:S(2)}, u32[]{:S(2)}) collective-permute-start(bf16[96,256]{1,0:T(8,128)(2,1)S(1)} %get-tuple-element.74), channel_id=1, source_target_pairs={{0,8},{4,12},{8,0},{12,4},{16,24},{20,28},{24,16},{28,20},{1,9},{5... | collective-permute-start | bytes 147464 | tf_op jit(solution)/shard_map/ppermute | solution.py:515
  54.0 6.8 %collective-permute-start.17 = (bf16[96,256]{1,0:T(8,128)(2,1)S(1)}, bf16[96,256]{1,0:T(8,128)(2,1)S(1)}, u32[]{:S(2)}, u32[]{:S(2)}) collective-permute-start(bf16[96,256]{1,0:T(8,128)(2,1)S(1)} %get-tuple-element.75), channel_id=1, source_target_pairs={{0,12},{4,8},{8,4},{12,0},{16,28},{20,24},{24,20},{28,16},{1,13},{... | collective-permute-start | bytes 147464 | tf_op jit(solution)/shard_map/ppermute | solution.py:515
  55.5 5.3 %collective-permute-start.19 = (bf16[96,256]{1,0:T(8,128)(2,1)S(1)}, bf16[96,256]{1,0:T(8,128)(2,1)S(1)}, u32[]{:S(2)}, u32[]{:S(2)}) collective-permute-start(bf16[96,256]{1,0:T(8,128)(2,1)S(1)} %get-tuple-element.78), channel_id=1, source_target_pairs={{0,16},{4,20},{8,24},{12,28},{16,0},{20,4},{24,8},{28,12},{1,17},{... | collective-permute-start | bytes 147464 | tf_op jit(solution)/shard_map/ppermute | solution.py:515
  58.7 5.9 %collective-permute-start.20 = (bf16[96,256]{1,0:T(8,128)(2,1)S(1)}, bf16[96,256]{1,0:T(8,128)(2,1)S(1)}, u32[]{:S(2)}, u32[]{:S(2)}) collective-permute-start(bf16[96,256]{1,0:T(8,128)(2,1)S(1)} %get-tuple-element.79), channel_id=1, source_target_pairs={{0,24},{4,28},{8,16},{12,20},{16,8},{20,12},{24,0},{28,4},{1,25},{... | collective-permute-start | bytes 147464 | tf_op jit(solution)/shard_map/ppermute | solution.py:515
  64.7 6.0 %collective-permute-start.22 = (bf16[96,256]{1,0:T(8,128)(2,1)S(1)}, bf16[96,256]{1,0:T(8,128)(2,1)S(1)}, u32[]{:S(2)}, u32[]{:S(2)}) collective-permute-start(bf16[96,256]{1,0:T(8,128)(2,1)S(1)} %shard_map.94.refs_0_), channel_id=1, source_target_pairs={{0,24},{4,28},{8,16},{12,20},{16,8},{20,12},{24,0},{28,4},{1,25},{... | collective-permute-start | bytes 147464 | tf_op jit(solution)/shard_map/ppermute | solution.py:515
  66.8 5.0 %collective-permute-start.21 = (bf16[96,256]{1,0:T(8,128)(2,1)S(1)}, bf16[96,256]{1,0:T(8,128)(2,1)S(1)}, u32[]{:S(2)}, u32[]{:S(2)}) collective-permute-start(bf16[96,256]{1,0:T(8,128)(2,1)S(1)} %shard_map.94.refs_0_), channel_id=1, source_target_pairs={{0,16},{4,20},{8,24},{12,28},{16,0},{20,4},{24,8},{28,12},{1,17},{... | collective-permute-start | bytes 147464 | tf_op jit(solution)/shard_map/ppermute | solution.py:515
  71.9 7.3 %collective-permute-start.23 = (bf16[288,256]{1,0:T(8,128)(2,1)S(1)}, bf16[288,256]{1,0:T(8,128)(2,1)S(1)}, u32[]{:S(2)}, u32[]{:S(2)}) collective-permute-start(bf16[288,256]{1,0:T(8,128)(2,1)S(1)} %shard_map.95), channel_id=1, source_target_pairs={{0,4},{4,0},{8,12},{12,8},{16,20},{20,16},{24,28},{28,24},{1,5},{5... | collective-permute-start | bytes 442376 | tf_op jit(solution)/shard_map/ppermute | solution.py:515
  73.3 5.0 %collective-permute-start.25 = (bf16[96,256]{1,0:T(8,128)(2,1)S(1)}, bf16[96,256]{1,0:T(8,128)(2,1)S(1)}, u32[]{:S(2)}, u32[]{:S(2)}) collective-permute-start(bf16[96,256]{1,0:T(8,128)(2,1)S(1)} %shard_map.94.refs_0_), channel_id=1, source_target_pairs={{0,12},{4,8},{8,4},{12,0},{16,28},{20,24},{24,20},{28,16},{1,13},{... | collective-permute-start | bytes 147464 | tf_op jit(solution)/shard_map/ppermute | solution.py:515
  73.3 5.0 %collective-permute-start.24 = (bf16[96,256]{1,0:T(8,128)(2,1)S(1)}, bf16[96,256]{1,0:T(8,128)(2,1)S(1)}, u32[]{:S(2)}, u32[]{:S(2)}) collective-permute-start(bf16[96,256]{1,0:T(8,128)(2,1)S(1)} %shard_map.94.refs_0_), channel_id=1, source_target_pairs={{0,8},{4,12},{8,0},{12,4},{16,24},{20,28},{24,16},{28,20},{1,9},{5... | collective-permute-start | bytes 147464 | tf_op jit(solution)/shard_map/ppermute | solution.py:515
